TPU v7x, 256 devices: a whole 4x4x8 slice. The times are simulated.
256 devices in a mesh: line: 4 (over x), cross: 64 (over y, z, core).
Axes of the slice: x: 4, y: 4, z: 8, core: 2. Of those that a mesh axis runs over, the one named last changes fastest.
Arguments:
- velocity: float32 [3, 512, 512, 256], P(None, 'line', 'cross'), may hold values from -6 to 6
Outputs:
- advection: float32 [3, 512, 512, 256], P(None, 'line', 'cross')
- x_derivative: float32 [3, 512, 512, 256], P(None, 'line', 'cross')
All inputs are finite; a program needn't handle non-finite values.
Results may differ from a plain program's by a relative error of at most 0.0001.
Values sent between devices are 32-bit elements; how exact they have to be, the bound alone decides.
No kernel may reach another device: no remote copies, remote signals or barrier semaphores. Data moves between devices by JAX's collectives and lax.ppermute only.
A program may use at most 128 MiB of HBM per device.

v0:
```python
import jax
import jax.numpy as jnp
import numpy as np
from jax import lax
from jax.sharding import PartitionSpec as P

ALPHA = 1.0 / 3.0
COEF_A = 14.0 / 9.0
COEF_B = 1.0 / 9.0
FIRST = 45.0 / 60.0
SECOND = -9.0 / 60.0
THIRD = 1.0 / 60.0


def extended_2(block, sides, width):
    for axis, dim in sides:
        count = lax.axis_size(axis)
        forward = [(i, i + 1) for i in range(count - 1)]
        forward.append((count - 1, 0))
        backward = [(target, source) for source, target in forward]
        low = lax.ppermute(
            lax.slice_in_dim(block, block.shape[dim] - width, None, axis=dim), axis, forward
        )
        high = lax.ppermute(lax.slice_in_dim(block, 0, width, axis=dim), axis, backward)
        block = jnp.concatenate([low, block, high], axis=dim)
    return block


def local_inverse(count):
    theta = np.ones(count + 1)
    for step in range(2, count + 1):
        theta[step] = theta[step - 1] - ALPHA * ALPHA * theta[step - 2]
    rows = np.arange(1, count + 1)[:, None]
    cols = np.arange(1, count + 1)[None, :]
    lower = np.minimum(rows, cols)
    upper = np.maximum(rows, cols)
    signs = np.power(-ALPHA, upper - lower)
    return signs * theta[lower - 1] * theta[count - upper] / theta[count]


def explicit_x(extended, count):
    near = extended[:, 3 : 3 + count] - extended[:, 1 : 1 + count]
    far = extended[:, 4 : 4 + count] - extended[:, 0:count]
    return 0.5 * COEF_A * near + 0.25 * COEF_B * far


def apply_rows(table, values):
    return jnp.einsum("ij,cjyz->ciyz", table, values, precision=lax.Precision.HIGHEST)


def explicit_z(field):
    total = FIRST * (jnp.roll(field, -1, 3) - jnp.roll(field, 1, 3))
    total = total + SECOND * (jnp.roll(field, -2, 3) - jnp.roll(field, 2, 3))
    return total + THIRD * (jnp.roll(field, -3, 3) - jnp.roll(field, 3, 3))


def stencil_y(padded, count):
    total = FIRST * (padded[:, :, 4 : 4 + count] - padded[:, :, 2 : 2 + count])
    total = total + SECOND * (padded[:, :, 5 : 5 + count] - padded[:, :, 1 : 1 + count])
    return total + THIRD * (padded[:, :, 6 : 6 + count] - padded[:, :, 0:count])


def on_device(velocity):
    seg_len = velocity.shape[1]
    tile_len = velocity.shape[2]
    extended = extended_2(velocity, (("line", 1),), 2)
    forcing = explicit_x(extended, seg_len)
    inverse = local_inverse(seg_len)
    table = jnp.asarray(inverse, jnp.float32)
    partial_sol = apply_rows(table, forcing)
    ends = jnp.stack([partial_sol[:, 0], partial_sol[:, -1]], axis=1)
    beside_all = extended_2(ends, (("line", 1),), 1)
    corner = float(inverse[0, 0])
    denom = 1.0 - ALPHA * ALPHA * corner * corner
    left_value = (beside_all[:, 0] - ALPHA * corner * partial_sol[:, 0]) / denom
    right_value = (beside_all[:, 3] - ALPHA * corner * partial_sol[:, -1]) / denom
    first_col = table[:, 0][None, :, None, None]
    last_col = table[:, -1][None, :, None, None]
    along_x = partial_sol - ALPHA * (
        left_value[:, None] * first_col + right_value[:, None] * last_col
    )
    padded = extended_2(velocity, (("cross", 2),), 3)
    along_y = stencil_y(padded, tile_len)
    along_z = explicit_z(velocity)
    speed_u = velocity[0:1]
    speed_v = velocity[1:2]
    speed_w = velocity[2:3]
    advection = -(speed_u * along_x + speed_v * along_y + speed_w * along_z)
    return (advection, along_x)


def solution(mesh):
    in_specs = (P(None, "line", "cross", None),)
    out_specs = (P(None, "line", "cross", None), P(None, "line", "cross", None))
    return jax.shard_map(
        on_device, mesh=mesh, in_specs=in_specs, out_specs=out_specs, check_vma=False
    )
```

profile of v0, /device:TPU:6, one launch (start us, length us, event | category | flops | bytes accessed | tf_op | source)
XLA Modules:
  0.0 90.0 jit_solution(12127957603011734741)
XLA Ops:
  0.6 0.8 fusion.24
  1.5 0.9 collective-permute-start
  2.4 2.4 %collective-permute-start.1 = (f32[3,2,8,256]{3,2,1,0:T(8,128)S(1)}, f32[3,2,8,256]{3,2,1,0:T(8,128)S(1)}, u32[]{:S(2)}, u32[]{:S(2)}) collective-permute-start(f32[3,2,8,256]{3,2,1,0:T(8,128)S(1)} %get-tuple-element.11), channel_id=1, source_target_pairs={{0,64},{64,128},{128,192},{192,0},{1,65},{65,129},{129,193},{193,1... | collective-permute-start | bytes 147464 | tf_op jit(solution)/shard_map/ppermute | solution.py:21
  4.8 3.4 %fusion.31 = (f32[3,128,3,256]{3,2,1,0:T(4,128)S(1)}, f32[3,128,3,256]{3,2,1,0:T(4,128)S(1)}) fusion(f32[3,128,8,256]{3,2,1,0:T(8,128)} %param.2), kind=kLoop, calls=%fused_computation.53 | loop fusion | bytes 4718592 | tf_op jit(solution)/shard_map/slice | solution.py:24
  8.2 0.0 copy-start
  8.2 1.2 %copy.37 = f32[3,128,3,256]{3,1,2,0:T(8,128)} copy(f32[3,128,3,256]{3,2,1,0:T(4,128)S(1)} %get-tuple-element.30) | data formatting | bytes 2359296
  9.4 0.0 collective-permute-start.5
  9.4 1.2 %copy.38 = f32[3,128,3,256]{3,1,2,0:T(8,128)} copy(f32[3,128,3,256]{3,2,1,0:T(4,128)S(1)} %get-tuple-element.29) | data formatting | bytes 2359296
  10.6 7.2 %collective-permute-start.4 = (f32[3,128,3,256]{3,1,2,0:T(8,128)}, f32[3,128,3,256]{3,1,2,0:T(8,128)}, u32[]{:S(2)}, u32[]{:S(2)}) collective-permute-start(f32[3,128,3,256]{3,1,2,0:T(8,128)} %copy.38), channel_id=1, source_target_pairs={{1,0},{2,1},{3,2},{4,3},{5,4},{6,5},{7,6},{8,7},{9,8},{10,9},{11,1... | collective-permute-start | bytes 3538952 | tf_op jit(solution)/shard_map/ppermute | solution.py:24
  17.8 0.0 copy-done
  17.8 2.2 %fusion.27 = (f32[3,128,8,2]{3,2,1,0:T(8,128)}, f32[3,128,8,2]{3,2,1,0:T(8,128)}) fusion(f32[3,128,8,256]{3,2,1,0:T(8,128)S(1)} %copy-done), kind=kLoop, calls=%fused_computation.49 | loop fusion | bytes 98304 | tf_op jit(solution)/shard_map/jit(_roll_static)/slice | solution.py:53
  20.0 1.7 %fusion.29 = (f32[3,128,8,1]{3,2,1,0:T(8,128)}, f32[3,128,8,1]{3,2,1,0:T(8,128)S(1)}) fusion(f32[3,128,8,256]{3,2,1,0:T(8,128)S(1)} %copy-done), kind=kLoop, calls=%fused_computation.51 | loop fusion | bytes 49152 | tf_op jit(solution)/shard_map/jit(_roll_static)/slice | solution.py:52
  21.7 1.0 %fusion.30 = (f32[3,128,8,255]{3,2,1,0:T(8,128)S(1)}, f32[3,128,8,255]{3,2,1,0:T(8,128)S(1)}) fusion(f32[3,128,8,256]{3,2,1,0:T(8,128)S(1)} %copy-done), kind=kLoop, calls=%fused_computation.52 | loop fusion | bytes 12533760 | tf_op jit(solution)/shard_map/jit(_roll_static)/slice | solution.py:52
  22.7 3.7 %fusion.26 = (f32[3,128,8,253]{3,2,1,0:T(8,128)}, f32[3,128,8,253]{3,2,1,0:T(8,128)}) fusion(f32[3,128,8,256]{3,2,1,0:T(8,128)S(1)} %copy-done), kind=kLoop, calls=%fused_computation.48 | loop fusion | bytes 12435456 | tf_op jit(solution)/shard_map/jit(_roll_static)/slice | solution.py:54
  26.4 3.8 %fusion.28 = (f32[3,128,8,254]{3,2,1,0:T(8,128)}, f32[3,128,8,254]{3,2,1,0:T(8,128)}) fusion(f32[3,128,8,256]{3,2,1,0:T(8,128)S(1)} %copy-done), kind=kLoop, calls=%fused_computation.50 | loop fusion | bytes 12484608 | tf_op jit(solution)/shard_map/jit(_roll_static)/slice | solution.py:53
  30.1 2.1 %fusion.25 = (f32[3,128,8,3]{3,2,1,0:T(8,128)}, f32[3,128,8,3]{3,2,1,0:T(8,128)}) fusion(f32[3,128,8,256]{3,2,1,0:T(8,128)S(1)} %copy-done), kind=kLoop, calls=%fused_computation.47 | loop fusion | bytes 147456 | tf_op jit(solution)/shard_map/jit(_roll_static)/slice | solution.py:54
  32.3 0.0 collective-permute-done.1
  32.3 0.5 constant_dynamic-update-slice_fusion.1
  32.8 0.0 collective-permute-done
  32.8 0.0 copy-start.11
  32.9 0.5 fusion.10
  33.4 0.3 copy-done.11
  33.7 4.0 %fusion.20 = f32[3,128,8,256]{3,1,2,0:T(8,128)S(1)} fusion(f32[128,128,1,1]{1,0,3,2:T(8,128)S(1)} %copy-done.11, f32[3,128,8,256]{3,2,1,0:T(8,128)S(1)} %fusion.10), kind=kOutput, calls=%fused_computation.29 | convolution fusion | flops 1207959552 | bytes 6356992 | tf_op jit(solution)/shard_map/ij,cjyz->ciyz/dot_general | solution.py:48
  37.7 0.4 collective-permute-start.2
  38.1 1.7 %collective-permute-start.3 = (f32[3,1,8,256]{3,1,2,0:T(1,128)S(1)}, f32[3,1,8,256]{3,1,2,0:T(1,128)S(1)}, u32[]{:S(2)}, u32[]{:S(2)}) collective-permute-start(f32[3,1,8,256]{3,1,2,0:T(1,128)S(1)} %get-tuple-element.9), channel_id=1, source_target_pairs={{64,0},{128,64},{192,128},{0,192},{65,1},{129,65},{193,129},{1,193... | collective-permute-start | bytes 73736 | tf_op jit(solution)/shard_map/ppermute | solution.py:24
  39.8 0.2 slice_bitcast_fusion.2
  40.0 0.0 copy-start.8
  40.0 0.3 copy.4
  40.4 1.3 %copy.6 = f32[128,8,256]{2,0,1:T(8,128)} copy(f32[128,8,256]{2,1,0:T(8,128)S(1)} %get-tuple-element.15) | data formatting | bytes 2097152 | tf_op jit(solution)/shard_map/mul | solution.py:88
  41.7 1.3 %copy.11 = f32[128,8,256]{2,0,1:T(8,128)} copy(f32[128,8,256]{2,1,0:T(8,128)S(1)} %get-tuple-element.16) | data formatting | bytes 2097152 | tf_op jit(solution)/shard_map/mul | solution.py:88
  43.0 0.0 copy-done.8
  43.0 1.5 %copy.46 = f32[3,128,8,2]{3,1,2,0:T(8,128)} copy(f32[3,128,8,2]{3,2,1,0:T(8,128)S(1)} %copy-done.8) | data formatting | bytes 49152
  44.5 0.0 copy-done.7
  44.5 1.4 %copy.43 = f32[3,128,8,2]{3,1,2,0:T(8,128)} copy(f32[3,128,8,2]{3,2,1,0:T(8,128)S(1)} %copy-done.7) | data formatting | bytes 49152
  46.0 0.0 copy-done.6
  46.0 1.5 %copy.42 = f32[3,128,8,1]{3,1,2,0:T(8,128)} copy(f32[3,128,8,1]{3,2,1,0:T(8,128)S(1)} %copy-done.6) | data formatting | bytes 24576
  47.5 1.4 %copy.39 = f32[3,128,8,1]{3,1,2,0:T(8,128)} copy(f32[3,128,8,1]{3,2,1,0:T(8,128)S(1)} %get-tuple-element.26) | data formatting | bytes 24576
  48.9 0.0 copy-done.10
  48.9 1.4 %copy.50 = f32[3,128,8,3]{3,1,2,0:T(8,128)} copy(f32[3,128,8,3]{3,2,1,0:T(8,128)S(1)} %copy-done.10) | data formatting | bytes 73728
  50.3 0.0 copy-done.9
  50.3 1.4 %copy.47 = f32[3,128,8,3]{3,1,2,0:T(8,128)} copy(f32[3,128,8,3]{3,2,1,0:T(8,128)S(1)} %copy-done.9) | data formatting | bytes 73728
  51.8 1.0 %copy.41 = f32[3,128,8,255]{3,1,2,0:T(8,128)S(1)} copy(f32[3,128,8,255]{3,2,1,0:T(8,128)S(1)} %get-tuple-element.27) | data formatting | bytes 6266880
  52.8 0.0 copy-start.5
  52.8 1.0 %copy.40 = f32[3,128,8,255]{3,1,2,0:T(8,128)S(1)} copy(f32[3,128,8,255]{3,2,1,0:T(8,128)S(1)} %get-tuple-element.28) | data formatting | bytes 6266880
  53.8 0.9 copy-done.5
  54.7 1.0 %copy.49 = f32[3,128,8,253]{3,1,2,0:T(8,128)S(1)} copy(f32[3,128,8,253]{3,2,1,0:T(8,128)S(1)} %copy-done.5) | data formatting | bytes 6217728
  55.7 0.9 copy-done.4
  56.6 2.6 %copy.48 = f32[3,128,8,253]{3,1,2,0:T(8,128)} copy(f32[3,128,8,253]{3,2,1,0:T(8,128)S(1)} %copy-done.4) | data formatting | bytes 6217728
  59.2 0.0 copy-done.3
  59.2 2.6 %copy.45 = f32[3,128,8,254]{3,1,2,0:T(8,128)} copy(f32[3,128,8,254]{3,2,1,0:T(8,128)S(1)} %copy-done.3) | data formatting | bytes 6242304
  61.8 2.6 %copy.44 = f32[3,128,8,254]{3,1,2,0:T(8,128)} copy(f32[3,128,8,254]{3,2,1,0:T(8,128)S(1)} %copy-done.2) | data formatting | bytes 6242304
  64.4 0.0 collective-permute-done.2
  64.4 0.0 collective-permute-done.3
  64.4 0.1 subtract_multiply_fusion.1
  64.5 0.0 collective-permute-done.5
  64.6 1.3 %constant_dynamic-update-slice_fusion.7 = f32[3,128,11,256]{3,1,2,0:T(8,128)S(1)} fusion(f32[3,128,3,256]{3,1,2,0:T(8,128)} %collective-permute-done.5), kind=kLoop, calls=%fused_computation.44 | loop fusion | bytes 2359296
  65.9 0.0 copy-start.12
  65.9 0.0 copy-start.13
  65.9 1.1 %constant_dynamic-update-slice_fusion.5 = (f32[3,128,11,256]{3,1,2,0:T(8,128)S(1)}, f32[3,128,11,256]{3,1,2,0:T(8,128)S(1)}) fusion(f32[3,128,8,256]{3,2,1,0:T(8,128)S(1)} %copy-done, f32[3,128,11,256]{3,1,2,0:T(8,128)S(1)} %constant_dynamic-update-slice_fusion.7), kind=kLoop, calls=%fused_computation.42 | loop fusion | bytes 9437184
  67.0 0.0 collective-permute-done.4
  67.0 1.4 %constant_dynamic-update-slice_fusion.4 = f32[3,128,11,256]{3,1,2,0:T(8,128)S(1)} fusion(f32[3,128,11,256]{3,1,2,0:T(8,128)S(1)} %get-tuple-element.31, f32[3,128,3,256]{3,1,2,0:T(8,128)} %collective-permute-done.4), kind=kLoop, calls=%fused_computation.41 | loop fusion | bytes 2359296 | tf_op jit(solution)/shard_map/concatenate | solution.py:25
  68.4 12.6 %fusion.5 = (f32[3,128,8,256]{3,1,2,0:T(8,128)}, f32[3,128,8,256]{3,1,2,0:T(8,128)}) fusion(f32[3,128,11,256]{3,1,2,0:T(8,128)S(1)} %get-tuple-element.32, f32[3,128,11,256]{3,1,2,0:T(8,128)S(1)} %constant_dynamic-update-slice_fusion.4, f32[3,128,8,1]{3,1,2,0:T(8,128)} %copy.39, f32[3,128,8,255]{3,1,2,0:T(8,128)S(1)} %copy.40, ...), kind=kLoop, calls=%fused_computation.6 | loop fusion | flops 25952256 | bytes 50381824 | tf_op jit(solution)/shard_map/neg | solution.py:88
  81.0 5.5 %copy.24 = f32[3,128,8,256]{3,2,1,0:T(8,128)} copy(f32[3,128,8,256]{3,1,2,0:T(8,128)} %get-tuple-element.4) | data formatting | bytes 6291456
  86.5 3.5 %copy.25 = f32[3,128,8,256]{3,2,1,0:T(8,128)} copy(f32[3,128,8,256]{3,1,2,0:T(8,128)S(1)} %copy-done.1) | data formatting | bytes 6291456
  (16 shorter events, 0.1 us)
Async XLA Ops:
  1.5 31.4 %collective-permute-start = (f32[3,2,8,256]{3,2,1,0:T(8,128)S(1)}, f32[3,2,8,256]{3,2,1,0:T(8,128)S(1)}, u32[]{:S(2)}, u32[]{:S(2)}) collective-permute-start(f32[3,2,8,256]{3,2,1,0:T(8,128)S(1)} %get-tuple-element.10), channel_id=1, source_target_pairs={{64,0},{128,64},{192,128},{0,192},{65,1},{129,65},{193,129},{1,193... | collective-permute-start | bytes 147464 | tf_op jit(solution)/shard_map/ppermute | solution.py:24
  2.4 29.9 %collective-permute-start.1 = (f32[3,2,8,256]{3,2,1,0:T(8,128)S(1)}, f32[3,2,8,256]{3,2,1,0:T(8,128)S(1)}, u32[]{:S(2)}, u32[]{:S(2)}) collective-permute-start(f32[3,2,8,256]{3,2,1,0:T(8,128)S(1)} %get-tuple-element.11), channel_id=1, source_target_pairs={{0,64},{64,128},{128,192},{192,0},{1,65},{65,129},{129,193},{193,1... | collective-permute-start | bytes 147464 | tf_op jit(solution)/shard_map/ppermute | solution.py:21
  8.2 9.7 %copy-start = (f32[3,128,8,256]{3,2,1,0:T(8,128)S(1)}, f32[3,128,8,256]{3,2,1,0:T(8,128)}, u32[]{:S(2)}) copy-start(f32[3,128,8,256]{3,2,1,0:T(8,128)} %param.2) | copy-start | bytes 9437188
  9.4 55.1 %collective-permute-start.5 = (f32[3,128,3,256]{3,1,2,0:T(8,128)}, f32[3,128,3,256]{3,1,2,0:T(8,128)}, u32[]{:S(2)}, u32[]{:S(2)}) collective-permute-start(f32[3,128,3,256]{3,1,2,0:T(8,128)} %copy.37), channel_id=1, source_target_pairs={{0,1},{1,2},{2,3},{3,4},{4,5},{5,6},{6,7},{7,8},{8,9},{9,10},{10,1... | collective-permute-start | bytes 3538952 | tf_op jit(solution)/shard_map/ppermute | solution.py:21
  10.6 56.4 %collective-permute-start.4 = (f32[3,128,3,256]{3,1,2,0:T(8,128)}, f32[3,128,3,256]{3,1,2,0:T(8,128)}, u32[]{:S(2)}, u32[]{:S(2)}) collective-permute-start(f32[3,128,3,256]{3,1,2,0:T(8,128)} %copy.38), channel_id=1, source_target_pairs={{1,0},{2,1},{3,2},{4,3},{5,4},{6,5},{7,6},{8,7},{9,8},{10,9},{11,1... | collective-permute-start | bytes 3538952 | tf_op jit(solution)/shard_map/ppermute | solution.py:24
  32.8 0.8 copy-start.11
  37.7 26.7 %collective-permute-start.2 = (f32[3,1,8,256]{3,1,2,0:T(1,128)S(1)}, f32[3,1,8,256]{3,1,2,0:T(1,128)S(1)}, u32[]{:S(2)}, u32[]{:S(2)}) collective-permute-start(f32[3,1,8,256]{3,1,2,0:T(1,128)S(1)} %get-tuple-element.8), channel_id=1, source_target_pairs={{0,64},{64,128},{128,192},{192,0},{1,65},{65,129},{129,193},{193,1... | collective-permute-start | bytes 73736 | tf_op jit(solution)/shard_map/ppermute | solution.py:21
  38.1 26.4 %collective-permute-start.3 = (f32[3,1,8,256]{3,1,2,0:T(1,128)S(1)}, f32[3,1,8,256]{3,1,2,0:T(1,128)S(1)}, u32[]{:S(2)}, u32[]{:S(2)}) collective-permute-start(f32[3,1,8,256]{3,1,2,0:T(1,128)S(1)} %get-tuple-element.9), channel_id=1, source_target_pairs={{64,0},{128,64},{192,128},{0,192},{65,1},{129,65},{193,129},{1,193... | collective-permute-start | bytes 73736 | tf_op jit(solution)/shard_map/ppermute | solution.py:24
  40.0 3.0 %copy-start.8 = (f32[3,128,8,2]{3,2,1,0:T(8,128)S(1)}, f32[3,128,8,2]{3,2,1,0:T(8,128)}, u32[]{:S(2)}) copy-start(f32[3,128,8,2]{3,2,1,0:T(8,128)} %get-tuple-element.21) | copy-start | bytes 73732
  41.7 2.8 %copy-start.7 = (f32[3,128,8,2]{3,2,1,0:T(8,128)S(1)}, f32[3,128,8,2]{3,2,1,0:T(8,128)}, u32[]{:S(2)}) copy-start(f32[3,128,8,2]{3,2,1,0:T(8,128)} %get-tuple-element.22) | copy-start | bytes 73732
  43.0 3.0 %copy-start.6 = (f32[3,128,8,1]{3,2,1,0:T(8,128)S(1)}, f32[3,128,8,1]{3,2,1,0:T(8,128)}, u32[]{:S(2)}) copy-start(f32[3,128,8,1]{3,2,1,0:T(8,128)} %get-tuple-element.25) | copy-start | bytes 36868
  46.0 2.9 %copy-start.10 = (f32[3,128,8,3]{3,2,1,0:T(8,128)S(1)}, f32[3,128,8,3]{3,2,1,0:T(8,128)}, u32[]{:S(2)}) copy-start(f32[3,128,8,3]{3,2,1,0:T(8,128)} %get-tuple-element.17) | copy-start | bytes 110596
  47.5 2.9 %copy-start.9 = (f32[3,128,8,3]{3,2,1,0:T(8,128)S(1)}, f32[3,128,8,3]{3,2,1,0:T(8,128)}, u32[]{:S(2)}) copy-start(f32[3,128,8,3]{3,2,1,0:T(8,128)} %get-tuple-element.18) | copy-start | bytes 110596
  52.8 1.9 %copy-start.5 = (f32[3,128,8,253]{3,2,1,0:T(8,128)S(1)}, f32[3,128,8,253]{3,2,1,0:T(8,128)}, u32[]{:S(2)}) copy-start(f32[3,128,8,253]{3,2,1,0:T(8,128)} %get-tuple-element.19) | copy-start | bytes 9326596
  54.7 1.9 %copy-start.4 = (f32[3,128,8,253]{3,2,1,0:T(8,128)S(1)}, f32[3,128,8,253]{3,2,1,0:T(8,128)}, u32[]{:S(2)}) copy-start(f32[3,128,8,253]{3,2,1,0:T(8,128)} %get-tuple-element.20) | copy-start | bytes 9326596
  56.6 2.6 %copy-start.3 = (f32[3,128,8,254]{3,2,1,0:T(8,128)S(1)}, f32[3,128,8,254]{3,2,1,0:T(8,128)}, u32[]{:S(2)}) copy-start(f32[3,128,8,254]{3,2,1,0:T(8,128)} %get-tuple-element.23) | copy-start | bytes 9363460
  59.2 2.6 %copy-start.2 = (f32[3,128,8,254]{3,2,1,0:T(8,128)S(1)}, f32[3,128,8,254]{3,2,1,0:T(8,128)}, u32[]{:S(2)}) copy-start(f32[3,128,8,254]{3,2,1,0:T(8,128)} %get-tuple-element.24) | copy-start | bytes 9363460
  65.9 2.5 %copy-start.12 = (f32[128]{0:T(128)S(1)}, f32[128]{0:T(128)}, u32[]{:S(2)}) copy-start(f32[128]{0:T(128)} %constant.25) | copy-start | bytes 1540
  65.9 2.5 %copy-start.13 = (f32[128]{0:T(128)S(1)}, f32[128]{0:T(128)}, u32[]{:S(2)}) copy-start(f32[128]{0:T(128)} %constant.23) | copy-start | bytes 1540
  80.9 5.5 %copy-start.1 = (f32[3,128,8,256]{3,1,2,0:T(8,128)S(1)}, f32[3,128,8,256]{3,1,2,0:T(8,128)}, u32[]{:S(2)}) copy-start(f32[3,128,8,256]{3,1,2,0:T(8,128)} %get-tuple-element.5) | copy-start | bytes 9437188
where the time goes:
time: 90.3 us; the launch traced here: 90 us
  local copies, waits for them, and re-layouts  59.4 us (66%)
  other arithmetic  13.2 us (15%)
  starting transfers between devices  12.6 us (14%)
  matrix products  3.96 us (4%)
    unnamed x49, local copies, waits for them, and re-layouts  36.2 us
    neg x1, other arithmetic, on_device(): advection = -(speed_u * along_x + speed_v * along_y + speed_w * along_z)  12.6 us
    ppermute x3, starting transfers between devices, extended_2(): lax.ppermute(lax.slice_in_dim(block, 0, width, axis=dim), axis, backward)  9.82 us
    slice x2, local copies, waits for them, and re-layouts, explicit_z(): total = total + SECOND * (jnp.roll(field, -2, 3) - jnp.roll(field, 2, 3))  5.97 us
    slice x2, local copies, waits for them, and re-layouts, explicit_z(): return total + THIRD * (jnp.roll(field, -3, 3) - jnp.roll(field, 3, 3))  5.78 us
    slice x2, local copies, waits for them, and re-layouts, extended_2(): lax.slice_in_dim(block, 0, width, axis=dim)  4.22 us
    dot_general x1, matrix products, apply_rows(): jnp.einsum('ij,cjyz->ciyz', table, values, precision=lax.Precision.HIGHEST)  3.96 us
    mul x4, local copies, waits for them, and re-layouts, on_device(): advection = -(speed_u * along_x + speed_v * along_y + speed_w * along_z)  3.19 us
  transfers between devices with their start and end apart: 6, of which 0 were waited for; matrix products, arithmetic and copies ran while one was open for 56% of the time, Pallas kernels for 0%

commit v1 on v0

v1 whole, which is shorter than its diff:
```python
import functools

import jax
import jax.numpy as jnp
import numpy as np
from jax import lax
from jax.experimental import pallas as pl
from jax.experimental.pallas import tpu as pltpu
from jax.sharding import PartitionSpec as P

ALPHA = 1.0 / 3.0
ROOT = (-1.0 + np.sqrt(1.0 - 4.0 * ALPHA * ALPHA)) / (2.0 * ALPHA)
KAPPA = -ALPHA / ROOT
NEAR = float(7.0 / 9.0 / KAPPA)
FAR = float(1.0 / 36.0 / KAPPA)
R = float(ROOT)
GAIN = float(1.0 / (1.0 - ROOT * ROOT))
TAPS = {1: 45.0, 2: -9.0, 3: 1.0, -1: -45.0, -2: 9.0, -3: -1.0}
CHUNKS = 1
XB = 32


def z_matrix(n):
    m = np.zeros((n, n), np.float32)
    for k, t in TAPS.items():
        for z in range(n):
            m[(z + k) % n, z] += t
    return m


def y_matrix(tile, xb):
    m = np.zeros((tile, tile), np.float32)
    for k, t in TAPS.items():
        for y in range(tile):
            if 0 <= y + k < tile:
                m[y, y + k] += t
    return np.kron(np.eye(xb, dtype=np.float32), m)


def halo_matrix(tile, xb):
    m = np.zeros((xb, tile, 2, 3, xb), np.float32)
    for k, t in TAPS.items():
        for y in range(tile):
            for x in range(xb):
                if y + k < 0:
                    m[x, y, 0, y + k + 3, x] += t
                if y + k >= tile:
                    m[x, y, 1, y + k - tile, x] += t
    return m.reshape(xb * tile, 6 * xb)


def split_dot(mat, val, flip=False):
    hi = val.astype(jnp.bfloat16)
    lo = (val - hi.astype(jnp.float32)).astype(jnp.bfloat16)
    if flip:
        return jnp.dot(hi, mat, preferred_element_type=jnp.float32) + jnp.dot(
            lo, mat, preferred_element_type=jnp.float32
        )
    return jnp.dot(mat, hi, preferred_element_type=jnp.float32) + jnp.dot(
        mat, lo, preferred_element_type=jnp.float32
    )


def pack_kernel(x0, xs, vel, low, high, buf, sem):
    copies = []
    for zb in range(2):
        cp = pltpu.make_async_copy(
            vel.at[:, pl.ds(x0, xs), :, pl.ds(zb * 128, 128)], buf.at[zb], sem.at[zb]
        )
        cp.start()
        copies.append(cp)
    for zb in range(2):
        copies[zb].wait()
        flat = buf.at[zb].reshape(3 * xs * 8, 128)
        for c in range(3):
            for y in range(3):
                low[c, y, :, zb * 128 : (zb + 1) * 128] = flat[
                    pl.ds(c * xs * 8 + y, xs, stride=8), :
                ]
                high[c, y, :, zb * 128 : (zb + 1) * 128] = flat[
                    pl.ds(c * xs * 8 + 5 + y, xs, stride=8), :
                ]


def pack(vel, k):
    comps, nx, ty, nz = vel.shape
    xs = nx // CHUNKS
    out = jax.ShapeDtypeStruct((comps, 3, xs, nz), jnp.float32)
    return pl.pallas_call(
        functools.partial(pack_kernel, k * xs, xs),
        out_shape=(out, out),
        in_specs=[pl.BlockSpec(memory_space=pl.ANY)],
        out_specs=[pl.BlockSpec(memory_space=pltpu.VMEM)] * 2,
        scratch_shapes=[
            pltpu.VMEM((2, comps, xs, ty, 128), jnp.float32),
            pltpu.SemaphoreType.DMA((2,)),
        ],
        compiler_params=pltpu.CompilerParams(vmem_limit_bytes=16 << 20),
        name="pack",
    )(vel)


def ends_kernel(vel, right, left):
    n = vel.shape[1]

    def step(i, carry):
        p_old, p, t_old, t = carry
        return (p, vel[:, i] + R * p, t, vel[:, n - 1 - i] + R * t)

    def steps(b, carry):
        for j in range(8):
            carry = step(b * 8 + j, carry)
        return carry

    carry = (vel[:, 0], vel[:, 0], vel[:, n - 1], vel[:, n - 1])
    for i in range(1, 8):
        carry = step(i, carry)
    p_old, p, t_old, t = lax.fori_loop(1, n // 8, steps, carry)
    right[0] = p_old
    right[1] = p
    left[0] = GAIN * t
    left[1] = GAIN * (t_old + R * vel[:, 0])


def ends(vel):
    comps, nx, ty, nz = vel.shape
    out = jax.ShapeDtypeStruct((2, comps, ty, nz), jnp.float32)
    return pl.pallas_call(
        ends_kernel,
        out_shape=(out, out),
        in_specs=[pl.BlockSpec(memory_space=pltpu.VMEM)],
        out_specs=[pl.BlockSpec(memory_space=pltpu.VMEM)] * 2,
        compiler_params=pltpu.CompilerParams(vmem_limit_bytes=16 << 20),
        name="ends",
    )(vel)


def main_kernel(vel, from_left, from_right, zmat, ymat, adv, deriv):
    comps, n, ty, nz = vel.shape

    def block(b, _):
        rows = pl.ds(b * XB, XB)
        sv = vel[1, rows].reshape(XB * ty, nz) * (-1.0 / 60.0)
        sw = vel[2, rows].reshape(XB * ty, nz) * (-1.0 / 60.0)
        for c in range(comps):
            f = vel[c, rows].reshape(XB * ty, nz)
            gz = split_dot(zmat[...], f, flip=True)
            gy = split_dot(ymat[...], f)
            adv[c, rows] = (sv * gy + sw * gz).reshape(XB, ty, nz)
        return 0

    lax.fori_loop(0, n // XB, block, 0)

    def forward(i, p):
        p = vel[:, i] + R * p
        deriv[:, i] = p
        return p

    p_left = from_left[1]
    p_end = lax.fori_loop(0, n, forward, p_left, unroll=8)
    h_n = from_right[0] + (GAIN * R) * p_end
    h_n1 = from_right[1] + (GAIN * R * R) * p_end

    def emit(i, h2, h1, h_1, h_2):
        g = NEAR * (h1 - h_1) + FAR * (h2 - h_2)
        deriv[:, i] = g
        adv[:, i] = adv[:, i] - vel[0, i][None] * g

    h_a = deriv[:, n - 1] + R * h_n
    h_b = deriv[:, n - 2] + R * h_a

    def backward(k, carry):
        h4, h3, h2, h1 = carry
        i = n - 3 - k
        h = deriv[:, i] + R * h1
        emit(i + 2, h4, h3, h1, h)
        return (h3, h2, h1, h)

    h4, h3, h2, h1 = lax.fori_loop(
        0, n - 2, backward, (h_n1, h_n, h_a, h_b), unroll=6
    )
    h = p_left + R * h1
    emit(1, h4, h3, h1, h)
    h4, h3, h2, h1 = h3, h2, h1, h
    h = from_left[0] + R * h1
    emit(0, h4, h3, h1, h)


def main(vel, from_left, from_right, zmat, ymat):
    out = jax.ShapeDtypeStruct(vel.shape, jnp.float32)
    return pl.pallas_call(
        main_kernel,
        out_shape=(out, out),
        in_specs=[pl.BlockSpec(memory_space=pltpu.VMEM)] * 5,
        out_specs=[pl.BlockSpec(memory_space=pltpu.VMEM)] * 2,
        compiler_params=pltpu.CompilerParams(vmem_limit_bytes=32 << 20),
        name="inner",
    )(vel, from_left, from_right, zmat, ymat)


def final_kernel(adv_in, speed, low, high, hmat, adv):
    comps, xs, ty, nz = adv.shape
    for b in range(xs // XB):
        rows = slice(b * XB, (b + 1) * XB)
        sv = speed[0, rows].reshape(XB * ty, nz) * (1.0 / 60.0)
        for c in range(comps):
            halo = jnp.concatenate(
                [
                    low[c, :, rows].reshape(3 * XB, nz),
                    high[c, :, rows].reshape(3 * XB, nz),
                ],
                axis=0,
            )
            gy = split_dot(hmat[...], halo)
            adv[c, rows] = adv_in[c, rows] - (sv * gy).reshape(XB, ty, nz)


def final(adv, vel, low, high, hmat, k):
    comps, nx, ty, nz = vel.shape
    xs = low.shape[2]
    return pl.pallas_call(
        final_kernel,
        out_shape=jax.ShapeDtypeStruct(vel.shape, jnp.float32),
        grid=(1,),
        in_specs=[
            pl.BlockSpec((comps, xs, ty, nz), lambda i: (0, k, 0, 0)),
            pl.BlockSpec((1, xs, ty, nz), lambda i: (1, k, 0, 0)),
            pl.BlockSpec(memory_space=pltpu.VMEM),
            pl.BlockSpec(memory_space=pltpu.VMEM),
            pl.BlockSpec(memory_space=pltpu.VMEM),
        ],
        out_specs=pl.BlockSpec((comps, xs, ty, nz), lambda i: (0, k, 0, 0)),
        input_output_aliases={0: 0},
        compiler_params=pltpu.CompilerParams(vmem_limit_bytes=32 << 20),
        name="outer",
    )(adv, vel, low, high, hmat)


def shift(x, axis, step):
    count = lax.axis_size(axis)
    return lax.ppermute(x, axis, [(i, (i + step) % count) for i in range(count)])


def on_device(vel):
    comps, nx, ty, nz = vel.shape
    zmat = jnp.asarray(z_matrix(nz), jnp.bfloat16)
    ymat = jnp.asarray(y_matrix(ty, XB), jnp.bfloat16)
    hmat = jnp.asarray(halo_matrix(ty, XB), jnp.bfloat16)
    halos = []
    for k in range(CHUNKS):
        low_rows, high_rows = pack(vel, k)
        halos.append((shift(high_rows, "cross", 1), shift(low_rows, "cross", -1)))
    right, left = ends(vel)
    from_left = shift(right, "line", 1)
    from_right = shift(left, "line", -1)
    adv, deriv = main(vel, from_left, from_right, zmat, ymat)
    for k in range(CHUNKS):
        low, high = halos[k]
        adv = final(adv, vel, low, high, hmat, k)
    return adv, deriv


def solution(mesh):
    spec = P(None, "line", "cross", None)
    return jax.shard_map(
        on_device, mesh=mesh, in_specs=(spec,), out_specs=(spec, spec), check_vma=False
    )
```

time: 90.3 us -> 29.7 us (0.33)
  local copies, waits for them, and re-layouts: 59.4 us -> 1.9 us
  other arithmetic: 13.2 us -> 0 us
  Pallas kernels: 0 us -> 12.5 us
  waiting for transfers between devices: 0.02 us -> 4.41 us
  matrix products: 3.96 us -> 0 us
  starting transfers between devices: 12.6 us -> 10 us
    unnamed x49 -> x10, local copies, waits for them, and re-layouts: 36.2 us -> 1.9 us
    slice x9 -> x0, local copies, waits for them, and re-layouts: 18.7 us -> none  [the longest x2 5.97 us: explicit_z(): total = total + SECOND * (jnp.roll(field, -2, 3) - jnp.roll(field, 2, 3))]
    neg x1 -> x0, other arithmetic: 12.6 us -> none  [on_device(): advection = -(speed_u * along_x + speed_v * along_y + speed_w * along_z)]
    pallas_call x0 -> x4, Pallas kernels: none -> 12.5 us  [the longest x1 6.74 us: main(): pl.pallas_call(main_kernel, out_shape=(out, out), in_specs=[pl.BlockSpec(...]
    ppermute x6 -> x4, waiting for transfers between devices: 0.02 us -> 4.41 us  [shift(): lax.ppermute(x, axis, [(i, (i + step) % count) for i in range(count)])]
    dot_general x1 -> x0, matrix products: 3.96 us -> none  [apply_rows(): jnp.einsum('ij,cjyz->ciyz', table, values, precision=lax.Precision.HIGHEST)]
    mul x4 -> x0, local copies, waits for them, and re-layouts: 3.19 us -> none  [on_device(): advection = -(speed_u * along_x + speed_v * along_y + speed_w * along_z)]
    ppermute x6 -> x4, starting transfers between devices: 12.6 us -> 10 us  [shift(): lax.ppermute(x, axis, [(i, (i + step) % count) for i in range(count)])]
  transfers between devices with their start and end apart: 6 -> 4, of which waited for: 0 -> 3; matrix products, arithmetic and copies ran while one was open for 56% -> 0% of each run, Pallas kernels for 0% -> 25%
where the time goes in v1:
time: 29.7 us; the launch traced here: 29.5 us
  Pallas kernels  12.5 us (42%)
  starting transfers between devices  10 us (34%)
  waiting for transfers between devices  4.41 us (15%)
  local copies, waits for them, and re-layouts  1.9 us (6%)
  between operations  0.67 us (2%)
    ppermute x4, starting transfers between devices, shift(): lax.ppermute(x, axis, [(i, (i + step) % count) for i in range(count)])  10 us
    pallas_call x1, Pallas kernels, main(): pl.pallas_call(main_kernel, out_shape=(out, out), in_specs=[pl.BlockSpec(...  6.74 us
    pallas_call x1, Pallas kernels, final(): pl.pallas_call(final_kernel, out_shape=jax.ShapeDtypeStruct(vel.shape, jn...  4.64 us
    ppermute x4, waiting for transfers between devices, shift(): lax.ppermute(x, axis, [(i, (i + step) % count) for i in range(count)])  4.41 us
    unnamed x10, local copies, waits for them, and re-layouts  1.9 us
    pallas_call x1, Pallas kernels, pack(): pl.pallas_call(functools.partial(pack_kernel, k * xs, xs), out_shape=(out...  0.64 us
  transfers between devices with their start and end apart: 4, of which 3 were waited for; matrix products, arithmetic and copies ran while one was open for 0% of the time, Pallas kernels for 25%

profile of v1, /device:TPU:6, one launch (start us, length us, event | category | flops | bytes accessed | tf_op | source)
XLA Modules:
  0.0 29.5 jit_solution(4712566475796146207)
XLA Ops:
  0.6 0.0 copy-start
  0.6 1.9 %copy-done = f32[3,128,8,256]{3,2,1,0:T(8,128)S(1)} copy-done((f32[3,128,8,256]{3,2,1,0:T(8,128)S(1)}, f32[3,128,8,256]{3,2,1,0:T(8,128)}, u32[]{:S(2)}) %copy-start) | copy-done | bytes 3145752
  2.5 0.0 copy-start.1
  2.5 0.0 copy-start.3
  2.5 0.0 copy-start.4
  2.5 0.6 %pack.1 = (f32[3,3,128,256]{3,2,1,0:T(8,128)S(1)}, f32[3,3,128,256]{3,2,1,0:T(8,128)S(1)}) custom-call(f32[3,128,8,256]{3,2,1,0:T(8,128)S(1)} %copy-done), custom_call_target="tpu_custom_call" | custom-call | tf_op jit(solution)/shard_map/pack/pallas_call | solution.py:89
  3.2 0.1 collective-permute-start.2
  3.3 0.0 copy-start.2
  3.3 7.8 %collective-permute-start.3 = (f32[3,3,128,256]{3,2,1,0:T(8,128)S(1)}, f32[3,3,128,256]{3,2,1,0:T(8,128)S(1)}, u32[]{:S(2)}, u32[]{:S(2)}) collective-permute-start(f32[3,3,128,256]{3,2,1,0:T(8,128)S(1)} %get-tuple-element.12), channel_id=1, source_target_pairs={{0,63},{1,0},{2,1},{3,2},{4,3},{5,4},{6,5},{7,6},{8,7},{9,8},{10,9... | collective-permute-start | bytes 3538952 | tf_op jit(solution)/shard_map/ppermute | solution.py:241
  11.1 0.5 %ends.1 = (f32[2,3,8,256]{3,2,1,0:T(8,128)S(1)}, f32[2,3,8,256]{3,2,1,0:T(8,128)S(1)}) custom-call(f32[3,128,8,256]{3,2,1,0:T(8,128)S(1)} %copy-done), custom_call_target="tpu_custom_call" | custom-call | tf_op jit(solution)/shard_map/ends/pallas_call | solution.py:128
  11.6 0.6 %collective-permute-start = (f32[2,3,8,256]{3,2,1,0:T(8,128)S(1)}, f32[2,3,8,256]{3,2,1,0:T(8,128)S(1)}, u32[]{:S(2)}, u32[]{:S(2)}) collective-permute-start(f32[2,3,8,256]{3,2,1,0:T(8,128)S(1)} %get-tuple-element.8), channel_id=1, source_target_pairs={{0,64},{64,128},{128,192},{192,0},{1,65},{65,129},{129,193},{193,1... | collective-permute-start | bytes 147464 | tf_op jit(solution)/shard_map/ppermute | solution.py:241
  12.2 1.5 %collective-permute-start.1 = (f32[2,3,8,256]{3,2,1,0:T(8,128)S(1)}, f32[2,3,8,256]{3,2,1,0:T(8,128)S(1)}, u32[]{:S(2)}, u32[]{:S(2)}) collective-permute-start(f32[2,3,8,256]{3,2,1,0:T(8,128)S(1)} %get-tuple-element.9), channel_id=1, source_target_pairs={{0,192},{64,0},{128,64},{192,128},{1,193},{65,1},{129,65},{193,129... | collective-permute-start | bytes 147464 | tf_op jit(solution)/shard_map/ppermute | solution.py:241
  13.7 2.1 %collective-permute-done.from_left = f32[2,3,8,256]{3,2,1,0:T(8,128)S(1)} collective-permute-done((f32[2,3,8,256]{3,2,1,0:T(8,128)S(1)}, f32[2,3,8,256]{3,2,1,0:T(8,128)S(1)}, u32[]{:S(2)}, u32[]{:S(2)}) %collective-permute-start) | collective-permute-done | bytes 49184 | tf_op jit(solution)/shard_map/ppermute | solution.py:241
  15.8 1.7 %collective-permute-done.1.from_right = f32[2,3,8,256]{3,2,1,0:T(8,128)S(1)} collective-permute-done((f32[2,3,8,256]{3,2,1,0:T(8,128)S(1)}, f32[2,3,8,256]{3,2,1,0:T(8,128)S(1)}, u32[]{:S(2)}, u32[]{:S(2)}) %collective-permute-start.1) | collective-permute-done | bytes 49184 | tf_op jit(solution)/shard_map/ppermute | solution.py:241
  17.5 0.0 copy-done.1
  17.5 0.0 copy-done.3
  17.5 0.0 copy-done.4
  17.5 6.7 %inner.1 = (f32[3,128,8,256]{3,2,1,0:T(8,128)}, f32[3,128,8,256]{3,2,1,0:T(8,128)}) custom-call(f32[3,128,8,256]{3,2,1,0:T(8,128)S(1)} %copy-done.1, f32[2,3,8,256]{3,2,1,0:T(8,128)S(1)} %collective-permute-done.from_left, f32[2,3,8,256]{3,2,1,0:T(8,128)S(1)} %collective-permute-done.1.from_right, bf16[256,256]{1,0:T(8,128)(2,1)S(1)} %copy-done.4, ...), custom_call_target="tpu_custom_call" | custom-call | tf_op jit(solution)/shard_map/inner/pallas_call | solution.py:191
  24.2 0.7 %collective-permute-done.2.low = f32[3,3,128,256]{3,2,1,0:T(8,128)S(1)} collective-permute-done((f32[3,3,128,256]{3,2,1,0:T(8,128)S(1)}, f32[3,3,128,256]{3,2,1,0:T(8,128)S(1)}, u32[]{:S(2)}, u32[]{:S(2)}) %collective-permute-start.2) | collective-permute-done | bytes 1179680 | tf_op jit(solution)/shard_map/ppermute | solution.py:241
  24.9 0.0 collective-permute-done.3.high
  24.9 0.0 copy-done.2
  24.9 4.6 %outer.1 = f32[3,128,8,256]{3,2,1,0:T(8,128)} custom-call(f32[3,128,8,256]{3,2,1,0:T(8,128)} %get-tuple-element.10.adv_in, f32[3,128,8,256]{3,2,1,0:T(8,128)S(1)} %copy-done.1, f32[3,3,128,256]{3,2,1,0:T(8,128)S(1)} %collective-permute-done.2.low, f32[3,3,128,256]{3,2,1,0:T(8,128)S(1)} %collective-permute-done.3.high, ...), custom_call_target="tpu_custom_call", output_to_operand_aliasing={{}: (0, {})} | custom-call | tf_op jit(solution)/shard_map/outer/pallas_call | solution.py:221
Async XLA Ops:
  0.6 1.9 %copy-start = (f32[3,128,8,256]{3,2,1,0:T(8,128)S(1)}, f32[3,128,8,256]{3,2,1,0:T(8,128)}, u32[]{:S(2)}) copy-start(f32[3,128,8,256]{3,2,1,0:T(8,128)} %speed.1) | copy-start | bytes 9437188
  2.5 15.0 %copy-start.1 = (f32[3,128,8,256]{3,2,1,0:T(8,128)S(1)}, f32[3,128,8,256]{3,2,1,0:T(8,128)}, u32[]{:S(2)}) copy-start(f32[3,128,8,256]{3,2,1,0:T(8,128)} %speed.1) | copy-start | bytes 9437188
  2.5 15.0 %copy-start.3 = (bf16[256,256]{1,0:T(8,128)(2,1)S(1)}, bf16[256,256]{1,0:T(8,128)(2,1)}, u32[]{:S(2)}) copy-start(bf16[256,256]{1,0:T(8,128)(2,1)} %constant.7.clone.ymat) | copy-start | bytes 393220
  2.5 15.0 %copy-start.4 = (bf16[256,256]{1,0:T(8,128)(2,1)S(1)}, bf16[256,256]{1,0:T(8,128)(2,1)}, u32[]{:S(2)}) copy-start(bf16[256,256]{1,0:T(8,128)(2,1)} %constant.6.clone.zmat) | copy-start | bytes 393220
  3.2 21.7 %collective-permute-start.2 = (f32[3,3,128,256]{3,2,1,0:T(8,128)S(1)}, f32[3,3,128,256]{3,2,1,0:T(8,128)S(1)}, u32[]{:S(2)}, u32[]{:S(2)}) collective-permute-start(f32[3,3,128,256]{3,2,1,0:T(8,128)S(1)} %get-tuple-element.11), channel_id=1, source_target_pairs={{0,1},{1,2},{2,3},{3,4},{4,5},{5,6},{6,7},{7,8},{8,9},{9,10},{10,1... | collective-permute-start | bytes 3538952 | tf_op jit(solution)/shard_map/ppermute | solution.py:241
  3.3 21.6 %copy-start.2 = (bf16[256,192]{1,0:T(8,128)(2,1)S(1)}, bf16[256,192]{1,0:T(8,128)(2,1)}, u32[]{:S(2)}) copy-start(bf16[256,192]{1,0:T(8,128)(2,1)} %constant.8.clone.hmat) | copy-start | bytes 294916
  3.3 21.6 %collective-permute-start.3 = (f32[3,3,128,256]{3,2,1,0:T(8,128)S(1)}, f32[3,3,128,256]{3,2,1,0:T(8,128)S(1)}, u32[]{:S(2)}, u32[]{:S(2)}) collective-permute-start(f32[3,3,128,256]{3,2,1,0:T(8,128)S(1)} %get-tuple-element.12), channel_id=1, source_target_pairs={{0,63},{1,0},{2,1},{3,2},{4,3},{5,4},{6,5},{7,6},{8,7},{9,8},{10,9... | collective-permute-start | bytes 3538952 | tf_op jit(solution)/shard_map/ppermute | solution.py:241
  11.6 4.2 %collective-permute-start = (f32[2,3,8,256]{3,2,1,0:T(8,128)S(1)}, f32[2,3,8,256]{3,2,1,0:T(8,128)S(1)}, u32[]{:S(2)}, u32[]{:S(2)}) collective-permute-start(f32[2,3,8,256]{3,2,1,0:T(8,128)S(1)} %get-tuple-element.8), channel_id=1, source_target_pairs={{0,64},{64,128},{128,192},{192,0},{1,65},{65,129},{129,193},{193,1... | collective-permute-start | bytes 147464 | tf_op jit(solution)/shard_map/ppermute | solution.py:241
  12.2 5.3 %collective-permute-start.1 = (f32[2,3,8,256]{3,2,1,0:T(8,128)S(1)}, f32[2,3,8,256]{3,2,1,0:T(8,128)S(1)}, u32[]{:S(2)}, u32[]{:S(2)}) collective-permute-start(f32[2,3,8,256]{3,2,1,0:T(8,128)S(1)} %get-tuple-element.9), channel_id=1, source_target_pairs={{0,192},{64,0},{128,64},{192,128},{1,193},{65,1},{129,65},{193,129... | collective-permute-start | bytes 147464 | tf_op jit(solution)/shard_map/ppermute | solution.py:241

commit v2 on v1

v2 whole, which is shorter than its diff:
```python
import functools

import jax
import jax.numpy as jnp
import numpy as np
from jax import lax
from jax.experimental import pallas as pl
from jax.experimental.pallas import tpu as pltpu
from jax.sharding import PartitionSpec as P

ALPHA = 1.0 / 3.0
ROOT = (-1.0 + np.sqrt(1.0 - 4.0 * ALPHA * ALPHA)) / (2.0 * ALPHA)
KAPPA = -ALPHA / ROOT
NEAR = float(7.0 / 9.0 / KAPPA)
FAR = float(1.0 / 36.0 / KAPPA)
R = float(ROOT)
GAIN = float(1.0 / (1.0 - ROOT * ROOT))
TAPS = {1: 45.0, 2: -9.0, 3: 1.0, -1: -45.0, -2: 9.0, -3: -1.0}
CHUNKS = (32, 64, 32)
XB = 32
LB = 16
EB = 8
LANES = 128


def z_matrix(n):
    m = np.zeros((n, n), np.float32)
    for k, t in TAPS.items():
        for z in range(n):
            m[(z + k) % n, z] += t
    return m


def y_matrix(tile, xb):
    m = np.zeros((tile, tile), np.float32)
    for k, t in TAPS.items():
        for y in range(tile):
            if 0 <= y + k < tile:
                m[y, y + k] += t
    return np.kron(np.eye(xb, dtype=np.float32), m)


def halo_matrix(tile, xb):
    m = np.zeros((xb, tile, 2, 3, xb), np.float32)
    for k, t in TAPS.items():
        for y in range(tile):
            for x in range(xb):
                if y + k < 0:
                    m[x, y, 0, y + k + 3, x] += t
                if y + k >= tile:
                    m[x, y, 1, y + k - tile, x] += t
    return m.reshape(xb * tile, 6 * xb)


def split_dot(mat, val, flip=False):
    hi = val.astype(jnp.bfloat16)
    lo = (val - hi.astype(jnp.float32)).astype(jnp.bfloat16)
    if flip:
        return jnp.dot(hi, mat, preferred_element_type=jnp.float32) + jnp.dot(
            lo, mat, preferred_element_type=jnp.float32
        )
    return jnp.dot(mat, hi, preferred_element_type=jnp.float32) + jnp.dot(
        mat, lo, preferred_element_type=jnp.float32
    )


def pack_rows(held, low, high, row, x0, xs):
    halves, comps, n, tile, lanes = held.shape
    flat = held.reshape(halves * comps * n * tile, lanes)
    for half in range(halves):
        cols = pl.ds(half * lanes, lanes)
        for c in range(comps):
            for y in range(3):
                start = ((half * comps + c) * n + row) * tile + y
                low[c, y, pl.ds(x0, xs), cols] = flat[pl.ds(start, xs, stride=tile)]
                high[c, y, pl.ds(x0, xs), cols] = flat[
                    pl.ds(start + tile - 3, xs, stride=tile)
                ]


def fetch(vel, held, sems, row, count, at):
    copies = []
    for half in range(held.shape[0]):
        copies.append(
            pltpu.make_async_copy(
                vel.at[:, pl.ds(row, count), :, pl.ds(half * LANES, LANES)],
                held.at[half, :, pl.ds(at, count)],
                sems.at[half],
            )
        )
        copies[-1].start()
    return copies


def rows_of(held, c, rows):
    both = [held[half, c, rows] for half in range(held.shape[0])]
    return jnp.concatenate([h.reshape(-1, LANES) for h in both], axis=1)


def put_rows(held, c, rows, val):
    tile = held.shape[3]
    for half in range(held.shape[0]):
        held[half, c, rows] = val[:, half * LANES : (half + 1) * LANES].reshape(
            -1, tile, LANES
        )


def pack_kernel(xs, vel, low, high, buf, sems):
    for cp in fetch(vel, buf, sems, 0, xs, 0):
        cp.wait()
    pack_rows(buf, low, high, 0, 0, xs)


def held_shape(vel, n=None):
    comps, nx, tile, nz = vel.shape
    return pltpu.VMEM((nz // LANES, comps, n or nx, tile, LANES), jnp.float32)


def halo_shape(vel, xs):
    return pltpu.VMEM((vel.shape[0], 3, xs, vel.shape[3]), jnp.float32)


def in_hbm(x):
    return pltpu.with_memory_space_constraint(x, pltpu.HBM)


def pack(vel, xs):
    _, _, _, nz = vel.shape
    return pl.pallas_call(
        functools.partial(pack_kernel, xs),
        out_shape=(halo_shape(vel, xs),) * 2,
        in_specs=[pl.BlockSpec(memory_space=pltpu.HBM)],
        out_specs=[pl.BlockSpec(memory_space=pltpu.VMEM)] * 2,
        scratch_shapes=[
            held_shape(vel, xs),
            pltpu.SemaphoreType.DMA((nz // LANES,)),
        ],
        compiler_params=pltpu.CompilerParams(vmem_limit_bytes=8 << 20),
        name="pack",
    )(in_hbm(vel))


def load_kernel(chunks, vel_in, *refs):
    vel, right, left = refs[:3]
    sends, sems = refs[3:-1], refs[-1]
    n = vel.shape[2]
    copies = [
        fetch(vel_in, vel, sems.at[b], b * LB, LB, b * LB) for b in range(n // LB)
    ]
    where = []
    x0 = 0
    for k, xs in enumerate(chunks):
        where += [(k, x0)] * (xs // LB)
        x0 += xs
    p_old = p = t = t_one = None
    power = 1.0
    for b in range(n // LB):
        for cp in copies[b]:
            cp.wait()
        k, x0 = where[b]
        if k > 0:
            pack_rows(
                vel, sends[2 * k - 2], sends[2 * k - 1], b * LB, b * LB - x0, LB
            )
        for i in range(b * LB, (b + 1) * LB):
            f = vel[:, :, i]
            if i == 0:
                p, t = f, f
            else:
                p_old, p = p, f + R * p
                t = t + float(np.float32(power)) * f
            power *= R
    right[0] = p_old
    right[1] = p
    first = vel[:, :, 0]
    left[0] = GAIN * t
    left[1] = GAIN * ((t - first) * (1.0 / R) + R * first)


def load(vel, chunks):
    comps, nx, tile, nz = vel.shape
    edge = pltpu.VMEM((2, nz // LANES, comps, tile, LANES), jnp.float32)
    outs = [held_shape(vel), edge, edge]
    for xs in chunks[1:]:
        outs += [halo_shape(vel, xs)] * 2
    return pl.pallas_call(
        functools.partial(load_kernel, chunks),
        out_shape=tuple(outs),
        in_specs=[pl.BlockSpec(memory_space=pltpu.HBM)],
        out_specs=[pl.BlockSpec(memory_space=pltpu.VMEM)] * len(outs),
        scratch_shapes=[pltpu.SemaphoreType.DMA((nx // LB, nz // LANES))],
        compiler_params=pltpu.CompilerParams(vmem_limit_bytes=16 << 20),
        name="load",
    )(in_hbm(vel))


def inner_kernel(vel, zmat, ymat, adv):
    _, comps, n, _, _ = vel.shape

    def block(b, _):
        rows = pl.ds(b * XB, XB)
        sv = rows_of(vel, 1, rows) * (-1.0 / 60.0)
        sw = rows_of(vel, 2, rows) * (-1.0 / 60.0)
        for c in range(comps):
            f = rows_of(vel, c, rows)
            gz = split_dot(zmat[...], f, flip=True)
            gy = split_dot(ymat[...], f)
            put_rows(adv, c, rows, sv * gy + sw * gz)
        return 0

    lax.fori_loop(0, n // XB, block, 0)


def inner(vel, zmat, ymat):
    return pl.pallas_call(
        inner_kernel,
        out_shape=pltpu.VMEM(vel.shape, jnp.float32),
        in_specs=[pl.BlockSpec(memory_space=pltpu.VMEM)] * 3,
        out_specs=pl.BlockSpec(memory_space=pltpu.VMEM),
        compiler_params=pltpu.CompilerParams(vmem_limit_bytes=8 << 20),
        name="inner",
    )(vel, zmat, ymat)


def along_kernel(vel, from_left, from_right, adv_in, adv, deriv_out, deriv, sems):
    halves, _, n, _, _ = vel.shape

    def forward(b, p):
        for j in range(EB):
            i = b * EB + j
            p = vel[:, :, i] + R * p
            deriv[:, :, i] = p
        return p

    p_left = from_left[1]
    p_end = lax.fori_loop(0, n // EB, forward, p_left)
    h_n = from_right[0] + (GAIN * R) * p_end
    h_n1 = from_right[1] + (GAIN * R * R) * p_end
    h_a = deriv[:, :, n - 1] + R * h_n
    h_b = deriv[:, :, n - 2] + R * h_a

    def copy_out(b):
        rows = pl.ds(b * EB, EB)
        return [
            pltpu.make_async_copy(
                deriv.at[half, :, rows],
                deriv_out.at[:, rows, :, pl.ds(half * LANES, LANES)],
                sems.at[b, half],
            )
            for half in range(halves)
        ]

    def backward(b, carry, last=False):
        h4, h3, h2, h1 = carry
        for j in range(EB):
            i = b * EB + EB - 1 - j
            if last and i < 2:
                p = p_left if i == 1 else from_left[0]
            else:
                p = deriv[:, :, i - 2]
            h = p + R * h1
            g = NEAR * (h3 - h1) + FAR * (h4 - h)
            deriv[:, :, i] = g
            adv[:, :, i] = adv_in[:, :, i] - vel[:, 0, i][:, None] * g
            h4, h3, h2, h1 = h3, h2, h1, h
        for cp in copy_out(b):
            cp.start()
        return (h4, h3, h2, h1)

    blocks = n // EB
    carry = lax.fori_loop(
        0, blocks - 1, lambda k, c: backward(blocks - 1 - k, c), (h_n1, h_n, h_a, h_b)
    )
    backward(0, carry, last=True)
    for b in range(blocks):
        for cp in copy_out(b):
            cp.wait()


def along(vel, from_left, from_right, adv):
    halves, comps, nx, tile, lanes = vel.shape
    return pl.pallas_call(
        along_kernel,
        out_shape=(pltpu.VMEM(vel.shape, jnp.float32), jax.ShapeDtypeStruct((comps, nx, tile, halves * lanes), jnp.float32)),
        in_specs=[pl.BlockSpec(memory_space=pltpu.VMEM)] * 4,
        out_specs=[
            pl.BlockSpec(memory_space=pltpu.VMEM),
            pl.BlockSpec(memory_space=pl.ANY),
        ],
        scratch_shapes=[
            pltpu.VMEM(vel.shape, jnp.float32),
            pltpu.SemaphoreType.DMA((nx // EB, halves)),
        ],
        input_output_aliases={3: 0},
        compiler_params=pltpu.CompilerParams(vmem_limit_bytes=16 << 20),
        name="along",
    )(vel, from_left, from_right, adv)


def outer_kernel(x0, *refs):
    vel, adv_in, low, high, hmat = refs[:5]
    adv_out, adv, sems = refs[-3:]
    halves, comps, xs, _, lanes = adv.shape
    copies = []
    for b in range(xs // XB):
        here = pl.ds(b * XB, XB)
        rows = pl.ds(x0 + b * XB, XB)
        sv = rows_of(vel, 1, rows) * (1.0 / 60.0)
        for c in range(comps):
            halo = jnp.concatenate(
                [
                    low[c, :, here].reshape(-1, halves * lanes),
                    high[c, :, here].reshape(-1, halves * lanes),
                ],
                axis=0,
            )
            gy = split_dot(hmat[...], halo)
            put_rows(adv, c, here, rows_of(adv_in, c, rows) - sv * gy)
            for half in range(halves):
                copies.append(
                    pltpu.make_async_copy(
                        adv.at[half, c, here],
                        adv_out.at[c, rows, :, pl.ds(half * LANES, LANES)],
                        sems.at[b * comps + c, half],
                    )
                )
                copies[-1].start()
    for cp in copies:
        cp.wait()


def outer(vel, adv, low, high, hmat, x0, out):
    halves, comps, nx, tile, lanes = vel.shape
    xs = low.shape[2]
    args = [vel, adv, low, high, hmat]
    specs = [pl.BlockSpec(memory_space=pltpu.VMEM)] * 5
    alias = {}
    if out is not None:
        args.append(out)
        specs.append(pl.BlockSpec(memory_space=pl.ANY))
        alias = {5: 0}
    return pl.pallas_call(
        functools.partial(outer_kernel, x0),
        out_shape=jax.ShapeDtypeStruct((comps, nx, tile, halves * lanes), jnp.float32),
        in_specs=specs,
        out_specs=pl.BlockSpec(memory_space=pl.ANY),
        scratch_shapes=[
            pltpu.VMEM((halves, comps, xs, tile, lanes), jnp.float32),
            pltpu.SemaphoreType.DMA((comps * (xs // XB), halves)),
        ],
        input_output_aliases=alias,
        compiler_params=pltpu.CompilerParams(vmem_limit_bytes=8 << 20),
        name="outer",
    )(*args)


def shift(x, axis, step):
    count = lax.axis_size(axis)
    return lax.ppermute(x, axis, [(i, (i + step) % count) for i in range(count)])


def on_device(vel):
    _, _, tile, nz = vel.shape
    zmat = jnp.asarray(z_matrix(nz), jnp.bfloat16)
    ymat = jnp.asarray(y_matrix(tile, XB), jnp.bfloat16)
    hmat = jnp.asarray(halo_matrix(tile, XB), jnp.bfloat16)
    sends = list(pack(vel, CHUNKS[0]))
    held, right, left, *rest = load(vel, CHUNKS)
    sends += rest
    halos = []
    for k in range(len(CHUNKS)):
        low_rows, high_rows = sends[2 * k : 2 * k + 2]
        halos.append((shift(high_rows, "cross", 1), shift(low_rows, "cross", -1)))
    from_left = shift(right, "line", 1)
    from_right = shift(left, "line", -1)
    adv = inner(held, zmat, ymat)
    adv, deriv = along(held, from_left, from_right, adv)
    out = None
    x0 = 0
    for xs, (low, high) in zip(CHUNKS, halos):
        out = outer(held, adv, low, high, hmat, x0, out)
        x0 += xs
    return out, deriv


def solution(mesh):
    spec = P(None, "line", "cross", None)
    return jax.shard_map(
        on_device,
        mesh=mesh,
        in_specs=(spec,),
        out_specs=(spec, spec),
        check_vma=False,
    )
```

time: 29.7 us -> 34.9 us (1.18)
  starting transfers between devices: 10 us -> 18.1 us
  local copies, waits for them, and re-layouts: 1.9 us -> 0.02 us
  waiting for transfers between devices: 4.41 us -> 3.24 us
    ppermute x4 -> x8, starting transfers between devices: 10 us -> 18.1 us  [shift(): lax.ppermute(x, axis, [(i, (i + step) % count) for i in range(count)])]
    unnamed x10 -> x6, local copies, waits for them, and re-layouts: 1.9 us -> 0.02 us
    ppermute x4 -> x8, waiting for transfers between devices: 4.41 us -> 3.24 us  [shift(): lax.ppermute(x, axis, [(i, (i + step) % count) for i in range(count)])]
    pallas_call x4 -> x7, Pallas kernels: 12.5 us -> 12.6 us  [the longest x3 4.07 us: outer(): pl.pallas_call(functools.partial(outer_kernel, x0), out_shape=jax.ShapeDt...]
  transfers between devices with their start and end apart: 4 -> 8, of which waited for: 3 -> 2; matrix products, arithmetic and copies ran while one was open for 0% -> 0% of each run, Pallas kernels for 25% -> 26%
where the time goes in v2:
time: 34.9 us; the launch traced here: 34.8 us
  starting transfers between devices  18.1 us (52%)
  Pallas kernels  12.6 us (36%)
  waiting for transfers between devices  3.24 us (9%)
  between operations  0.77 us (2%)
    ppermute x8, starting transfers between devices, shift(): lax.ppermute(x, axis, [(i, (i + step) % count) for i in range(count)])  18.1 us
    pallas_call x3, Pallas kernels, outer(): pl.pallas_call(functools.partial(outer_kernel, x0), out_shape=jax.ShapeDt...  4.07 us
    ppermute x8, waiting for transfers between devices, shift(): lax.ppermute(x, axis, [(i, (i + step) % count) for i in range(count)])  3.24 us
    pallas_call x1, Pallas kernels, along(): pl.pallas_call(along_kernel, out_shape=(pltpu.VMEM(vel.shape, jnp.float32...  2.59 us
    pallas_call x1, Pallas kernels, inner(): pl.pallas_call(inner_kernel, out_shape=pltpu.VMEM(vel.shape, jnp.float32)...  2.39 us
    pallas_call x1, Pallas kernels, load(): pl.pallas_call(functools.partial(load_kernel, chunks), out_shape=tuple(ou...  2.34 us
    pallas_call x1, Pallas kernels, pack(): pl.pallas_call(functools.partial(pack_kernel, xs), out_shape=(halo_shape(...  1.25 us
  transfers between devices with their start and end apart: 8, of which 2 were waited for; matrix products, arithmetic and copies ran while one was open for 0% of the time, Pallas kernels for 26%

profile of v2, /device:TPU:6, one launch (start us, length us, event | category | flops | bytes accessed | tf_op | source)
XLA Modules:
  0.0 34.8 jit_solution(1662016272066457129)
XLA Ops:
  0.6 0.0 copy-start.1
  0.6 0.0 copy-start.2
  0.7 2.3 %load.1 = (f32[2,3,128,8,128]{4,3,2,1,0:T(8,128)S(1)}, f32[2,2,3,8,128]{4,3,2,1,0:T(8,128)S(1)}, f32[2,2,3,8,128]{4,3,2,1,0:T(8,128)S(1)}, f32[3,3,64,256]{3,2,1...) custom-call(f32[3,128,8,256]{3,2,1,0:T(8,128)} %vel.1), custom_call_target="tpu_custom_call" | custom-call | tf_op jit(solution)/shard_map/load/pallas_call | solution.py:186
  3.0 0.1 collective-permute-start.4
  3.1 7.8 %collective-permute-start.5 = (f32[3,3,64,256]{3,2,1,0:T(8,128)S(1)}, f32[3,3,64,256]{3,2,1,0:T(8,128)S(1)}, u32[]{:S(2)}, u32[]{:S(2)}) collective-permute-start(f32[3,3,64,256]{3,2,1,0:T(8,128)S(1)} %get-tuple-element.20), channel_id=1, source_target_pairs={{0,63},{1,0},{2,1},{3,2},{4,3},{5,4},{6,5},{7,6},{8,7},{9,8},{10,9... | collective-permute-start | bytes 1769480 | tf_op jit(solution)/shard_map/ppermute | solution.py:359
  10.9 1.3 %pack.1 = (f32[3,3,32,256]{3,2,1,0:T(8,128)S(1)}, f32[3,3,32,256]{3,2,1,0:T(8,128)S(1)}) custom-call(f32[3,128,8,256]{3,2,1,0:T(8,128)} %vel.1), custom_call_target="tpu_custom_call" | custom-call | tf_op jit(solution)/shard_map/pack/pallas_call | solution.py:129
  12.2 0.1 collective-permute-start.6
  12.3 0.6 %collective-permute-start = (f32[2,2,3,8,128]{4,3,2,1,0:T(8,128)S(1)}, f32[2,2,3,8,128]{4,3,2,1,0:T(8,128)S(1)}, u32[]{:S(2)}, u32[]{:S(2)}) collective-permute-start(f32[2,2,3,8,128]{4,3,2,1,0:T(8,128)S(1)} %get-tuple-element.14), channel_id=1, source_target_pairs={{0,64},{64,128},{128,192},{192,0},{1,65},{65,129},{129,193},{193,1... | collective-permute-start | bytes 147464 | tf_op jit(solution)/shard_map/ppermute | solution.py:359
  12.8 1.5 %collective-permute-start.1 = (f32[2,2,3,8,128]{4,3,2,1,0:T(8,128)S(1)}, f32[2,2,3,8,128]{4,3,2,1,0:T(8,128)S(1)}, u32[]{:S(2)}, u32[]{:S(2)}) collective-permute-start(f32[2,2,3,8,128]{4,3,2,1,0:T(8,128)S(1)} %get-tuple-element.15), channel_id=1, source_target_pairs={{0,192},{64,0},{128,64},{192,128},{1,193},{65,1},{129,65},{193,129... | collective-permute-start | bytes 147464 | tf_op jit(solution)/shard_map/ppermute | solution.py:359
  14.4 2.1 %collective-permute-done.from_left = f32[2,2,3,8,128]{4,3,2,1,0:T(8,128)S(1)} collective-permute-done((f32[2,2,3,8,128]{4,3,2,1,0:T(8,128)S(1)}, f32[2,2,3,8,128]{4,3,2,1,0:T(8,128)S(1)}, u32[]{:S(2)}, u32[]{:S(2)}) %collective-permute-start) | collective-permute-done | bytes 49184 | tf_op jit(solution)/shard_map/ppermute | solution.py:359
  16.4 4.1 %collective-permute-start.7 = (f32[3,3,32,256]{3,2,1,0:T(8,128)S(1)}, f32[3,3,32,256]{3,2,1,0:T(8,128)S(1)}, u32[]{:S(2)}, u32[]{:S(2)}) collective-permute-start(f32[3,3,32,256]{3,2,1,0:T(8,128)S(1)} %get-tuple-element.22), channel_id=1, source_target_pairs={{0,63},{1,0},{2,1},{3,2},{4,3},{5,4},{6,5},{7,6},{8,7},{9,8},{10,9... | collective-permute-start | bytes 884744 | tf_op jit(solution)/shard_map/ppermute | solution.py:359
  20.6 0.0 collective-permute-done.1.from_right
  20.6 0.0 collective-permute-start.2
  20.6 1.2 %collective-permute-done.6.refs_2_ = f32[3,3,32,256]{3,2,1,0:T(8,128)S(1)} collective-permute-done((f32[3,3,32,256]{3,2,1,0:T(8,128)S(1)}, f32[3,3,32,256]{3,2,1,0:T(8,128)S(1)}, u32[]{:S(2)}, u32[]{:S(2)}) %collective-permute-start.6) | collective-permute-done | bytes 294944 | tf_op jit(solution)/shard_map/ppermute | solution.py:359
  21.7 3.9 %collective-permute-start.3 = (f32[3,3,32,256]{3,2,1,0:T(8,128)S(1)}, f32[3,3,32,256]{3,2,1,0:T(8,128)S(1)}, u32[]{:S(2)}, u32[]{:S(2)}) collective-permute-start(f32[3,3,32,256]{3,2,1,0:T(8,128)S(1)} %get-tuple-element.18), channel_id=1, source_target_pairs={{0,63},{1,0},{2,1},{3,2},{4,3},{5,4},{6,5},{7,6},{8,7},{9,8},{10,9... | collective-permute-start | bytes 884744 | tf_op jit(solution)/shard_map/ppermute | solution.py:359
  25.6 0.0 copy-done.1
  25.6 0.0 copy-done.2
  25.6 2.4 %inner.1.adv_in = f32[2,3,128,8,128]{4,3,2,1,0:T(8,128)S(1)} custom-call(f32[2,3,128,8,128]{4,3,2,1,0:T(8,128)S(1)} %get-tuple-element.13.vel.refs_0_, bf16[256,256]{1,0:T(8,128)(2,1)S(1)} %copy-done.2, bf16[256,256]{1,0:T(8,128)(2,1)S(1)} %copy-done.1), custom_call_target="tpu_custom_call" | custom-call | tf_op jit(solution)/shard_map/inner/pallas_call | solution.py:215
  28.0 0.0 copy-start
  28.1 2.6 %along.1 = (f32[2,3,128,8,128]{4,3,2,1,0:T(8,128)S(1)}, f32[3,128,8,256]{3,2,1,0:T(8,128)}) custom-call(f32[2,3,128,8,128]{4,3,2,1,0:T(8,128)S(1)} %get-tuple-element.13.vel.refs_0_, f32[2,2,3,8,128]{4,3,2,1,0:T(8,128)S(1)} %collective-permute-done.from_left, ...), custom_call_target="tpu_custom_call", output_to_operand_aliasing={{0}: (3, {})} | custom-call | tf_op jit(solution)/shard_map/along/pallas_call | solution.py:282
  30.7 0.0 collective-permute-done.7.refs_3_
  30.7 0.0 copy-done
  30.7 1.2 %outer.3.refs_5_ = f32[3,128,8,256]{3,2,1,0:T(8,128)} custom-call(f32[2,3,128,8,128]{4,3,2,1,0:T(8,128)S(1)} %get-tuple-element.13.vel.refs_0_, f32[2,3,128,8,128]{4,3,2,1,0:T(8,128)S(1)} %get-tuple-element.16.refs_1_, f32[3,3,32,256]{3,2,1,0:T(8,128)S(1)} %collective-permute-done.6.refs_2_, f32[3,3,32,256]{3,2,1,0:T(8,128)S(1)} %collective-permute-done.7.refs_3_, ...), custom_call_target="tpu_custom_call" | custom-call | tf_op jit(solution)/shard_map/outer/pallas_call | solution.py:342
  31.9 0.0 collective-permute-done.4.refs_2_
  31.9 0.0 collective-permute-done.5.refs_3_
  31.9 1.6 %outer.4.refs_5_ = f32[3,128,8,256]{3,2,1,0:T(8,128)} custom-call(f32[2,3,128,8,128]{4,3,2,1,0:T(8,128)S(1)} %get-tuple-element.13.vel.refs_0_, f32[2,3,128,8,128]{4,3,2,1,0:T(8,128)S(1)} %get-tuple-element.16.refs_1_, f32[3,3,64,256]{3,2,1,0:T(8,128)S(1)} %collective-permute-done.4.refs_2_, ...), custom_call_target="tpu_custom_call", output_to_operand_aliasing={{}: (5, {})} | custom-call | tf_op jit(solution)/shard_map/outer/pallas_call | solution.py:342
  33.5 0.0 collective-permute-done.2.refs_2_
  33.6 0.0 collective-permute-done.3.refs_3_
  33.6 1.2 %outer.5 = f32[3,128,8,256]{3,2,1,0:T(8,128)} custom-call(f32[2,3,128,8,128]{4,3,2,1,0:T(8,128)S(1)} %get-tuple-element.13.vel.refs_0_, f32[2,3,128,8,128]{4,3,2,1,0:T(8,128)S(1)} %get-tuple-element.16.refs_1_, f32[3,3,32,256]{3,2,1,0:T(8,128)S(1)} %collective-permute-done.2.refs_2_, ...), custom_call_target="tpu_custom_call", output_to_operand_aliasing={{}: (5, {})} | custom-call | tf_op jit(solution)/shard_map/outer/pallas_call | solution.py:342
Async XLA Ops:
  0.6 25.0 %copy-start.1 = (bf16[256,256]{1,0:T(8,128)(2,1)S(1)}, bf16[256,256]{1,0:T(8,128)(2,1)}, u32[]{:S(2)}) copy-start(bf16[256,256]{1,0:T(8,128)(2,1)} %constant.7.clone.ymat) | copy-start | bytes 393220
  0.6 25.0 %copy-start.2 = (bf16[256,256]{1,0:T(8,128)(2,1)S(1)}, bf16[256,256]{1,0:T(8,128)(2,1)}, u32[]{:S(2)}) copy-start(bf16[256,256]{1,0:T(8,128)(2,1)} %constant.6.clone.zmat) | copy-start | bytes 393220
  3.0 28.9 %collective-permute-start.4 = (f32[3,3,64,256]{3,2,1,0:T(8,128)S(1)}, f32[3,3,64,256]{3,2,1,0:T(8,128)S(1)}, u32[]{:S(2)}, u32[]{:S(2)}) collective-permute-start(f32[3,3,64,256]{3,2,1,0:T(8,128)S(1)} %get-tuple-element.19), channel_id=1, source_target_pairs={{0,1},{1,2},{2,3},{3,4},{4,5},{5,6},{6,7},{7,8},{8,9},{9,10},{10,1... | collective-permute-start | bytes 1769480 | tf_op jit(solution)/shard_map/ppermute | solution.py:359
  3.1 28.8 %collective-permute-start.5 = (f32[3,3,64,256]{3,2,1,0:T(8,128)S(1)}, f32[3,3,64,256]{3,2,1,0:T(8,128)S(1)}, u32[]{:S(2)}, u32[]{:S(2)}) collective-permute-start(f32[3,3,64,256]{3,2,1,0:T(8,128)S(1)} %get-tuple-element.20), channel_id=1, source_target_pairs={{0,63},{1,0},{2,1},{3,2},{4,3},{5,4},{6,5},{7,6},{8,7},{9,8},{10,9... | collective-permute-start | bytes 1769480 | tf_op jit(solution)/shard_map/ppermute | solution.py:359
  12.2 9.5 %collective-permute-start.6 = (f32[3,3,32,256]{3,2,1,0:T(8,128)S(1)}, f32[3,3,32,256]{3,2,1,0:T(8,128)S(1)}, u32[]{:S(2)}, u32[]{:S(2)}) collective-permute-start(f32[3,3,32,256]{3,2,1,0:T(8,128)S(1)} %get-tuple-element.21), channel_id=1, source_target_pairs={{0,1},{1,2},{2,3},{3,4},{4,5},{5,6},{6,7},{7,8},{8,9},{9,10},{10,1... | collective-permute-start | bytes 884744 | tf_op jit(solution)/shard_map/ppermute | solution.py:359
  12.3 4.2 %collective-permute-start = (f32[2,2,3,8,128]{4,3,2,1,0:T(8,128)S(1)}, f32[2,2,3,8,128]{4,3,2,1,0:T(8,128)S(1)}, u32[]{:S(2)}, u32[]{:S(2)}) collective-permute-start(f32[2,2,3,8,128]{4,3,2,1,0:T(8,128)S(1)} %get-tuple-element.14), channel_id=1, source_target_pairs={{0,64},{64,128},{128,192},{192,0},{1,65},{65,129},{129,193},{193,1... | collective-permute-start | bytes 147464 | tf_op jit(solution)/shard_map/ppermute | solution.py:359
  12.8 7.7 %collective-permute-start.1 = (f32[2,2,3,8,128]{4,3,2,1,0:T(8,128)S(1)}, f32[2,2,3,8,128]{4,3,2,1,0:T(8,128)S(1)}, u32[]{:S(2)}, u32[]{:S(2)}) collective-permute-start(f32[2,2,3,8,128]{4,3,2,1,0:T(8,128)S(1)} %get-tuple-element.15), channel_id=1, source_target_pairs={{0,192},{64,0},{128,64},{192,128},{1,193},{65,1},{129,65},{193,129... | collective-permute-start | bytes 147464 | tf_op jit(solution)/shard_map/ppermute | solution.py:359
  16.4 14.2 %collective-permute-start.7 = (f32[3,3,32,256]{3,2,1,0:T(8,128)S(1)}, f32[3,3,32,256]{3,2,1,0:T(8,128)S(1)}, u32[]{:S(2)}, u32[]{:S(2)}) collective-permute-start(f32[3,3,32,256]{3,2,1,0:T(8,128)S(1)} %get-tuple-element.22), channel_id=1, source_target_pairs={{0,63},{1,0},{2,1},{3,2},{4,3},{5,4},{6,5},{7,6},{8,7},{9,8},{10,9... | collective-permute-start | bytes 884744 | tf_op jit(solution)/shard_map/ppermute | solution.py:359
  20.6 13.0 %collective-permute-start.2 = (f32[3,3,32,256]{3,2,1,0:T(8,128)S(1)}, f32[3,3,32,256]{3,2,1,0:T(8,128)S(1)}, u32[]{:S(2)}, u32[]{:S(2)}) collective-permute-start(f32[3,3,32,256]{3,2,1,0:T(8,128)S(1)} %get-tuple-element.17), channel_id=1, source_target_pairs={{0,1},{1,2},{2,3},{3,4},{4,5},{5,6},{6,7},{7,8},{8,9},{9,10},{10,1... | collective-permute-start | bytes 884744 | tf_op jit(solution)/shard_map/ppermute | solution.py:359
  21.7 11.8 %collective-permute-start.3 = (f32[3,3,32,256]{3,2,1,0:T(8,128)S(1)}, f32[3,3,32,256]{3,2,1,0:T(8,128)S(1)}, u32[]{:S(2)}, u32[]{:S(2)}) collective-permute-start(f32[3,3,32,256]{3,2,1,0:T(8,128)S(1)} %get-tuple-element.18), channel_id=1, source_target_pairs={{0,63},{1,0},{2,1},{3,2},{4,3},{5,4},{6,5},{7,6},{8,7},{9,8},{10,9... | collective-permute-start | bytes 884744 | tf_op jit(solution)/shard_map/ppermute | solution.py:359
  28.0 2.6 %copy-start = (bf16[256,192]{1,0:T(8,128)(2,1)S(1)}, bf16[256,192]{1,0:T(8,128)(2,1)}, u32[]{:S(2)}) copy-start(bf16[256,192]{1,0:T(8,128)(2,1)} %constant.8.clone.refs_4_) | copy-start | bytes 294916

commit v3 on v2

--- a/solution.py
+++ b/solution.py
@@ -40,16 +40,20 @@
     return np.kron(np.eye(xb, dtype=np.float32), m)
 
 
-def halo_matrix(tile, xb):
-    m = np.zeros((xb, tile, 2, 3, xb), np.float32)
+def halo_matrices(tile, xb):
+    m = np.zeros((2, xb, tile, 3, xb), np.float32)
     for k, t in TAPS.items():
         for y in range(tile):
             for x in range(xb):
                 if y + k < 0:
-                    m[x, y, 0, y + k + 3, x] += t
+                    m[0, x, y, y + k + 3, x] += t
                 if y + k >= tile:
-                    m[x, y, 1, y + k - tile, x] += t
-    return m.reshape(xb * tile, 6 * xb)
+                    m[1, x, y, y + k - tile, x] += t
+    return m.reshape(2, xb * tile, 3 * xb)
+
+
+def parity():
+    return lax.rem(lax.axis_index("cross"), 2)
 
 
 def split_dot(mat, val, flip=False):
@@ -64,7 +68,7 @@
     )
 
 
-def pack_rows(held, low, high, row, x0, xs):
+def pack_rows(held, out, first, row, x0, xs):
     halves, comps, n, tile, lanes = held.shape
     flat = held.reshape(halves * comps * n * tile, lanes)
     for half in range(halves):
@@ -72,9 +76,8 @@
         for c in range(comps):
             for y in range(3):
                 start = ((half * comps + c) * n + row) * tile + y
-                low[c, y, pl.ds(x0, xs), cols] = flat[pl.ds(start, xs, stride=tile)]
-                high[c, y, pl.ds(x0, xs), cols] = flat[
-                    pl.ds(start + tile - 3, xs, stride=tile)
+                out[c, y, pl.ds(x0, xs), cols] = flat[
+                    pl.ds(start + first, xs, stride=tile)
                 ]
 
 
@@ -105,10 +108,12 @@
         )
 
 
-def pack_kernel(xs, vel, low, high, buf, sems):
-    for cp in fetch(vel, buf, sems, 0, xs, 0):
+def pack_kernel(xs, vel, cross, buf, sems):
+    copies = fetch(vel, buf, sems, 0, xs, 0)
+    first = parity() * (buf.shape[3] - 3)
+    for cp in copies:
         cp.wait()
-    pack_rows(buf, low, high, 0, 0, xs)
+    pack_rows(buf, cross, first, 0, 0, xs)
 
 
 def held_shape(vel, n=None):
@@ -128,9 +133,9 @@
     _, _, _, nz = vel.shape
     return pl.pallas_call(
         functools.partial(pack_kernel, xs),
-        out_shape=(halo_shape(vel, xs),) * 2,
+        out_shape=halo_shape(vel, xs),
         in_specs=[pl.BlockSpec(memory_space=pltpu.HBM)],
-        out_specs=[pl.BlockSpec(memory_space=pltpu.VMEM)] * 2,
+        out_specs=pl.BlockSpec(memory_space=pltpu.VMEM),
         scratch_shapes=[
             held_shape(vel, xs),
             pltpu.SemaphoreType.DMA((nz // LANES,)),
@@ -141,9 +146,11 @@
 
 
 def load_kernel(chunks, vel_in, *refs):
-    vel, right, left = refs[:3]
-    sends, sems = refs[3:-1], refs[-1]
-    n = vel.shape[2]
+    vel, right, left, chip = refs[:4]
+    cross, sems = refs[4:-1], refs[-1]
+    n, tile = vel.shape[2:4]
+    to_cross = parity() * (tile - 3)
+    to_chip = tile - 3 - to_cross
     copies = [
         fetch(vel_in, vel, sems.at[b], b * LB, LB, b * LB) for b in range(n // LB)
     ]
@@ -158,10 +165,9 @@
         for cp in copies[b]:
             cp.wait()
         k, x0 = where[b]
+        pack_rows(vel, chip, to_chip, b * LB, b * LB, LB)
         if k > 0:
-            pack_rows(
-                vel, sends[2 * k - 2], sends[2 * k - 1], b * LB, b * LB - x0, LB
-            )
+            pack_rows(vel, cross[k - 1], to_cross, b * LB, b * LB - x0, LB)
         for i in range(b * LB, (b + 1) * LB):
             f = vel[:, :, i]
             if i == 0:
@@ -180,9 +186,8 @@
 def load(vel, chunks):
     comps, nx, tile, nz = vel.shape
     edge = pltpu.VMEM((2, nz // LANES, comps, tile, LANES), jnp.float32)
-    outs = [held_shape(vel), edge, edge]
-    for xs in chunks[1:]:
-        outs += [halo_shape(vel, xs)] * 2
+    outs = [held_shape(vel), edge, edge, halo_shape(vel, nx)]
+    outs += [halo_shape(vel, xs) for xs in chunks[1:]]
     return pl.pallas_call(
         functools.partial(load_kernel, chunks),
         out_shape=tuple(outs),
@@ -194,8 +199,9 @@
     )(in_hbm(vel))
 
 
-def inner_kernel(vel, zmat, ymat, adv):
-    _, comps, n, _, _ = vel.shape
+def inner_kernel(vel, chip, zmat, ymat, hmat, adv):
+    halves, comps, n, _, lanes = vel.shape
+    side = 1 - parity()
 
     def block(b, _):
         rows = pl.ds(b * XB, XB)
@@ -205,21 +211,23 @@
             f = rows_of(vel, c, rows)
             gz = split_dot(zmat[...], f, flip=True)
             gy = split_dot(ymat[...], f)
+            halo = chip[c, :, rows].reshape(-1, halves * lanes)
+            gy = gy + split_dot(hmat[side], halo)
             put_rows(adv, c, rows, sv * gy + sw * gz)
         return 0
 
     lax.fori_loop(0, n // XB, block, 0)
 
 
-def inner(vel, zmat, ymat):
+def inner(vel, chip, zmat, ymat, hmat):
     return pl.pallas_call(
         inner_kernel,
         out_shape=pltpu.VMEM(vel.shape, jnp.float32),
-        in_specs=[pl.BlockSpec(memory_space=pltpu.VMEM)] * 3,
+        in_specs=[pl.BlockSpec(memory_space=pltpu.VMEM)] * 5,
         out_specs=pl.BlockSpec(memory_space=pltpu.VMEM),
         compiler_params=pltpu.CompilerParams(vmem_limit_bytes=8 << 20),
         name="inner",
-    )(vel, zmat, ymat)
+    )(vel, chip, zmat, ymat, hmat)
 
 
 def along_kernel(vel, from_left, from_right, adv_in, adv, deriv_out, deriv, sems):
@@ -298,23 +306,18 @@
 
 
 def outer_kernel(x0, *refs):
-    vel, adv_in, low, high, hmat = refs[:5]
+    vel, adv_in, cross, hmat = refs[:4]
     adv_out, adv, sems = refs[-3:]
     halves, comps, xs, _, lanes = adv.shape
+    side = parity()
     copies = []
     for b in range(xs // XB):
         here = pl.ds(b * XB, XB)
         rows = pl.ds(x0 + b * XB, XB)
         sv = rows_of(vel, 1, rows) * (1.0 / 60.0)
         for c in range(comps):
-            halo = jnp.concatenate(
-                [
-                    low[c, :, here].reshape(-1, halves * lanes),
-                    high[c, :, here].reshape(-1, halves * lanes),
-                ],
-                axis=0,
-            )
-            gy = split_dot(hmat[...], halo)
+            halo = cross[c, :, here].reshape(-1, halves * lanes)
+            gy = split_dot(hmat[side], halo)
             put_rows(adv, c, here, rows_of(adv_in, c, rows) - sv * gy)
             for half in range(halves):
                 copies.append(
@@ -329,16 +332,16 @@
         cp.wait()
 
 
-def outer(vel, adv, low, high, hmat, x0, out):
+def outer(vel, adv, cross, hmat, x0, out):
     halves, comps, nx, tile, lanes = vel.shape
-    xs = low.shape[2]
-    args = [vel, adv, low, high, hmat]
-    specs = [pl.BlockSpec(memory_space=pltpu.VMEM)] * 5
+    xs = cross.shape[2]
+    args = [vel, adv, cross, hmat]
+    specs = [pl.BlockSpec(memory_space=pltpu.VMEM)] * 4
     alias = {}
     if out is not None:
         args.append(out)
         specs.append(pl.BlockSpec(memory_space=pl.ANY))
-        alias = {5: 0}
+        alias = {4: 0}
     return pl.pallas_call(
         functools.partial(outer_kernel, x0),
         out_shape=jax.ShapeDtypeStruct((comps, nx, tile, halves * lanes), jnp.float32),
@@ -359,26 +362,32 @@
     return lax.ppermute(x, axis, [(i, (i + step) % count) for i in range(count)])
 
 
+def swap(x, axis, step):
+    count = lax.axis_size(axis)
+    pairs = []
+    for i in range(0, count, 2):
+        j = (i + step) % count
+        pairs += [(i, j), (j, i)]
+    return lax.ppermute(x, axis, pairs)
+
+
 def on_device(vel):
     _, _, tile, nz = vel.shape
     zmat = jnp.asarray(z_matrix(nz), jnp.bfloat16)
     ymat = jnp.asarray(y_matrix(tile, XB), jnp.bfloat16)
-    hmat = jnp.asarray(halo_matrix(tile, XB), jnp.bfloat16)
-    sends = list(pack(vel, CHUNKS[0]))
-    held, right, left, *rest = load(vel, CHUNKS)
-    sends += rest
-    halos = []
-    for k in range(len(CHUNKS)):
-        low_rows, high_rows = sends[2 * k : 2 * k + 2]
-        halos.append((shift(high_rows, "cross", 1), shift(low_rows, "cross", -1)))
+    hmat = jnp.asarray(halo_matrices(tile, XB), jnp.bfloat16)
+    first = pack(vel, CHUNKS[0])
+    held, right, left, chip, *rest = load(vel, CHUNKS)
+    halos = [swap(x, "cross", -1) for x in [first] + rest]
+    chip = swap(chip, "cross", 1)
     from_left = shift(right, "line", 1)
     from_right = shift(left, "line", -1)
-    adv = inner(held, zmat, ymat)
+    adv = inner(held, chip, zmat, ymat, hmat)
     adv, deriv = along(held, from_left, from_right, adv)
     out = None
     x0 = 0
-    for xs, (low, high) in zip(CHUNKS, halos):
-        out = outer(held, adv, low, high, hmat, x0, out)
+    for xs, halo in zip(CHUNKS, halos):
+        out = outer(held, adv, halo, hmat, x0, out)
         x0 += xs
     return out, deriv
 

time: 34.9 us -> 30.4 us (0.87)
  waiting for transfers between devices: 3.24 us -> 0.51 us
  starting transfers between devices: 18.1 us -> 15.7 us
  Pallas kernels: 12.6 us -> 13.3 us
    ppermute x8 -> x2, starting transfers between devices: 18.1 us -> 2.03 us  [shift(): lax.ppermute(x, axis, [(i, (i + step) % count) for i in range(count)])]
    ppermute x0 -> x4, starting transfers between devices: none -> 13.6 us  [swap(): return lax.ppermute(x, axis, pairs)]
    ppermute x8 -> x2, waiting for transfers between devices: 3.24 us -> 0.49 us  [shift(): lax.ppermute(x, axis, [(i, (i + step) % count) for i in range(count)])]
    pallas_call x1, Pallas kernels: 2.39 us -> 3.23 us  [inner(): pl.pallas_call(inner_kernel, out_shape=pltpu.VMEM(vel.shape, jnp.float32)...]
  transfers between devices with their start and end apart: 8 -> 6, of which waited for: 2 -> 1; matrix products, arithmetic and copies ran while one was open for 0% -> 0% of each run, Pallas kernels for 26% -> 32%
where the time goes in v3:
time: 30.4 us; the launch traced here: 30.3 us
  starting transfers between devices  15.7 us (52%)
  Pallas kernels  13.3 us (44%)
  between operations  0.75 us (2%)
  waiting for transfers between devices  0.51 us (2%)
    ppermute x4, starting transfers between devices, swap(): return lax.ppermute(x, axis, pairs)  13.6 us
    pallas_call x3, Pallas kernels, outer(): pl.pallas_call(functools.partial(outer_kernel, x0), out_shape=jax.ShapeDt...  4 us
    pallas_call x1, Pallas kernels, inner(): pl.pallas_call(inner_kernel, out_shape=pltpu.VMEM(vel.shape, jnp.float32)...  3.23 us
    pallas_call x1, Pallas kernels, along(): pl.pallas_call(along_kernel, out_shape=(pltpu.VMEM(vel.shape, jnp.float32...  2.59 us
    pallas_call x1, Pallas kernels, load(): pl.pallas_call(functools.partial(load_kernel, chunks), out_shape=tuple(ou...  2.32 us
    ppermute x2, starting transfers between devices, shift(): lax.ppermute(x, axis, [(i, (i + step) % count) for i in range(count)])  2.03 us
    pallas_call x1, Pallas kernels, pack(): pl.pallas_call(functools.partial(pack_kernel, xs), out_shape=halo_shape(v...  1.2 us
  transfers between devices with their start and end apart: 6, of which 1 were waited for; matrix products, arithmetic and copies ran while one was open for 0% of the time, Pallas kernels for 32%

profile of v3, /device:TPU:6, one launch (start us, length us, event | category | flops | bytes accessed | tf_op | source)
XLA Modules:
  0.0 30.3 jit_solution(10786487931300833110)
XLA Ops:
  0.6 0.0 copy-start
  0.6 0.0 copy-start.1
  0.7 0.0 copy-start.2
  0.7 2.3 %load.1 = (f32[2,3,128,8,128]{4,3,2,1,0:T(8,128)S(1)}, f32[2,2,3,8,128]{4,3,2,1,0:T(8,128)S(1)}, f32[2,2,3,8,128]{4,3,2,1,0:T(8,128)S(1)}, f32[3,3,128,256]{3,2,...) custom-call(f32[3,128,8,256]{3,2,1,0:T(8,128)} %vel.1), custom_call_target="tpu_custom_call" | custom-call | tf_op jit(solution)/shard_map/load/pallas_call | solution.py:191
  3.0 0.1 collective-permute-start.2
  3.1 8.4 %collective-permute-start.4 = (f32[3,3,64,256]{3,2,1,0:T(8,128)S(1)}, f32[3,3,64,256]{3,2,1,0:T(8,128)S(1)}, u32[]{:S(2)}, u32[]{:S(2)}) collective-permute-start(f32[3,3,64,256]{3,2,1,0:T(8,128)S(1)} %get-tuple-element.16), channel_id=1, source_target_pairs={{0,63},{63,0},{2,1},{1,2},{4,3},{3,4},{6,5},{5,6},{8,7},{7,8},{10,... | collective-permute-start | bytes 1769480 | tf_op jit(solution)/shard_map/ppermute | solution.py:371
  11.5 1.2 %pack.1 = f32[3,3,32,256]{3,2,1,0:T(8,128)S(1)} custom-call(f32[3,128,8,256]{3,2,1,0:T(8,128)} %vel.1), custom_call_target="tpu_custom_call" | custom-call | tf_op jit(solution)/shard_map/pack/pallas_call | solution.py:134
  12.7 0.1 collective-permute-start.5
  12.8 5.1 %collective-permute-start.3 = (f32[3,3,32,256]{3,2,1,0:T(8,128)S(1)}, f32[3,3,32,256]{3,2,1,0:T(8,128)S(1)}, u32[]{:S(2)}, u32[]{:S(2)}) collective-permute-start(f32[3,3,32,256]{3,2,1,0:T(8,128)S(1)} %get-tuple-element.15), channel_id=1, source_target_pairs={{0,63},{63,0},{2,1},{1,2},{4,3},{3,4},{6,5},{5,6},{8,7},{7,8},{10,... | collective-permute-start | bytes 884744 | tf_op jit(solution)/shard_map/ppermute | solution.py:371
  17.9 0.5 %collective-permute-start = (f32[2,2,3,8,128]{4,3,2,1,0:T(8,128)S(1)}, f32[2,2,3,8,128]{4,3,2,1,0:T(8,128)S(1)}, u32[]{:S(2)}, u32[]{:S(2)}) collective-permute-start(f32[2,2,3,8,128]{4,3,2,1,0:T(8,128)S(1)} %get-tuple-element.11), channel_id=1, source_target_pairs={{0,64},{64,128},{128,192},{192,0},{1,65},{65,129},{129,193},{193,1... | collective-permute-start | bytes 147464 | tf_op jit(solution)/shard_map/ppermute | solution.py:362
  18.3 0.0 collective-permute-done.2.chip
  18.3 1.5 %collective-permute-start.1 = (f32[2,2,3,8,128]{4,3,2,1,0:T(8,128)S(1)}, f32[2,2,3,8,128]{4,3,2,1,0:T(8,128)S(1)}, u32[]{:S(2)}, u32[]{:S(2)}) collective-permute-start(f32[2,2,3,8,128]{4,3,2,1,0:T(8,128)S(1)} %get-tuple-element.12), channel_id=1, source_target_pairs={{0,192},{64,0},{128,64},{192,128},{1,193},{65,1},{129,65},{193,129... | collective-permute-start | bytes 147464 | tf_op jit(solution)/shard_map/ppermute | solution.py:362
  19.9 0.0 copy-done
  19.9 0.0 copy-done.1
  19.9 0.0 copy-done.2
  19.9 3.2 %inner.1.adv_in = f32[2,3,128,8,128]{4,3,2,1,0:T(8,128)S(1)} custom-call(f32[2,3,128,8,128]{4,3,2,1,0:T(8,128)S(1)} %get-tuple-element.10.vel.refs_0_, f32[3,3,128,256]{3,2,1,0:T(8,128)S(1)} %collective-permute-done.2.chip, bf16[256,256]{1,0:T(8,128)(2,1)S(1)} %copy-done.2, bf16[256,256]{1,0:T(8,128)(2,1)S(1)} %copy-done.1, bf16[2,256,96]{2,1,0:T(8,128)(2,1)S(1)} %copy-done), custom_call_target="tpu_custom_call" | custom-call | tf_op jit(solution)/shard_map/inner/pallas_call | solution.py:223
  23.1 0.0 collective-permute-done.from_left
  23.2 0.5 %collective-permute-done.1.from_right = f32[2,2,3,8,128]{4,3,2,1,0:T(8,128)S(1)} collective-permute-done((f32[2,2,3,8,128]{4,3,2,1,0:T(8,128)S(1)}, f32[2,2,3,8,128]{4,3,2,1,0:T(8,128)S(1)}, u32[]{:S(2)}, u32[]{:S(2)}) %collective-permute-start.1) | collective-permute-done | bytes 49184 | tf_op jit(solution)/shard_map/ppermute | solution.py:362
  23.6 2.6 %along.1 = (f32[2,3,128,8,128]{4,3,2,1,0:T(8,128)S(1)}, f32[3,128,8,256]{3,2,1,0:T(8,128)}) custom-call(f32[2,3,128,8,128]{4,3,2,1,0:T(8,128)S(1)} %get-tuple-element.10.vel.refs_0_, f32[2,2,3,8,128]{4,3,2,1,0:T(8,128)S(1)} %collective-permute-done.from_left, ...), custom_call_target="tpu_custom_call", output_to_operand_aliasing={{0}: (3, {})} | custom-call | tf_op jit(solution)/shard_map/along/pallas_call | solution.py:290
  26.2 0.0 collective-permute-done.5.refs_2_
  26.3 1.2 %outer.3.refs_4_ = f32[3,128,8,256]{3,2,1,0:T(8,128)} custom-call(f32[2,3,128,8,128]{4,3,2,1,0:T(8,128)S(1)} %get-tuple-element.10.vel.refs_0_, f32[2,3,128,8,128]{4,3,2,1,0:T(8,128)S(1)} %get-tuple-element.14.refs_1_, f32[3,3,32,256]{3,2,1,0:T(8,128)S(1)} %collective-permute-done.5.refs_2_, bf16[2,256,96]{2,1,0:T(8,128)(2,1)S(1)} %copy-done), custom_call_target="tpu_custom_call" | custom-call | tf_op jit(solution)/shard_map/outer/pallas_call | solution.py:345
  27.5 0.0 collective-permute-done.4.refs_2_
  27.5 1.6 %outer.4.refs_4_ = f32[3,128,8,256]{3,2,1,0:T(8,128)} custom-call(f32[2,3,128,8,128]{4,3,2,1,0:T(8,128)S(1)} %get-tuple-element.10.vel.refs_0_, f32[2,3,128,8,128]{4,3,2,1,0:T(8,128)S(1)} %get-tuple-element.14.refs_1_, f32[3,3,64,256]{3,2,1,0:T(8,128)S(1)} %collective-permute-done.4.refs_2_, ...), custom_call_target="tpu_custom_call", output_to_operand_aliasing={{}: (4, {})} | custom-call | tf_op jit(solution)/shard_map/outer/pallas_call | solution.py:345
  29.1 0.0 collective-permute-done.3.refs_2_
  29.1 1.2 %outer.5 = f32[3,128,8,256]{3,2,1,0:T(8,128)} custom-call(f32[2,3,128,8,128]{4,3,2,1,0:T(8,128)S(1)} %get-tuple-element.10.vel.refs_0_, f32[2,3,128,8,128]{4,3,2,1,0:T(8,128)S(1)} %get-tuple-element.14.refs_1_, f32[3,3,32,256]{3,2,1,0:T(8,128)S(1)} %collective-permute-done.3.refs_2_, ...), custom_call_target="tpu_custom_call", output_to_operand_aliasing={{}: (4, {})} | custom-call | tf_op jit(solution)/shard_map/outer/pallas_call | solution.py:345
Async XLA Ops:
  0.6 19.3 %copy-start = (bf16[2,256,96]{2,1,0:T(8,128)(2,1)S(1)}, bf16[2,256,96]{2,1,0:T(8,128)(2,1)}, u32[]{:S(2)}) copy-start(bf16[2,256,96]{2,1,0:T(8,128)(2,1)} %constant.8.clone.hmat.refs_3_) | copy-start | bytes 294916
  0.6 19.3 %copy-start.1 = (bf16[256,256]{1,0:T(8,128)(2,1)S(1)}, bf16[256,256]{1,0:T(8,128)(2,1)}, u32[]{:S(2)}) copy-start(bf16[256,256]{1,0:T(8,128)(2,1)} %constant.7.clone.ymat) | copy-start | bytes 393220
  0.7 19.2 %copy-start.2 = (bf16[256,256]{1,0:T(8,128)(2,1)S(1)}, bf16[256,256]{1,0:T(8,128)(2,1)}, u32[]{:S(2)}) copy-start(bf16[256,256]{1,0:T(8,128)(2,1)} %constant.6.clone.zmat) | copy-start | bytes 393220
  3.0 15.4 %collective-permute-start.2 = (f32[3,3,128,256]{3,2,1,0:T(8,128)S(1)}, f32[3,3,128,256]{3,2,1,0:T(8,128)S(1)}, u32[]{:S(2)}, u32[]{:S(2)}) collective-permute-start(f32[3,3,128,256]{3,2,1,0:T(8,128)S(1)} %get-tuple-element.13), channel_id=1, source_target_pairs={{0,1},{1,0},{2,3},{3,2},{4,5},{5,4},{6,7},{7,6},{8,9},{9,8},{10,11... | collective-permute-start | bytes 3538952 | tf_op jit(solution)/shard_map/ppermute | solution.py:371
  3.1 24.4 %collective-permute-start.4 = (f32[3,3,64,256]{3,2,1,0:T(8,128)S(1)}, f32[3,3,64,256]{3,2,1,0:T(8,128)S(1)}, u32[]{:S(2)}, u32[]{:S(2)}) collective-permute-start(f32[3,3,64,256]{3,2,1,0:T(8,128)S(1)} %get-tuple-element.16), channel_id=1, source_target_pairs={{0,63},{63,0},{2,1},{1,2},{4,3},{3,4},{6,5},{5,6},{8,7},{7,8},{10,... | collective-permute-start | bytes 1769480 | tf_op jit(solution)/shard_map/ppermute | solution.py:371
  12.7 13.5 %collective-permute-start.5 = (f32[3,3,32,256]{3,2,1,0:T(8,128)S(1)}, f32[3,3,32,256]{3,2,1,0:T(8,128)S(1)}, u32[]{:S(2)}, u32[]{:S(2)}) collective-permute-start(f32[3,3,32,256]{3,2,1,0:T(8,128)S(1)} %pack.1), channel_id=1, source_target_pairs={{0,63},{63,0},{2,1},{1,2},{4,3},{3,4},{6,5},{5,6},{8,7},{7,8},{10,... | collective-permute-start | bytes 884744 | tf_op jit(solution)/shard_map/ppermute | solution.py:371
  12.8 16.3 %collective-permute-start.3 = (f32[3,3,32,256]{3,2,1,0:T(8,128)S(1)}, f32[3,3,32,256]{3,2,1,0:T(8,128)S(1)}, u32[]{:S(2)}, u32[]{:S(2)}) collective-permute-start(f32[3,3,32,256]{3,2,1,0:T(8,128)S(1)} %get-tuple-element.15), channel_id=1, source_target_pairs={{0,63},{63,0},{2,1},{1,2},{4,3},{3,4},{6,5},{5,6},{8,7},{7,8},{10,... | collective-permute-start | bytes 884744 | tf_op jit(solution)/shard_map/ppermute | solution.py:371
  17.9 5.3 %collective-permute-start = (f32[2,2,3,8,128]{4,3,2,1,0:T(8,128)S(1)}, f32[2,2,3,8,128]{4,3,2,1,0:T(8,128)S(1)}, u32[]{:S(2)}, u32[]{:S(2)}) collective-permute-start(f32[2,2,3,8,128]{4,3,2,1,0:T(8,128)S(1)} %get-tuple-element.11), channel_id=1, source_target_pairs={{0,64},{64,128},{128,192},{192,0},{1,65},{65,129},{129,193},{193,1... | collective-permute-start | bytes 147464 | tf_op jit(solution)/shard_map/ppermute | solution.py:362
  18.3 5.3 %collective-permute-start.1 = (f32[2,2,3,8,128]{4,3,2,1,0:T(8,128)S(1)}, f32[2,2,3,8,128]{4,3,2,1,0:T(8,128)S(1)}, u32[]{:S(2)}, u32[]{:S(2)}) collective-permute-start(f32[2,2,3,8,128]{4,3,2,1,0:T(8,128)S(1)} %get-tuple-element.12), channel_id=1, source_target_pairs={{0,192},{64,0},{128,64},{192,128},{1,193},{65,1},{129,65},{193,129... | collective-permute-start | bytes 147464 | tf_op jit(solution)/shard_map/ppermute | solution.py:362

commit v4 on v3

--- a/solution.py
+++ b/solution.py
@@ -16,7 +16,7 @@
 R = float(ROOT)
 GAIN = float(1.0 / (1.0 - ROOT * ROOT))
 TAPS = {1: 45.0, 2: -9.0, 3: 1.0, -1: -45.0, -2: 9.0, -3: -1.0}
-CHUNKS = (32, 64, 32)
+CHUNKS = (96, 32)
 XB = 32
 LB = 16
 EB = 8
@@ -108,14 +108,6 @@
         )
 
 
-def pack_kernel(xs, vel, cross, buf, sems):
-    copies = fetch(vel, buf, sems, 0, xs, 0)
-    first = parity() * (buf.shape[3] - 3)
-    for cp in copies:
-        cp.wait()
-    pack_rows(buf, cross, first, 0, 0, xs)
-
-
 def held_shape(vel, n=None):
     comps, nx, tile, nz = vel.shape
     return pltpu.VMEM((nz // LANES, comps, n or nx, tile, LANES), jnp.float32)
@@ -127,22 +119,6 @@
 
 def in_hbm(x):
     return pltpu.with_memory_space_constraint(x, pltpu.HBM)
-
-
-def pack(vel, xs):
-    _, _, _, nz = vel.shape
-    return pl.pallas_call(
-        functools.partial(pack_kernel, xs),
-        out_shape=halo_shape(vel, xs),
-        in_specs=[pl.BlockSpec(memory_space=pltpu.HBM)],
-        out_specs=pl.BlockSpec(memory_space=pltpu.VMEM),
-        scratch_shapes=[
-            held_shape(vel, xs),
-            pltpu.SemaphoreType.DMA((nz // LANES,)),
-        ],
-        compiler_params=pltpu.CompilerParams(vmem_limit_bytes=8 << 20),
-        name="pack",
-    )(in_hbm(vel))
 
 
 def load_kernel(chunks, vel_in, *refs):
@@ -166,8 +142,7 @@
             cp.wait()
         k, x0 = where[b]
         pack_rows(vel, chip, to_chip, b * LB, b * LB, LB)
-        if k > 0:
-            pack_rows(vel, cross[k - 1], to_cross, b * LB, b * LB - x0, LB)
+        pack_rows(vel, cross[k], to_cross, b * LB, b * LB - x0, LB)
         for i in range(b * LB, (b + 1) * LB):
             f = vel[:, :, i]
             if i == 0:
@@ -187,7 +162,7 @@
     comps, nx, tile, nz = vel.shape
     edge = pltpu.VMEM((2, nz // LANES, comps, tile, LANES), jnp.float32)
     outs = [held_shape(vel), edge, edge, halo_shape(vel, nx)]
-    outs += [halo_shape(vel, xs) for xs in chunks[1:]]
+    outs += [halo_shape(vel, xs) for xs in chunks]
     return pl.pallas_call(
         functools.partial(load_kernel, chunks),
         out_shape=tuple(outs),
@@ -376,9 +351,8 @@
     zmat = jnp.asarray(z_matrix(nz), jnp.bfloat16)
     ymat = jnp.asarray(y_matrix(tile, XB), jnp.bfloat16)
     hmat = jnp.asarray(halo_matrices(tile, XB), jnp.bfloat16)
-    first = pack(vel, CHUNKS[0])
-    held, right, left, chip, *rest = load(vel, CHUNKS)
-    halos = [swap(x, "cross", -1) for x in [first] + rest]
+    held, right, left, chip, *cross = load(vel, CHUNKS)
+    halos = [swap(x, "cross", -1) for x in cross]
     chip = swap(chip, "cross", 1)
     from_left = shift(right, "line", 1)
     from_right = shift(left, "line", -1)

time: 30.4 us -> 26.7 us (0.88)
  starting transfers between devices: 15.7 us -> 10.6 us
  waiting for transfers between devices: 0.51 us -> 4.07 us
  Pallas kernels: 13.3 us -> 11.2 us
    ppermute x4 -> x3, starting transfers between devices: 13.6 us -> 8.54 us  [swap(): return lax.ppermute(x, axis, pairs)]
    ppermute x4 -> x3, waiting for transfers between devices: 0.01 us -> 3.6 us  [swap(): return lax.ppermute(x, axis, pairs)]
    pallas_call x1 -> x0, Pallas kernels: 1.2 us -> none  [pack(): pl.pallas_call(functools.partial(pack_kernel, xs), out_shape=halo_shape(v...]
    pallas_call x3 -> x2, Pallas kernels: 4 us -> 3.08 us  [outer(): pl.pallas_call(functools.partial(outer_kernel, x0), out_shape=jax.ShapeDt...]
  transfers between devices with their start and end apart: 6 -> 5, of which waited for: 1 -> 3; matrix products, arithmetic and copies ran while one was open for 0% -> 0% of each run, Pallas kernels for 32% -> 29%
where the time goes in v4:
time: 26.7 us; the launch traced here: 26.6 us
  Pallas kernels  11.2 us (42%)
  starting transfers between devices  10.6 us (40%)
  waiting for transfers between devices  4.07 us (15%)
  between operations  0.72 us (3%)
    ppermute x3, starting transfers between devices, swap(): return lax.ppermute(x, axis, pairs)  8.54 us
    ppermute x3, waiting for transfers between devices, swap(): return lax.ppermute(x, axis, pairs)  3.6 us
    pallas_call x1, Pallas kernels, inner(): pl.pallas_call(inner_kernel, out_shape=pltpu.VMEM(vel.shape, jnp.float32)...  3.24 us
    pallas_call x2, Pallas kernels, outer(): pl.pallas_call(functools.partial(outer_kernel, x0), out_shape=jax.ShapeDt...  3.08 us
    pallas_call x1, Pallas kernels, along(): pl.pallas_call(along_kernel, out_shape=(pltpu.VMEM(vel.shape, jnp.float32...  2.59 us
    pallas_call x1, Pallas kernels, load(): pl.pallas_call(functools.partial(load_kernel, chunks), out_shape=tuple(ou...  2.32 us
    ppermute x2, starting transfers between devices, shift(): lax.ppermute(x, axis, [(i, (i + step) % count) for i in range(count)])  2.03 us
  transfers between devices with their start and end apart: 5, of which 3 were waited for; matrix products, arithmetic and copies ran while one was open for 0% of the time, Pallas kernels for 29%

profile of v4, /device:TPU:6, one launch (start us, length us, event | category | flops | bytes accessed | tf_op | source)
XLA Modules:
  0.0 26.6 jit_solution(1522933652953025710)
XLA Ops:
  0.6 0.0 copy-start
  0.6 0.0 copy-start.1
  0.7 0.0 copy-start.2
  0.7 2.3 %load.1 = (f32[2,3,128,8,128]{4,3,2,1,0:T(8,128)S(1)}, f32[2,2,3,8,128]{4,3,2,1,0:T(8,128)S(1)}, f32[2,2,3,8,128]{4,3,2,1,0:T(8,128)S(1)}, f32[3,3,128,256]{3,2,...) custom-call(f32[3,128,8,256]{3,2,1,0:T(8,128)} %vel_in.1), custom_call_target="tpu_custom_call" | custom-call | tf_op jit(solution)/shard_map/load/pallas_call | solution.py:166
  3.0 0.1 collective-permute-start.2
  3.1 8.4 %collective-permute-start.4 = (f32[3,3,96,256]{3,2,1,0:T(8,128)S(1)}, f32[3,3,96,256]{3,2,1,0:T(8,128)S(1)}, u32[]{:S(2)}, u32[]{:S(2)}) collective-permute-start(f32[3,3,96,256]{3,2,1,0:T(8,128)S(1)} %get-tuple-element.16), channel_id=1, source_target_pairs={{0,63},{63,0},{2,1},{1,2},{4,3},{3,4},{6,5},{5,6},{8,7},{7,8},{10,... | collective-permute-start | bytes 2654216 | tf_op jit(solution)/shard_map/ppermute | solution.py:346
  11.5 0.0 collective-permute-start.3
  11.5 0.5 %collective-permute-start = (f32[2,2,3,8,128]{4,3,2,1,0:T(8,128)S(1)}, f32[2,2,3,8,128]{4,3,2,1,0:T(8,128)S(1)}, u32[]{:S(2)}, u32[]{:S(2)}) collective-permute-start(f32[2,2,3,8,128]{4,3,2,1,0:T(8,128)S(1)} %get-tuple-element.11), channel_id=1, source_target_pairs={{0,64},{64,128},{128,192},{192,0},{1,65},{65,129},{129,193},{193,1... | collective-permute-start | bytes 147464 | tf_op jit(solution)/shard_map/ppermute | solution.py:337
  12.0 1.5 %collective-permute-start.1 = (f32[2,2,3,8,128]{4,3,2,1,0:T(8,128)S(1)}, f32[2,2,3,8,128]{4,3,2,1,0:T(8,128)S(1)}, u32[]{:S(2)}, u32[]{:S(2)}) collective-permute-start(f32[2,2,3,8,128]{4,3,2,1,0:T(8,128)S(1)} %get-tuple-element.12), channel_id=1, source_target_pairs={{0,192},{64,0},{128,64},{192,128},{1,193},{65,1},{129,65},{193,129... | collective-permute-start | bytes 147464 | tf_op jit(solution)/shard_map/ppermute | solution.py:337
  13.6 0.0 collective-permute-done.2.chip
  13.6 0.0 copy-done
  13.6 0.0 copy-done.1
  13.6 0.0 copy-done.2
  13.6 3.2 %inner.1.adv_in = f32[2,3,128,8,128]{4,3,2,1,0:T(8,128)S(1)} custom-call(f32[2,3,128,8,128]{4,3,2,1,0:T(8,128)S(1)} %get-tuple-element.10.vel.refs_0_, f32[3,3,128,256]{3,2,1,0:T(8,128)S(1)} %collective-permute-done.2.chip, bf16[256,256]{1,0:T(8,128)(2,1)S(1)} %copy-done.2, bf16[256,256]{1,0:T(8,128)(2,1)S(1)} %copy-done.1, bf16[2,256,96]{2,1,0:T(8,128)(2,1)S(1)} %copy-done), custom_call_target="tpu_custom_call" | custom-call | tf_op jit(solution)/shard_map/inner/pallas_call | solution.py:198
  16.8 0.0 collective-permute-done.from_left
  16.8 0.5 %collective-permute-done.1.from_right = f32[2,2,3,8,128]{4,3,2,1,0:T(8,128)S(1)} collective-permute-done((f32[2,2,3,8,128]{4,3,2,1,0:T(8,128)S(1)}, f32[2,2,3,8,128]{4,3,2,1,0:T(8,128)S(1)}, u32[]{:S(2)}, u32[]{:S(2)}) %collective-permute-start.1) | collective-permute-done | bytes 49184 | tf_op jit(solution)/shard_map/ppermute | solution.py:337
  17.3 2.6 %along.1 = (f32[2,3,128,8,128]{4,3,2,1,0:T(8,128)S(1)}, f32[3,128,8,256]{3,2,1,0:T(8,128)}) custom-call(f32[2,3,128,8,128]{4,3,2,1,0:T(8,128)S(1)} %get-tuple-element.10.vel.refs_0_, f32[2,2,3,8,128]{4,3,2,1,0:T(8,128)S(1)} %collective-permute-done.from_left, ...), custom_call_target="tpu_custom_call", output_to_operand_aliasing={{0}: (3, {})} | custom-call | tf_op jit(solution)/shard_map/along/pallas_call | solution.py:265
  19.9 2.3 %collective-permute-done.4.refs_2_ = f32[3,3,96,256]{3,2,1,0:T(8,128)S(1)} collective-permute-done((f32[3,3,96,256]{3,2,1,0:T(8,128)S(1)}, f32[3,3,96,256]{3,2,1,0:T(8,128)S(1)}, u32[]{:S(2)}, u32[]{:S(2)}) %collective-permute-start.4) | collective-permute-done | bytes 884768 | tf_op jit(solution)/shard_map/ppermute | solution.py:346
  22.2 1.9 %outer.2.refs_4_ = f32[3,128,8,256]{3,2,1,0:T(8,128)} custom-call(f32[2,3,128,8,128]{4,3,2,1,0:T(8,128)S(1)} %get-tuple-element.10.vel.refs_0_, f32[2,3,128,8,128]{4,3,2,1,0:T(8,128)S(1)} %get-tuple-element.14.refs_1_, f32[3,3,96,256]{3,2,1,0:T(8,128)S(1)} %collective-permute-done.4.refs_2_, bf16[2,256,96]{2,1,0:T(8,128)(2,1)S(1)} %copy-done), custom_call_target="tpu_custom_call" | custom-call | tf_op jit(solution)/shard_map/outer/pallas_call | solution.py:320
  24.1 1.3 %collective-permute-done.3.refs_2_ = f32[3,3,32,256]{3,2,1,0:T(8,128)S(1)} collective-permute-done((f32[3,3,32,256]{3,2,1,0:T(8,128)S(1)}, f32[3,3,32,256]{3,2,1,0:T(8,128)S(1)}, u32[]{:S(2)}, u32[]{:S(2)}) %collective-permute-start.3) | collective-permute-done | bytes 294944 | tf_op jit(solution)/shard_map/ppermute | solution.py:346
  25.4 1.2 %outer.3 = f32[3,128,8,256]{3,2,1,0:T(8,128)} custom-call(f32[2,3,128,8,128]{4,3,2,1,0:T(8,128)S(1)} %get-tuple-element.10.vel.refs_0_, f32[2,3,128,8,128]{4,3,2,1,0:T(8,128)S(1)} %get-tuple-element.14.refs_1_, f32[3,3,32,256]{3,2,1,0:T(8,128)S(1)} %collective-permute-done.3.refs_2_, ...), custom_call_target="tpu_custom_call", output_to_operand_aliasing={{}: (4, {})} | custom-call | tf_op jit(solution)/shard_map/outer/pallas_call | solution.py:320
Async XLA Ops:
  0.6 12.9 %copy-start = (bf16[2,256,96]{2,1,0:T(8,128)(2,1)S(1)}, bf16[2,256,96]{2,1,0:T(8,128)(2,1)}, u32[]{:S(2)}) copy-start(bf16[2,256,96]{2,1,0:T(8,128)(2,1)} %constant.8.clone.hmat.refs_3_) | copy-start | bytes 294916
  0.6 12.9 %copy-start.1 = (bf16[256,256]{1,0:T(8,128)(2,1)S(1)}, bf16[256,256]{1,0:T(8,128)(2,1)}, u32[]{:S(2)}) copy-start(bf16[256,256]{1,0:T(8,128)(2,1)} %constant.7.clone.ymat) | copy-start | bytes 393220
  0.7 12.9 %copy-start.2 = (bf16[256,256]{1,0:T(8,128)(2,1)S(1)}, bf16[256,256]{1,0:T(8,128)(2,1)}, u32[]{:S(2)}) copy-start(bf16[256,256]{1,0:T(8,128)(2,1)} %constant.6.clone.zmat) | copy-start | bytes 393220
  3.0 10.6 %collective-permute-start.2 = (f32[3,3,128,256]{3,2,1,0:T(8,128)S(1)}, f32[3,3,128,256]{3,2,1,0:T(8,128)S(1)}, u32[]{:S(2)}, u32[]{:S(2)}) collective-permute-start(f32[3,3,128,256]{3,2,1,0:T(8,128)S(1)} %get-tuple-element.13), channel_id=1, source_target_pairs={{0,1},{1,0},{2,3},{3,2},{4,5},{5,4},{6,7},{7,6},{8,9},{9,8},{10,11... | collective-permute-start | bytes 3538952 | tf_op jit(solution)/shard_map/ppermute | solution.py:346
  3.1 19.1 %collective-permute-start.4 = (f32[3,3,96,256]{3,2,1,0:T(8,128)S(1)}, f32[3,3,96,256]{3,2,1,0:T(8,128)S(1)}, u32[]{:S(2)}, u32[]{:S(2)}) collective-permute-start(f32[3,3,96,256]{3,2,1,0:T(8,128)S(1)} %get-tuple-element.16), channel_id=1, source_target_pairs={{0,63},{63,0},{2,1},{1,2},{4,3},{3,4},{6,5},{5,6},{8,7},{7,8},{10,... | collective-permute-start | bytes 2654216 | tf_op jit(solution)/shard_map/ppermute | solution.py:346
  11.5 13.9 %collective-permute-start.3 = (f32[3,3,32,256]{3,2,1,0:T(8,128)S(1)}, f32[3,3,32,256]{3,2,1,0:T(8,128)S(1)}, u32[]{:S(2)}, u32[]{:S(2)}) collective-permute-start(f32[3,3,32,256]{3,2,1,0:T(8,128)S(1)} %get-tuple-element.15), channel_id=1, source_target_pairs={{0,63},{63,0},{2,1},{1,2},{4,3},{3,4},{6,5},{5,6},{8,7},{7,8},{10,... | collective-permute-start | bytes 884744 | tf_op jit(solution)/shard_map/ppermute | solution.py:346
  11.5 5.3 %collective-permute-start = (f32[2,2,3,8,128]{4,3,2,1,0:T(8,128)S(1)}, f32[2,2,3,8,128]{4,3,2,1,0:T(8,128)S(1)}, u32[]{:S(2)}, u32[]{:S(2)}) collective-permute-start(f32[2,2,3,8,128]{4,3,2,1,0:T(8,128)S(1)} %get-tuple-element.11), channel_id=1, source_target_pairs={{0,64},{64,128},{128,192},{192,0},{1,65},{65,129},{129,193},{193,1... | collective-permute-start | bytes 147464 | tf_op jit(solution)/shard_map/ppermute | solution.py:337
  12.0 5.3 %collective-permute-start.1 = (f32[2,2,3,8,128]{4,3,2,1,0:T(8,128)S(1)}, f32[2,2,3,8,128]{4,3,2,1,0:T(8,128)S(1)}, u32[]{:S(2)}, u32[]{:S(2)}) collective-permute-start(f32[2,2,3,8,128]{4,3,2,1,0:T(8,128)S(1)} %get-tuple-element.12), channel_id=1, source_target_pairs={{0,192},{64,0},{128,64},{192,128},{1,193},{65,1},{129,65},{193,129... | collective-permute-start | bytes 147464 | tf_op jit(solution)/shard_map/ppermute | solution.py:337

commit v5 on v4

v5 whole, which is shorter than its diff:
```python
import functools

import jax
import jax.numpy as jnp
import numpy as np
from jax import lax
from jax.experimental import pallas as pl
from jax.experimental.pallas import tpu as pltpu
from jax.sharding import PartitionSpec as P

ALPHA = 1.0 / 3.0
ROOT = (-1.0 + np.sqrt(1.0 - 4.0 * ALPHA * ALPHA)) / (2.0 * ALPHA)
KAPPA = -ALPHA / ROOT
NEAR = float(7.0 / 9.0 / KAPPA)
FAR = float(1.0 / 36.0 / KAPPA)
R = float(ROOT)
GAIN = float(1.0 / (1.0 - ROOT * ROOT))
TAPS = {1: 45.0, 2: -9.0, 3: 1.0, -1: -45.0, -2: 9.0, -3: -1.0}
UP = (16, 80, 32)
DOWN = (96, 32)
UP_STAGES = ((0, (0, 1)), (96, (2,)))
DOWN_STAGES = ((0, (0,)), (96, (1,)))
XB = 32
EB = 8
LANES = 128


def z_matrix(n):
    m = np.zeros((n, n), np.float32)
    for k, t in TAPS.items():
        for z in range(n):
            m[(z + k) % n, z] += t
    return m


def y_matrix(tile, xb):
    m = np.zeros((tile, tile), np.float32)
    for k, t in TAPS.items():
        for y in range(tile):
            if 0 <= y + k < tile:
                m[y, y + k] += t
    return np.kron(np.eye(xb, dtype=np.float32), m)


def halo_matrices(tile, xb):
    m = np.zeros((2, xb, tile, 3, xb), np.float32)
    for k, t in TAPS.items():
        for y in range(tile):
            for x in range(xb):
                if y + k < 0:
                    m[0, x, y, y + k + 3, x] += t
                if y + k >= tile:
                    m[1, x, y, y + k - tile, x] += t
    return m.reshape(2, xb * tile, 3 * xb)


def parity():
    return lax.rem(lax.axis_index("cross"), 2)


def split_dot(mat, val, flip=False):
    hi = val.astype(jnp.bfloat16)
    lo = (val - hi.astype(jnp.float32)).astype(jnp.bfloat16)
    if flip:
        return jnp.dot(hi, mat, preferred_element_type=jnp.float32) + jnp.dot(
            lo, mat, preferred_element_type=jnp.float32
        )
    return jnp.dot(mat, hi, preferred_element_type=jnp.float32) + jnp.dot(
        mat, lo, preferred_element_type=jnp.float32
    )


def pack_rows(held, out, first, row):
    comps, n, halves, tile, lanes = held.shape
    xs = out.shape[2]
    flat = held.reshape(comps * n * halves * tile, lanes)
    for c in range(comps):
        for half in range(halves):
            for y in range(3):
                start = ((c * n + row) * halves + half) * tile + first + y
                out[c, y, :, half * lanes : (half + 1) * lanes] = flat[
                    pl.ds(start, xs, stride=halves * tile)
                ]


def rows_of(held, c, rows):
    halves = held.shape[2]
    both = [held[c, rows, half].reshape(-1, LANES) for half in range(halves)]
    return jnp.concatenate(both, axis=1)


def put_rows(held, c, rows, val):
    halves, tile = held.shape[2:4]
    for half in range(halves):
        part = val[:, half * LANES : (half + 1) * LANES]
        held[c, rows, half] = part.reshape(-1, tile, LANES)


def halo_shape(vel, xs):
    comps, _, halves, _, lanes = vel.shape
    return pltpu.VMEM((comps, 3, xs, halves * lanes), jnp.float32)


def in_vmem(count):
    return [pl.BlockSpec(memory_space=pltpu.VMEM)] * count


def first_kernel(vel, up, buf, sem):
    xs = up.shape[2]
    cp = pltpu.make_async_copy(vel.at[:, pl.ds(0, xs)], buf, sem)
    cp.start()
    cp.wait()

    @pl.when(parity() == 1)
    def _():
        pack_rows(buf, up, buf.shape[3] - 3, 0)


def first(vel, xs):
    comps, _, halves, tile, lanes = vel.shape
    return pl.pallas_call(
        first_kernel,
        out_shape=halo_shape(vel, xs),
        in_specs=[pl.BlockSpec(memory_space=pltpu.HBM)],
        out_specs=pl.BlockSpec(memory_space=pltpu.VMEM),
        scratch_shapes=[
            pltpu.VMEM((comps, xs, halves, tile, lanes), jnp.float32),
            pltpu.SemaphoreType.DMA,
        ],
        compiler_params=pltpu.CompilerParams(vmem_limit_bytes=4 << 20),
        name="first",
    )(pltpu.with_memory_space_constraint(vel, pltpu.HBM))


def rest_kernel(vel, *outs):
    tile = vel.shape[3]
    side = parity()

    @pl.when(side == 1)
    def _():
        x0 = UP[0]
        for k, xs in enumerate(UP[1:]):
            pack_rows(vel, outs[k], tile - 3, x0)
            x0 += xs

    @pl.when(side == 0)
    def _():
        x0 = 0
        for k, xs in enumerate(DOWN):
            pack_rows(vel, outs[len(UP) - 1 + k], 0, x0)
            x0 += xs


def rest(vel):
    outs = [halo_shape(vel, xs) for xs in UP[1:] + DOWN]
    return pl.pallas_call(
        rest_kernel,
        out_shape=tuple(outs),
        in_specs=in_vmem(1),
        out_specs=in_vmem(len(outs)),
        compiler_params=pltpu.CompilerParams(vmem_limit_bytes=4 << 20),
        name="rest",
    )(vel)


def ends_kernel(vel, right, left, chip):
    n, tile = vel.shape[1], vel.shape[3]
    pack_rows(vel, chip, (1 - parity()) * (tile - 3), 0)

    def step(i, carry):
        _, p, _, t = carry
        return (p, vel[:, i] + R * p, t, vel[:, n - 1 - i] + R * t)

    def steps(b, carry):
        for j in range(8):
            carry = step(b * 8 + j, carry)
        return carry

    carry = (vel[:, 0], vel[:, 0], vel[:, n - 1], vel[:, n - 1])
    for i in range(1, 8):
        carry = step(i, carry)
    p_old, p, t_old, t = lax.fori_loop(1, n // 8, steps, carry)
    right[0] = p_old
    right[1] = p
    left[0] = GAIN * t
    left[1] = GAIN * (t_old + R * vel[:, 0])


def ends(vel):
    comps, nx, halves, tile, lanes = vel.shape
    out = pltpu.VMEM((2, comps, halves, tile, lanes), jnp.float32)
    return pl.pallas_call(
        ends_kernel,
        out_shape=(out, out, halo_shape(vel, nx)),
        in_specs=in_vmem(1),
        out_specs=in_vmem(3),
        compiler_params=pltpu.CompilerParams(vmem_limit_bytes=4 << 20),
        name="ends",
    )(vel)


def inner_kernel(vel, chip, zmat, ymat, hmat, adv):
    side = 1 - parity()
    comps, n, halves, _, lanes = vel.shape

    def block(b, _):
        rows = pl.ds(b * XB, XB)
        sv = rows_of(vel, 1, rows) * (-1.0 / 60.0)
        sw = rows_of(vel, 2, rows) * (-1.0 / 60.0)
        for c in range(comps):
            f = rows_of(vel, c, rows)
            gz = split_dot(zmat[...], f, flip=True)
            gy = split_dot(ymat[...], f)
            halo = chip[c, :, rows].reshape(-1, halves * lanes)
            gy = gy + split_dot(hmat[side], halo)
            put_rows(adv, c, rows, sv * gy + sw * gz)
        return 0

    lax.fori_loop(0, n // XB, block, 0)


def inner(vel, chip, zmat, ymat, hmat):
    return pl.pallas_call(
        inner_kernel,
        out_shape=pltpu.VMEM(vel.shape, jnp.float32),
        in_specs=in_vmem(5),
        out_specs=pl.BlockSpec(memory_space=pltpu.VMEM),
        compiler_params=pltpu.CompilerParams(vmem_limit_bytes=8 << 20),
        name="inner",
    )(vel, chip, zmat, ymat, hmat)


def along_kernel(vel, from_left, from_right, adv_in, adv, deriv_out, deriv, sems):
    n = vel.shape[1]

    def forward(b, p):
        for j in range(EB):
            i = b * EB + j
            p = vel[:, i] + R * p
            deriv[:, i] = p
        return p

    p_left = from_left[1]
    p_end = lax.fori_loop(0, n // EB, forward, p_left)
    h_n = from_right[0] + (GAIN * R) * p_end
    h_n1 = from_right[1] + (GAIN * R * R) * p_end
    h_a = deriv[:, n - 1] + R * h_n
    h_b = deriv[:, n - 2] + R * h_a

    def copy_out(b):
        rows = pl.ds(b * EB, EB)
        return pltpu.make_async_copy(deriv.at[:, rows], deriv_out.at[:, rows], sems.at[b])

    def backward(b, carry, last=False):
        h4, h3, h2, h1 = carry
        for j in range(EB):
            i = b * EB + EB - 1 - j
            if last and i < 2:
                p = p_left if i == 1 else from_left[0]
            else:
                p = deriv[:, i - 2]
            h = p + R * h1
            g = NEAR * (h3 - h1) + FAR * (h4 - h)
            deriv[:, i] = g
            adv[:, i] = adv_in[:, i] - vel[0, i][None] * g
            h4, h3, h2, h1 = h3, h2, h1, h
        copy_out(b).start()
        return (h4, h3, h2, h1)

    blocks = n // EB
    carry = lax.fori_loop(
        0, blocks - 1, lambda k, c: backward(blocks - 1 - k, c), (h_n1, h_n, h_a, h_b)
    )
    backward(0, carry, last=True)
    for b in range(blocks):
        copy_out(b).wait()


def along(vel, from_left, from_right, adv):
    return pl.pallas_call(
        along_kernel,
        out_shape=(
            pltpu.VMEM(vel.shape, jnp.float32),
            jax.ShapeDtypeStruct(vel.shape, jnp.float32),
        ),
        in_specs=in_vmem(4),
        out_specs=[
            pl.BlockSpec(memory_space=pltpu.VMEM),
            pl.BlockSpec(memory_space=pl.ANY),
        ],
        scratch_shapes=[
            pltpu.VMEM(vel.shape, jnp.float32),
            pltpu.SemaphoreType.DMA((vel.shape[1] // EB,)),
        ],
        input_output_aliases={3: 0},
        compiler_params=pltpu.CompilerParams(vmem_limit_bytes=8 << 20),
        name="along",
    )(vel, from_left, from_right, adv)


def outer_kernel(x0, side, sizes, *refs):
    vel, adv_in, hmat = refs[:3]
    pieces = refs[3 : 3 + len(sizes)]
    adv_out, adv, sems = refs[-3:]
    comps, xs, halves, _, lanes = adv.shape

    def take(c, at):
        parts = []
        need = XB
        for size, ref in zip(sizes, pieces):
            count = min(size - at, need)
            if count > 0:
                parts.append(ref[c, :, at : at + count])
                need -= count
                at = 0
            else:
                at -= size
        both = parts[0] if len(parts) == 1 else jnp.concatenate(parts, axis=1)
        return both.reshape(-1, halves * lanes)

    @pl.when(parity() == side)
    def _():
        copies = []
        for b in range(xs // XB):
            here = pl.ds(b * XB, XB)
            rows = pl.ds(x0 + b * XB, XB)
            sv = rows_of(vel, 1, rows) * (1.0 / 60.0)
            for c in range(comps):
                gy = split_dot(hmat[side], take(c, b * XB))
                put_rows(adv, c, here, rows_of(adv_in, c, rows) - sv * gy)
            copies.append(
                pltpu.make_async_copy(adv.at[:, here], adv_out.at[:, rows], sems.at[b])
            )
            copies[-1].start()
        for cp in copies:
            cp.wait()


def outer(vel, adv, hmat, pieces, x0, side, out):
    comps, _, halves, tile, lanes = vel.shape
    sizes = tuple(x.shape[2] for x in pieces)
    xs = sum(sizes)
    args = [vel, adv, hmat, *pieces]
    specs = in_vmem(len(args))
    alias = {}
    if out is not None:
        alias = {len(args): 0}
        args.append(out)
        specs.append(pl.BlockSpec(memory_space=pl.ANY))
    return pl.pallas_call(
        functools.partial(outer_kernel, x0, side, sizes),
        out_shape=jax.ShapeDtypeStruct(vel.shape, jnp.float32),
        in_specs=specs,
        out_specs=pl.BlockSpec(memory_space=pl.ANY),
        scratch_shapes=[
            pltpu.VMEM((comps, xs, halves, tile, lanes), jnp.float32),
            pltpu.SemaphoreType.DMA((xs // XB,)),
        ],
        input_output_aliases=alias,
        compiler_params=pltpu.CompilerParams(vmem_limit_bytes=8 << 20),
        name="outer",
    )(*args)


def send(x, axis, starts, step):
    count = lax.axis_size(axis)
    return lax.ppermute(x, axis, [(i, (i + s) % count) for i, s in zip(starts, step)])


def shift(x, axis, step):
    count = lax.axis_size(axis)
    return send(x, axis, range(count), [step] * count)


def swap(x, axis):
    count = lax.axis_size(axis)
    return send(x, axis, range(count), [1, -1] * (count // 2))


def on_device(velocity):
    comps, nx, tile, nz = velocity.shape
    halves = nz // LANES
    zmat = jnp.asarray(z_matrix(nz), jnp.bfloat16)
    ymat = jnp.asarray(y_matrix(tile, XB), jnp.bfloat16)
    hmat = jnp.asarray(halo_matrices(tile, XB), jnp.bfloat16)
    vel = velocity.reshape(comps, nx, tile, halves, LANES).transpose(0, 1, 3, 2, 4)
    up = [first(vel, UP[0])]
    sends = rest(vel)
    up += sends[: len(UP) - 1]
    down = sends[len(UP) - 1 :]
    lows = [shift(x, "cross", 1) for x in up]
    highs = [shift(x, "cross", -1) for x in down]
    right, left, chip = ends(vel)
    chip = swap(chip, "cross")
    from_left = shift(right, "line", 1)
    from_right = shift(left, "line", -1)
    adv = inner(vel, chip, zmat, ymat, hmat)
    adv, deriv = along(vel, from_left, from_right, adv)
    out = None
    for side, parts, stages in ((0, lows, UP_STAGES), (1, highs, DOWN_STAGES)):
        for x0, which in stages:
            out = outer(vel, adv, hmat, [parts[k] for k in which], x0, side, out)
    return tuple(
        v.transpose(0, 1, 3, 2, 4).reshape(velocity.shape) for v in (out, deriv)
    )


def solution(mesh):
    spec = P(None, "line", "cross", None)
    return jax.shard_map(
        on_device,
        mesh=mesh,
        in_specs=(spec,),
        out_specs=(spec, spec),
        check_vma=False,
    )
```

time: 26.7 us -> 34.7 us (1.30)
  starting transfers between devices: 10.6 us -> 14.3 us
  waiting for transfers between devices: 4.07 us -> 6.67 us
  local copies, waits for them, and re-layouts: 0.02 us -> 1.91 us
    ppermute x5 -> x8, starting transfers between devices: 10.6 us -> 14.3 us  [send(): lax.ppermute(x, axis, [(i, (i + s) % count) for i, s in zip(starts, step)])]
    ppermute x5 -> x8, waiting for transfers between devices: 4.07 us -> 6.67 us  [send(): lax.ppermute(x, axis, [(i, (i + s) % count) for i, s in zip(starts, step)])]
    unnamed x6 -> x10, local copies, waits for them, and re-layouts: 0.02 us -> 1.91 us
    pallas_call x1, Pallas kernels: 2.59 us -> 2.21 us  [along(): pl.pallas_call(along_kernel, out_shape=(pltpu.VMEM(vel.shape, jnp.float32...]
    pallas_call x3 -> x7, Pallas kernels: 5.4 us -> 5.48 us  [the longest x4 3.17 us: outer(): pl.pallas_call(functools.partial(outer_kernel, x0, side, sizes), out_shap...]
  transfers between devices with their start and end apart: 5 -> 8, of which waited for: 3 -> 3; matrix products, arithmetic and copies ran while one was open for 0% -> 0% of each run, Pallas kernels for 29% -> 29%
where the time goes in v5:
time: 34.7 us; the launch traced here: 34.6 us
  starting transfers between devices  14.3 us (41%)
  Pallas kernels  10.9 us (31%)
  waiting for transfers between devices  6.67 us (19%)
  local copies, waits for them, and re-layouts  1.91 us (6%)
  between operations  0.81 us (2%)
    ppermute x8, starting transfers between devices, send(): lax.ppermute(x, axis, [(i, (i + s) % count) for i, s in zip(starts, step)])  14.3 us
    ppermute x8, waiting for transfers between devices, send(): lax.ppermute(x, axis, [(i, (i + s) % count) for i, s in zip(starts, step)])  6.67 us
    pallas_call x1, Pallas kernels, inner(): pl.pallas_call(inner_kernel, out_shape=pltpu.VMEM(vel.shape, jnp.float32)...  3.24 us
    pallas_call x4, Pallas kernels, outer(): pl.pallas_call(functools.partial(outer_kernel, x0, side, sizes), out_shap...  3.17 us
    pallas_call x1, Pallas kernels, along(): pl.pallas_call(along_kernel, out_shape=(pltpu.VMEM(vel.shape, jnp.float32...  2.21 us
    unnamed x10, local copies, waits for them, and re-layouts  1.91 us
    pallas_call x1, Pallas kernels, first(): pl.pallas_call(first_kernel, out_shape=halo_shape(vel, xs), in_specs=[pl....  1 us
    pallas_call x1, Pallas kernels, ends(): pl.pallas_call(ends_kernel, out_shape=(out, out, halo_shape(vel, nx)), in...  0.92 us
  transfers between devices with their start and end apart: 8, of which 3 were waited for; matrix products, arithmetic and copies ran while one was open for 0% of the time, Pallas kernels for 29%

profile of v5, /device:TPU:6, one launch (start us, length us, event | category | flops | bytes accessed | tf_op | source)
XLA Modules:
  0.0 34.6 jit_solution(5252013216362947109)
XLA Ops:
  0.6 0.0 copy-start
  0.6 1.9 %copy-done = f32[3,128,8,256]{3,2,1,0:T(8,128)S(1)} copy-done((f32[3,128,8,256]{3,2,1,0:T(8,128)S(1)}, f32[3,128,8,256]{3,2,1,0:T(8,128)}, u32[]{:S(2)}) %copy-start) | copy-done | bytes 3145752
  2.5 0.9 %ends.1 = (f32[2,3,2,8,128]{4,3,2,1,0:T(8,128)S(1)}, f32[2,3,2,8,128]{4,3,2,1,0:T(8,128)S(1)}, f32[3,3,128,256]{3,2,1,0:T(8,128)S(1)}) custom-call(f32[3,128,2,8,128]{4,3,2,1,0:T(8,128)S(1)} %bitcast.10), custom_call_target="tpu_custom_call" | custom-call | tf_op jit(solution)/shard_map/ends/pallas_call | solution.py:192
  3.4 0.0 copy-start.1
  3.5 0.0 copy-start.2
  3.5 0.0 copy-start.3
  3.5 0.0 copy-start.4
  3.5 0.1 collective-permute-start.2
  3.6 0.4 %rest.1 = (f32[3,3,80,256]{3,2,1,0:T(8,128)S(1)}, f32[3,3,32,256]{3,2,1,0:T(8,128)S(1)}, f32[3,3,96,256]{3,2,1,0:T(8,128)S(1)}, f32[3,3,32,256]{3,2,1,0:T(8,128)S(1)}) custom-call(f32[3,128,2,8,128]{4,3,2,1,0:T(8,128)S(1)} %bitcast.11), custom_call_target="tpu_custom_call" | custom-call | tf_op jit(solution)/shard_map/rest/pallas_call | solution.py:156
  4.0 8.4 %collective-permute-start.4 = (f32[3,3,96,256]{3,2,1,0:T(8,128)S(1)}, f32[3,3,96,256]{3,2,1,0:T(8,128)S(1)}, u32[]{:S(2)}, u32[]{:S(2)}) collective-permute-start(f32[3,3,96,256]{3,2,1,0:T(8,128)S(1)} %get-tuple-element.16), channel_id=1, source_target_pairs={{0,63},{1,0},{2,1},{3,2},{4,3},{5,4},{6,5},{7,6},{8,7},{9,8},{10,9... | collective-permute-start | bytes 2654216 | tf_op jit(solution)/shard_map/ppermute | solution.py:367
  12.4 0.0 collective-permute-start.7
  12.4 0.5 %collective-permute-start = (f32[2,3,2,8,128]{4,3,2,1,0:T(8,128)S(1)}, f32[2,3,2,8,128]{4,3,2,1,0:T(8,128)S(1)}, u32[]{:S(2)}, u32[]{:S(2)}) collective-permute-start(f32[2,3,2,8,128]{4,3,2,1,0:T(8,128)S(1)} %get-tuple-element.11), channel_id=1, source_target_pairs={{0,64},{64,128},{128,192},{192,0},{1,65},{65,129},{129,193},{193,1... | collective-permute-start | bytes 147464 | tf_op jit(solution)/shard_map/ppermute | solution.py:367
  12.9 1.5 %collective-permute-start.1 = (f32[2,3,2,8,128]{4,3,2,1,0:T(8,128)S(1)}, f32[2,3,2,8,128]{4,3,2,1,0:T(8,128)S(1)}, u32[]{:S(2)}, u32[]{:S(2)}) collective-permute-start(f32[2,3,2,8,128]{4,3,2,1,0:T(8,128)S(1)} %get-tuple-element.12), channel_id=1, source_target_pairs={{0,192},{64,0},{128,64},{192,128},{1,193},{65,1},{129,65},{193,129... | collective-permute-start | bytes 147464 | tf_op jit(solution)/shard_map/ppermute | solution.py:367
  14.4 2.1 %collective-permute-done.from_left = f32[2,3,2,8,128]{4,3,2,1,0:T(8,128)S(1)} collective-permute-done((f32[2,3,2,8,128]{4,3,2,1,0:T(8,128)S(1)}, f32[2,3,2,8,128]{4,3,2,1,0:T(8,128)S(1)}, u32[]{:S(2)}, u32[]{:S(2)}) %collective-permute-start) | collective-permute-done | bytes 49184 | tf_op jit(solution)/shard_map/ppermute | solution.py:367
  16.5 0.0 collective-permute-start.5
  16.5 1.7 %collective-permute-done.1.from_right = f32[2,3,2,8,128]{4,3,2,1,0:T(8,128)S(1)} collective-permute-done((f32[2,3,2,8,128]{4,3,2,1,0:T(8,128)S(1)}, f32[2,3,2,8,128]{4,3,2,1,0:T(8,128)S(1)}, u32[]{:S(2)}, u32[]{:S(2)}) %collective-permute-start.1) | collective-permute-done | bytes 49184 | tf_op jit(solution)/shard_map/ppermute | solution.py:367
  18.2 3.6 %collective-permute-start.3 = (f32[3,3,32,256]{3,2,1,0:T(8,128)S(1)}, f32[3,3,32,256]{3,2,1,0:T(8,128)S(1)}, u32[]{:S(2)}, u32[]{:S(2)}) collective-permute-start(f32[3,3,32,256]{3,2,1,0:T(8,128)S(1)} %get-tuple-element.15), channel_id=1, source_target_pairs={{0,63},{1,0},{2,1},{3,2},{4,3},{5,4},{6,5},{7,6},{8,7},{9,8},{10,9... | collective-permute-start | bytes 884744 | tf_op jit(solution)/shard_map/ppermute | solution.py:367
  21.8 1.0 %first.1 = f32[3,3,16,256]{3,2,1,0:T(8,128)S(1)} custom-call(f32[3,128,2,8,128]{4,3,2,1,0:T(8,128)} %bitcast.9), custom_call_target="tpu_custom_call" | custom-call | tf_op jit(solution)/shard_map/first/pallas_call | solution.py:121
  22.8 0.0 collective-permute-done.2.chip
  22.8 0.1 collective-permute-start.6
  22.9 0.0 copy-done.1
  22.9 0.0 copy-done.2
  23.0 0.0 copy-done.3
  23.0 0.0 copy-done.4
  23.0 3.2 %inner.1.adv_in = f32[3,128,2,8,128]{4,3,2,1,0:T(8,128)S(1)} custom-call(f32[3,128,2,8,128]{4,3,2,1,0:T(8,128)S(1)} %bitcast.12, f32[3,3,128,256]{3,2,1,0:T(8,128)S(1)} %collective-permute-done.2.chip, bf16[256,256]{1,0:T(8,128)(2,1)S(1)} %copy-done.4, bf16[256,256]{1,0:T(8,128)(2,1)S(1)} %copy-done.3, bf16[2,256,96]{2,1,0:T(8,128)(2,1)S(1)} %copy-done.2), custom_call_target="tpu_custom_call" | custom-call | tf_op jit(solution)/shard_map/inner/pallas_call | solution.py:223
  26.2 2.2 %along.1 = (f32[3,128,2,8,128]{4,3,2,1,0:T(8,128)S(1)}, f32[3,128,2,8,128]{4,3,2,1,0:T(8,128)}) custom-call(f32[3,128,2,8,128]{4,3,2,1,0:T(8,128)S(1)} %bitcast.13, f32[2,3,2,8,128]{4,3,2,1,0:T(8,128)S(1)} %collective-permute-done.from_left, f32[2,3,2,8,128]{4,3,2,1,0:T(8,128)S(1)} %collective-permute-done.1.from_right, ...), custom_call_target="tpu_custom_call", output_to_operand_aliasing={{0}: (3, {})} | custom-call | tf_op jit(solution)/shard_map/along/pallas_call | solution.py:280
  28.4 2.9 %collective-permute-done.6.refs_3_ = f32[3,3,16,256]{3,2,1,0:T(8,128)S(1)} collective-permute-done((f32[3,3,16,256]{3,2,1,0:T(8,128)S(1)}, f32[3,3,16,256]{3,2,1,0:T(8,128)S(1)}, u32[]{:S(2)}, u32[]{:S(2)}) %collective-permute-start.6) | collective-permute-done | bytes 147488 | tf_op jit(solution)/shard_map/ppermute | solution.py:367
  31.4 0.0 collective-permute-done.7.refs_4_
  31.4 1.8 %outer.4.refs_4_ = f32[3,128,2,8,128]{4,3,2,1,0:T(8,128)} custom-call(f32[3,128,2,8,128]{4,3,2,1,0:T(8,128)S(1)} %bitcast.14, f32[3,128,2,8,128]{4,3,2,1,0:T(8,128)S(1)} %get-tuple-element.14.refs_1_, bf16[2,256,96]{2,1,0:T(8,128)(2,1)S(1)} %copy-done.2, f32[3,3,16,256]{3,2,1,0:T(8,128)S(1)} %collective-permute-done.6.refs_3_, ...), custom_call_target="tpu_custom_call" | custom-call | tf_op jit(solution)/shard_map/outer/pallas_call | solution.py:350
  33.2 0.0 collective-permute-done.5.refs_3_
  33.2 1.3 %outer.5.refs_4_ = f32[3,128,2,8,128]{4,3,2,1,0:T(8,128)} custom-call(f32[3,128,2,8,128]{4,3,2,1,0:T(8,128)S(1)} %bitcast.15, f32[3,128,2,8,128]{4,3,2,1,0:T(8,128)S(1)} %get-tuple-element.14.refs_1_, bf16[2,256,96]{2,1,0:T(8,128)(2,1)S(1)} %copy-done.2, f32[3,3,32,256]{3,2,1,0:T(8,128)S(1)} %collective-permute-done.5.refs_3_, ...), custom_call_target="tpu_custom_call", output_to_operand_aliasing={{}: (4, {})} | custom-call | tf_op jit(solution)/shard_map/outer/pallas_call | solution.py:350
  34.5 0.0 collective-permute-done.4.refs_3_
  34.5 0.0 collective-permute-done.3.refs_3_
  (2 shorter events, 0.1 us)
Async XLA Ops:
  0.6 1.9 %copy-start = (f32[3,128,8,256]{3,2,1,0:T(8,128)S(1)}, f32[3,128,8,256]{3,2,1,0:T(8,128)}, u32[]{:S(2)}) copy-start(f32[3,128,8,256]{3,2,1,0:T(8,128)} %param.4) | copy-start | bytes 9437188
  3.4 19.5 %copy-start.1 = (f32[3,128,8,256]{3,2,1,0:T(8,128)S(1)}, f32[3,128,8,256]{3,2,1,0:T(8,128)}, u32[]{:S(2)}) copy-start(f32[3,128,8,256]{3,2,1,0:T(8,128)} %param.4) | copy-start | bytes 9437188
  3.5 19.5 %copy-start.2 = (bf16[2,256,96]{2,1,0:T(8,128)(2,1)S(1)}, bf16[2,256,96]{2,1,0:T(8,128)(2,1)}, u32[]{:S(2)}) copy-start(bf16[2,256,96]{2,1,0:T(8,128)(2,1)} %constant.8.clone.hmat.refs_2_) | copy-start | bytes 294916
  3.5 19.5 %copy-start.3 = (bf16[256,256]{1,0:T(8,128)(2,1)S(1)}, bf16[256,256]{1,0:T(8,128)(2,1)}, u32[]{:S(2)}) copy-start(bf16[256,256]{1,0:T(8,128)(2,1)} %constant.7.clone.ymat) | copy-start | bytes 393220
  3.5 19.5 %copy-start.4 = (bf16[256,256]{1,0:T(8,128)(2,1)S(1)}, bf16[256,256]{1,0:T(8,128)(2,1)}, u32[]{:S(2)}) copy-start(bf16[256,256]{1,0:T(8,128)(2,1)} %constant.6.clone.zmat) | copy-start | bytes 393220
  3.5 19.3 %collective-permute-start.2 = (f32[3,3,128,256]{3,2,1,0:T(8,128)S(1)}, f32[3,3,128,256]{3,2,1,0:T(8,128)S(1)}, u32[]{:S(2)}, u32[]{:S(2)}) collective-permute-start(f32[3,3,128,256]{3,2,1,0:T(8,128)S(1)} %get-tuple-element.13), channel_id=1, source_target_pairs={{0,1},{1,0},{2,3},{3,2},{4,5},{5,4},{6,7},{7,6},{8,9},{9,8},{10,11... | collective-permute-start | bytes 3538952 | tf_op jit(solution)/shard_map/ppermute | solution.py:367
  4.0 30.5 %collective-permute-start.4 = (f32[3,3,96,256]{3,2,1,0:T(8,128)S(1)}, f32[3,3,96,256]{3,2,1,0:T(8,128)S(1)}, u32[]{:S(2)}, u32[]{:S(2)}) collective-permute-start(f32[3,3,96,256]{3,2,1,0:T(8,128)S(1)} %get-tuple-element.16), channel_id=1, source_target_pairs={{0,63},{1,0},{2,1},{3,2},{4,3},{5,4},{6,5},{7,6},{8,7},{9,8},{10,9... | collective-permute-start | bytes 2654216 | tf_op jit(solution)/shard_map/ppermute | solution.py:367
  12.4 19.0 %collective-permute-start.7 = (f32[3,3,80,256]{3,2,1,0:T(8,128)S(1)}, f32[3,3,80,256]{3,2,1,0:T(8,128)S(1)}, u32[]{:S(2)}, u32[]{:S(2)}) collective-permute-start(f32[3,3,80,256]{3,2,1,0:T(8,128)S(1)} %get-tuple-element.18), channel_id=1, source_target_pairs={{0,1},{1,2},{2,3},{3,4},{4,5},{5,6},{6,7},{7,8},{8,9},{9,10},{10,1... | collective-permute-start | bytes 2211848 | tf_op jit(solution)/shard_map/ppermute | solution.py:367
  12.4 4.1 %collective-permute-start = (f32[2,3,2,8,128]{4,3,2,1,0:T(8,128)S(1)}, f32[2,3,2,8,128]{4,3,2,1,0:T(8,128)S(1)}, u32[]{:S(2)}, u32[]{:S(2)}) collective-permute-start(f32[2,3,2,8,128]{4,3,2,1,0:T(8,128)S(1)} %get-tuple-element.11), channel_id=1, source_target_pairs={{0,64},{64,128},{128,192},{192,0},{1,65},{65,129},{129,193},{193,1... | collective-permute-start | bytes 147464 | tf_op jit(solution)/shard_map/ppermute | solution.py:367
  12.9 5.3 %collective-permute-start.1 = (f32[2,3,2,8,128]{4,3,2,1,0:T(8,128)S(1)}, f32[2,3,2,8,128]{4,3,2,1,0:T(8,128)S(1)}, u32[]{:S(2)}, u32[]{:S(2)}) collective-permute-start(f32[2,3,2,8,128]{4,3,2,1,0:T(8,128)S(1)} %get-tuple-element.12), channel_id=1, source_target_pairs={{0,192},{64,0},{128,64},{192,128},{1,193},{65,1},{129,65},{193,129... | collective-permute-start | bytes 147464 | tf_op jit(solution)/shard_map/ppermute | solution.py:367
  16.5 16.7 %collective-permute-start.5 = (f32[3,3,32,256]{3,2,1,0:T(8,128)S(1)}, f32[3,3,32,256]{3,2,1,0:T(8,128)S(1)}, u32[]{:S(2)}, u32[]{:S(2)}) collective-permute-start(f32[3,3,32,256]{3,2,1,0:T(8,128)S(1)} %get-tuple-element.17), channel_id=1, source_target_pairs={{0,1},{1,2},{2,3},{3,4},{4,5},{5,6},{6,7},{7,8},{8,9},{9,10},{10,1... | collective-permute-start | bytes 884744 | tf_op jit(solution)/shard_map/ppermute | solution.py:367
  18.2 16.4 %collective-permute-start.3 = (f32[3,3,32,256]{3,2,1,0:T(8,128)S(1)}, f32[3,3,32,256]{3,2,1,0:T(8,128)S(1)}, u32[]{:S(2)}, u32[]{:S(2)}) collective-permute-start(f32[3,3,32,256]{3,2,1,0:T(8,128)S(1)} %get-tuple-element.15), channel_id=1, source_target_pairs={{0,63},{1,0},{2,1},{3,2},{4,3},{5,4},{6,5},{7,6},{8,7},{9,8},{10,9... | collective-permute-start | bytes 884744 | tf_op jit(solution)/shard_map/ppermute | solution.py:367
  22.8 8.5 %collective-permute-start.6 = (f32[3,3,16,256]{3,2,1,0:T(8,128)S(1)}, f32[3,3,16,256]{3,2,1,0:T(8,128)S(1)}, u32[]{:S(2)}, u32[]{:S(2)}) collective-permute-start(f32[3,3,16,256]{3,2,1,0:T(8,128)S(1)} %first.1), channel_id=1, source_target_pairs={{0,1},{1,2},{2,3},{3,4},{4,5},{5,6},{6,7},{7,8},{8,9},{9,10},{10,1... | collective-permute-start | bytes 442376 | tf_op jit(solution)/shard_map/ppermute | solution.py:367

commit v6 on v5

--- a/solution.py
+++ b/solution.py
@@ -16,11 +16,12 @@
 R = float(ROOT)
 GAIN = float(1.0 / (1.0 - ROOT * ROOT))
 TAPS = {1: 45.0, 2: -9.0, 3: 1.0, -1: -45.0, -2: 9.0, -3: -1.0}
-UP = (16, 80, 32)
-DOWN = (96, 32)
-UP_STAGES = ((0, (0, 1)), (96, (2,)))
-DOWN_STAGES = ((0, (0,)), (96, (1,)))
-XB = 32
+UP = (16, 88, 24)
+DOWN = (104, 24)
+UP_STAGES = ((0, (0, 1)), (104, (2,)))
+DOWN_STAGES = ((0, (0,)), (104, (1,)))
+XB = 16
+OB = 8
 EB = 8
 LANES = 128
 
@@ -199,9 +200,9 @@
     )(vel)
 
 
-def inner_kernel(vel, chip, zmat, ymat, hmat, adv):
+def inner_kernel(vel, chip, zmat, ymat, adv):
+    comps, n, halves, _, lanes = vel.shape
     side = 1 - parity()
-    comps, n, halves, _, lanes = vel.shape
 
     def block(b, _):
         rows = pl.ds(b * XB, XB)
@@ -210,24 +211,23 @@
         for c in range(comps):
             f = rows_of(vel, c, rows)
             gz = split_dot(zmat[...], f, flip=True)
-            gy = split_dot(ymat[...], f)
             halo = chip[c, :, rows].reshape(-1, halves * lanes)
-            gy = gy + split_dot(hmat[side], halo)
+            gy = split_dot(ymat[side], jnp.concatenate([f, halo], axis=0))
             put_rows(adv, c, rows, sv * gy + sw * gz)
         return 0
 
     lax.fori_loop(0, n // XB, block, 0)
 
 
-def inner(vel, chip, zmat, ymat, hmat):
+def inner(vel, chip, zmat, ymat):
     return pl.pallas_call(
         inner_kernel,
         out_shape=pltpu.VMEM(vel.shape, jnp.float32),
-        in_specs=in_vmem(5),
+        in_specs=in_vmem(4),
         out_specs=pl.BlockSpec(memory_space=pltpu.VMEM),
         compiler_params=pltpu.CompilerParams(vmem_limit_bytes=8 << 20),
         name="inner",
-    )(vel, chip, zmat, ymat, hmat)
+    )(vel, chip, zmat, ymat)
 
 
 def along_kernel(vel, from_left, from_right, adv_in, adv, deriv_out, deriv, sems):
@@ -304,32 +304,33 @@
     adv_out, adv, sems = refs[-3:]
     comps, xs, halves, _, lanes = adv.shape
 
+    span = OB if xs <= 32 else 4 * OB
+
     def take(c, at):
-        parts = []
-        need = XB
         for size, ref in zip(sizes, pieces):
-            count = min(size - at, need)
-            if count > 0:
-                parts.append(ref[c, :, at : at + count])
-                need -= count
-                at = 0
-            else:
-                at -= size
-        both = parts[0] if len(parts) == 1 else jnp.concatenate(parts, axis=1)
-        return both.reshape(-1, halves * lanes)
+            if at < size:
+                return ref[c, :, at : at + OB].reshape(-1, halves * lanes)
+            at -= size
 
     @pl.when(parity() == side)
     def _():
         copies = []
-        for b in range(xs // XB):
-            here = pl.ds(b * XB, XB)
-            rows = pl.ds(x0 + b * XB, XB)
-            sv = rows_of(vel, 1, rows) * (1.0 / 60.0)
-            for c in range(comps):
-                gy = split_dot(hmat[side], take(c, b * XB))
-                put_rows(adv, c, here, rows_of(adv_in, c, rows) - sv * gy)
+        for start in range(0, xs, span):
+            count = min(span, xs - start)
+            for at in range(start, start + count, OB):
+                rows = pl.ds(x0 + at, OB)
+                sv = rows_of(vel, 1, rows) * (1.0 / 60.0)
+                for c in range(comps):
+                    gy = split_dot(hmat[side], take(c, at))
+                    put_rows(
+                        adv, c, pl.ds(at, OB), rows_of(adv_in, c, rows) - sv * gy
+                    )
             copies.append(
-                pltpu.make_async_copy(adv.at[:, here], adv_out.at[:, rows], sems.at[b])
+                pltpu.make_async_copy(
+                    adv.at[:, pl.ds(start, count)],
+                    adv_out.at[:, pl.ds(x0 + start, count)],
+                    sems.at[start // span],
+                )
             )
             copies[-1].start()
         for cp in copies:
@@ -354,7 +355,7 @@
         out_specs=pl.BlockSpec(memory_space=pl.ANY),
         scratch_shapes=[
             pltpu.VMEM((comps, xs, halves, tile, lanes), jnp.float32),
-            pltpu.SemaphoreType.DMA((xs // XB,)),
+            pltpu.SemaphoreType.DMA((4,)),
         ],
         input_output_aliases=alias,
         compiler_params=pltpu.CompilerParams(vmem_limit_bytes=8 << 20),
@@ -381,8 +382,9 @@
     comps, nx, tile, nz = velocity.shape
     halves = nz // LANES
     zmat = jnp.asarray(z_matrix(nz), jnp.bfloat16)
-    ymat = jnp.asarray(y_matrix(tile, XB), jnp.bfloat16)
-    hmat = jnp.asarray(halo_matrices(tile, XB), jnp.bfloat16)
+    both = [np.concatenate([y_matrix(tile, XB), m], 1) for m in halo_matrices(tile, XB)]
+    ymat = jnp.asarray(np.stack(both), jnp.bfloat16)
+    omat = jnp.asarray(halo_matrices(tile, OB), jnp.bfloat16)
     vel = velocity.reshape(comps, nx, tile, halves, LANES).transpose(0, 1, 3, 2, 4)
     up = [first(vel, UP[0])]
     sends = rest(vel)
@@ -394,12 +396,12 @@
     chip = swap(chip, "cross")
     from_left = shift(right, "line", 1)
     from_right = shift(left, "line", -1)
-    adv = inner(vel, chip, zmat, ymat, hmat)
+    adv = inner(vel, chip, zmat, ymat)
     adv, deriv = along(vel, from_left, from_right, adv)
     out = None
     for side, parts, stages in ((0, lows, UP_STAGES), (1, highs, DOWN_STAGES)):
         for x0, which in stages:
-            out = outer(vel, adv, hmat, [parts[k] for k in which], x0, side, out)
+            out = outer(vel, adv, omat, [parts[k] for k in which], x0, side, out)
     return tuple(
         v.transpose(0, 1, 3, 2, 4).reshape(velocity.shape) for v in (out, deriv)
     )

time: 34.7 us -> 34.6 us (level)
  transfers between devices with their start and end apart: 8 -> 8, of which waited for: 3 -> 3; matrix products, arithmetic and copies ran while one was open for 0% -> 0% of each run, Pallas kernels for 29% -> 28%
where the time goes in v6:
time: 34.6 us; the launch traced here: 34.4 us
  starting transfers between devices  14.3 us (41%)
  Pallas kernels  10.6 us (31%)
  waiting for transfers between devices  6.87 us (20%)
  local copies, waits for them, and re-layouts  1.91 us (6%)
  between operations  0.8 us (2%)
    ppermute x8, starting transfers between devices, send(): lax.ppermute(x, axis, [(i, (i + s) % count) for i, s in zip(starts, step)])  14.3 us
    ppermute x8, waiting for transfers between devices, send(): lax.ppermute(x, axis, [(i, (i + s) % count) for i, s in zip(starts, step)])  6.87 us
    pallas_call x1, Pallas kernels, inner(): pl.pallas_call(inner_kernel, out_shape=pltpu.VMEM(vel.shape, jnp.float32)...  3.04 us
    pallas_call x4, Pallas kernels, outer(): pl.pallas_call(functools.partial(outer_kernel, x0, side, sizes), out_shap...  3.02 us
    pallas_call x1, Pallas kernels, along(): pl.pallas_call(along_kernel, out_shape=(pltpu.VMEM(vel.shape, jnp.float32...  2.21 us
    unnamed x10, local copies, waits for them, and re-layouts  1.91 us
    pallas_call x1, Pallas kernels, first(): pl.pallas_call(first_kernel, out_shape=halo_shape(vel, xs), in_specs=[pl....  1 us
    pallas_call x1, Pallas kernels, ends(): pl.pallas_call(ends_kernel, out_shape=(out, out, halo_shape(vel, nx)), in...  0.92 us
  transfers between devices with their start and end apart: 8, of which 3 were waited for; matrix products, arithmetic and copies ran while one was open for 0% of the time, Pallas kernels for 28%

profile of v6, /device:TPU:6, one launch (start us, length us, event | category | flops | bytes accessed | tf_op | source)
XLA Modules:
  0.0 34.4 jit_solution(17563390614770578648)
XLA Ops:
  0.6 0.0 copy-start
  0.6 1.9 %copy-done = f32[3,128,8,256]{3,2,1,0:T(8,128)S(1)} copy-done((f32[3,128,8,256]{3,2,1,0:T(8,128)S(1)}, f32[3,128,8,256]{3,2,1,0:T(8,128)}, u32[]{:S(2)}) %copy-start) | copy-done | bytes 3145752
  2.5 0.9 %ends.1 = (f32[2,3,2,8,128]{4,3,2,1,0:T(8,128)S(1)}, f32[2,3,2,8,128]{4,3,2,1,0:T(8,128)S(1)}, f32[3,3,128,256]{3,2,1,0:T(8,128)S(1)}) custom-call(f32[3,128,2,8,128]{4,3,2,1,0:T(8,128)S(1)} %bitcast.10), custom_call_target="tpu_custom_call" | custom-call | tf_op jit(solution)/shard_map/ends/pallas_call | solution.py:193
  3.4 0.0 copy-start.1
  3.5 0.0 copy-start.3
  3.5 0.0 copy-start.4
  3.5 0.1 collective-permute-start.2
  3.6 0.4 %rest.1 = (f32[3,3,88,256]{3,2,1,0:T(8,128)S(1)}, f32[3,3,24,256]{3,2,1,0:T(8,128)S(1)}, f32[3,3,104,256]{3,2,1,0:T(8,128)S(1)}, f32[3,3,24,256]{3,2,1,0:T(8,128)S(1)}) custom-call(f32[3,128,2,8,128]{4,3,2,1,0:T(8,128)S(1)} %bitcast.11), custom_call_target="tpu_custom_call" | custom-call | tf_op jit(solution)/shard_map/rest/pallas_call | solution.py:157
  4.0 8.4 %collective-permute-start.4 = (f32[3,3,104,256]{3,2,1,0:T(8,128)S(1)}, f32[3,3,104,256]{3,2,1,0:T(8,128)S(1)}, u32[]{:S(2)}, u32[]{:S(2)}) collective-permute-start(f32[3,3,104,256]{3,2,1,0:T(8,128)S(1)} %get-tuple-element.16), channel_id=1, source_target_pairs={{0,63},{1,0},{2,1},{3,2},{4,3},{5,4},{6,5},{7,6},{8,7},{9,8},{10,9... | collective-permute-start | bytes 2875400 | tf_op jit(solution)/shard_map/ppermute | solution.py:368
  12.4 0.0 collective-permute-start.7
  12.4 0.5 %collective-permute-start = (f32[2,3,2,8,128]{4,3,2,1,0:T(8,128)S(1)}, f32[2,3,2,8,128]{4,3,2,1,0:T(8,128)S(1)}, u32[]{:S(2)}, u32[]{:S(2)}) collective-permute-start(f32[2,3,2,8,128]{4,3,2,1,0:T(8,128)S(1)} %get-tuple-element.11), channel_id=1, source_target_pairs={{0,64},{64,128},{128,192},{192,0},{1,65},{65,129},{129,193},{193,1... | collective-permute-start | bytes 147464 | tf_op jit(solution)/shard_map/ppermute | solution.py:368
  12.9 1.5 %collective-permute-start.1 = (f32[2,3,2,8,128]{4,3,2,1,0:T(8,128)S(1)}, f32[2,3,2,8,128]{4,3,2,1,0:T(8,128)S(1)}, u32[]{:S(2)}, u32[]{:S(2)}) collective-permute-start(f32[2,3,2,8,128]{4,3,2,1,0:T(8,128)S(1)} %get-tuple-element.12), channel_id=1, source_target_pairs={{0,192},{64,0},{128,64},{192,128},{1,193},{65,1},{129,65},{193,129... | collective-permute-start | bytes 147464 | tf_op jit(solution)/shard_map/ppermute | solution.py:368
  14.4 2.1 %collective-permute-done.from_left = f32[2,3,2,8,128]{4,3,2,1,0:T(8,128)S(1)} collective-permute-done((f32[2,3,2,8,128]{4,3,2,1,0:T(8,128)S(1)}, f32[2,3,2,8,128]{4,3,2,1,0:T(8,128)S(1)}, u32[]{:S(2)}, u32[]{:S(2)}) %collective-permute-start) | collective-permute-done | bytes 49184 | tf_op jit(solution)/shard_map/ppermute | solution.py:368
  16.5 0.0 collective-permute-start.5
  16.5 1.7 %collective-permute-done.1.from_right = f32[2,3,2,8,128]{4,3,2,1,0:T(8,128)S(1)} collective-permute-done((f32[2,3,2,8,128]{4,3,2,1,0:T(8,128)S(1)}, f32[2,3,2,8,128]{4,3,2,1,0:T(8,128)S(1)}, u32[]{:S(2)}, u32[]{:S(2)}) %collective-permute-start.1) | collective-permute-done | bytes 49184 | tf_op jit(solution)/shard_map/ppermute | solution.py:368
  18.2 3.6 %collective-permute-start.3 = (f32[3,3,24,256]{3,2,1,0:T(8,128)S(1)}, f32[3,3,24,256]{3,2,1,0:T(8,128)S(1)}, u32[]{:S(2)}, u32[]{:S(2)}) collective-permute-start(f32[3,3,24,256]{3,2,1,0:T(8,128)S(1)} %get-tuple-element.15), channel_id=1, source_target_pairs={{0,63},{1,0},{2,1},{3,2},{4,3},{5,4},{6,5},{7,6},{8,7},{9,8},{10,9... | collective-permute-start | bytes 663560 | tf_op jit(solution)/shard_map/ppermute | solution.py:368
  21.8 1.0 %first.1 = f32[3,3,16,256]{3,2,1,0:T(8,128)S(1)} custom-call(f32[3,128,2,8,128]{4,3,2,1,0:T(8,128)} %bitcast.9), custom_call_target="tpu_custom_call" | custom-call | tf_op jit(solution)/shard_map/first/pallas_call | solution.py:122
  22.8 0.0 collective-permute-done.2.chip
  22.8 0.1 collective-permute-start.6
  22.9 0.0 copy-done.1
  22.9 0.0 copy-done.3
  22.9 0.0 copy-done.4
  23.0 3.0 %inner.1.adv_in = f32[3,128,2,8,128]{4,3,2,1,0:T(8,128)S(1)} custom-call(f32[3,128,2,8,128]{4,3,2,1,0:T(8,128)S(1)} %bitcast.12, f32[3,3,128,256]{3,2,1,0:T(8,128)S(1)} %collective-permute-done.2.chip, bf16[256,256]{1,0:T(8,128)(2,1)S(1)} %copy-done.4, bf16[2,128,176]{2,1,0:T(8,128)(2,1)S(1)} %copy-done.3), custom_call_target="tpu_custom_call" | custom-call | tf_op jit(solution)/shard_map/inner/pallas_call | solution.py:223
  26.0 0.0 copy-start.2
  26.0 2.2 %along.1 = (f32[3,128,2,8,128]{4,3,2,1,0:T(8,128)S(1)}, f32[3,128,2,8,128]{4,3,2,1,0:T(8,128)}) custom-call(f32[3,128,2,8,128]{4,3,2,1,0:T(8,128)S(1)} %bitcast.13, f32[2,3,2,8,128]{4,3,2,1,0:T(8,128)S(1)} %collective-permute-done.from_left, f32[2,3,2,8,128]{4,3,2,1,0:T(8,128)S(1)} %collective-permute-done.1.from_right, ...), custom_call_target="tpu_custom_call", output_to_operand_aliasing={{0}: (3, {})} | custom-call | tf_op jit(solution)/shard_map/along/pallas_call | solution.py:280
  28.2 3.1 %collective-permute-done.6.refs_3_ = f32[3,3,16,256]{3,2,1,0:T(8,128)S(1)} collective-permute-done((f32[3,3,16,256]{3,2,1,0:T(8,128)S(1)}, f32[3,3,16,256]{3,2,1,0:T(8,128)S(1)}, u32[]{:S(2)}, u32[]{:S(2)}) %collective-permute-start.6) | collective-permute-done | bytes 147488 | tf_op jit(solution)/shard_map/ppermute | solution.py:368
  31.3 0.0 collective-permute-done.7.refs_4_
  31.3 0.0 copy-done.2
  31.3 1.9 %outer.4.refs_4_ = f32[3,128,2,8,128]{4,3,2,1,0:T(8,128)} custom-call(f32[3,128,2,8,128]{4,3,2,1,0:T(8,128)S(1)} %bitcast.14, f32[3,128,2,8,128]{4,3,2,1,0:T(8,128)S(1)} %get-tuple-element.14.refs_1_, bf16[2,64,24]{2,1,0:T(8,128)(2,1)S(1)} %copy-done.2, f32[3,3,16,256]{3,2,1,0:T(8,128)S(1)} %collective-permute-done.6.refs_3_, ...), custom_call_target="tpu_custom_call" | custom-call | tf_op jit(solution)/shard_map/outer/pallas_call | solution.py:351
  33.2 0.0 collective-permute-done.5.refs_3_
  33.2 1.1 %outer.5.refs_4_ = f32[3,128,2,8,128]{4,3,2,1,0:T(8,128)} custom-call(f32[3,128,2,8,128]{4,3,2,1,0:T(8,128)S(1)} %bitcast.15, f32[3,128,2,8,128]{4,3,2,1,0:T(8,128)S(1)} %get-tuple-element.14.refs_1_, bf16[2,64,24]{2,1,0:T(8,128)(2,1)S(1)} %copy-done.2, f32[3,3,24,256]{3,2,1,0:T(8,128)S(1)} %collective-permute-done.5.refs_3_, ...), custom_call_target="tpu_custom_call", output_to_operand_aliasing={{}: (4, {})} | custom-call | tf_op jit(solution)/shard_map/outer/pallas_call | solution.py:351
  34.3 0.0 collective-permute-done.4.refs_3_
  34.3 0.1 outer.6.refs_4_
  34.4 0.0 collective-permute-done.3.refs_3_
  34.4 0.1 outer.7
Async XLA Ops:
  0.6 1.9 %copy-start = (f32[3,128,8,256]{3,2,1,0:T(8,128)S(1)}, f32[3,128,8,256]{3,2,1,0:T(8,128)}, u32[]{:S(2)}) copy-start(f32[3,128,8,256]{3,2,1,0:T(8,128)} %param.4) | copy-start | bytes 9437188
  3.4 19.5 %copy-start.1 = (f32[3,128,8,256]{3,2,1,0:T(8,128)S(1)}, f32[3,128,8,256]{3,2,1,0:T(8,128)}, u32[]{:S(2)}) copy-start(f32[3,128,8,256]{3,2,1,0:T(8,128)} %param.4) | copy-start | bytes 9437188
  3.5 19.5 %copy-start.3 = (bf16[2,128,176]{2,1,0:T(8,128)(2,1)S(1)}, bf16[2,128,176]{2,1,0:T(8,128)(2,1)}, u32[]{:S(2)}) copy-start(bf16[2,128,176]{2,1,0:T(8,128)(2,1)} %constant.7.clone.ymat) | copy-start | bytes 270340
  3.5 19.5 %copy-start.4 = (bf16[256,256]{1,0:T(8,128)(2,1)S(1)}, bf16[256,256]{1,0:T(8,128)(2,1)}, u32[]{:S(2)}) copy-start(bf16[256,256]{1,0:T(8,128)(2,1)} %constant.6.clone.zmat) | copy-start | bytes 393220
  3.5 19.3 %collective-permute-start.2 = (f32[3,3,128,256]{3,2,1,0:T(8,128)S(1)}, f32[3,3,128,256]{3,2,1,0:T(8,128)S(1)}, u32[]{:S(2)}, u32[]{:S(2)}) collective-permute-start(f32[3,3,128,256]{3,2,1,0:T(8,128)S(1)} %get-tuple-element.13), channel_id=1, source_target_pairs={{0,1},{1,0},{2,3},{3,2},{4,5},{5,4},{6,7},{7,6},{8,9},{9,8},{10,11... | collective-permute-start | bytes 3538952 | tf_op jit(solution)/shard_map/ppermute | solution.py:368
  4.0 30.3 %collective-permute-start.4 = (f32[3,3,104,256]{3,2,1,0:T(8,128)S(1)}, f32[3,3,104,256]{3,2,1,0:T(8,128)S(1)}, u32[]{:S(2)}, u32[]{:S(2)}) collective-permute-start(f32[3,3,104,256]{3,2,1,0:T(8,128)S(1)} %get-tuple-element.16), channel_id=1, source_target_pairs={{0,63},{1,0},{2,1},{3,2},{4,3},{5,4},{6,5},{7,6},{8,7},{9,8},{10,9... | collective-permute-start | bytes 2875400 | tf_op jit(solution)/shard_map/ppermute | solution.py:368
  12.4 19.0 %collective-permute-start.7 = (f32[3,3,88,256]{3,2,1,0:T(8,128)S(1)}, f32[3,3,88,256]{3,2,1,0:T(8,128)S(1)}, u32[]{:S(2)}, u32[]{:S(2)}) collective-permute-start(f32[3,3,88,256]{3,2,1,0:T(8,128)S(1)} %get-tuple-element.18), channel_id=1, source_target_pairs={{0,1},{1,2},{2,3},{3,4},{4,5},{5,6},{6,7},{7,8},{8,9},{9,10},{10,1... | collective-permute-start | bytes 2433032 | tf_op jit(solution)/shard_map/ppermute | solution.py:368
  12.4 4.1 %collective-permute-start = (f32[2,3,2,8,128]{4,3,2,1,0:T(8,128)S(1)}, f32[2,3,2,8,128]{4,3,2,1,0:T(8,128)S(1)}, u32[]{:S(2)}, u32[]{:S(2)}) collective-permute-start(f32[2,3,2,8,128]{4,3,2,1,0:T(8,128)S(1)} %get-tuple-element.11), channel_id=1, source_target_pairs={{0,64},{64,128},{128,192},{192,0},{1,65},{65,129},{129,193},{193,1... | collective-permute-start | bytes 147464 | tf_op jit(solution)/shard_map/ppermute | solution.py:368
  12.9 5.3 %collective-permute-start.1 = (f32[2,3,2,8,128]{4,3,2,1,0:T(8,128)S(1)}, f32[2,3,2,8,128]{4,3,2,1,0:T(8,128)S(1)}, u32[]{:S(2)}, u32[]{:S(2)}) collective-permute-start(f32[2,3,2,8,128]{4,3,2,1,0:T(8,128)S(1)} %get-tuple-element.12), channel_id=1, source_target_pairs={{0,192},{64,0},{128,64},{192,128},{1,193},{65,1},{129,65},{193,129... | collective-permute-start | bytes 147464 | tf_op jit(solution)/shard_map/ppermute | solution.py:368
  16.5 16.7 %collective-permute-start.5 = (f32[3,3,24,256]{3,2,1,0:T(8,128)S(1)}, f32[3,3,24,256]{3,2,1,0:T(8,128)S(1)}, u32[]{:S(2)}, u32[]{:S(2)}) collective-permute-start(f32[3,3,24,256]{3,2,1,0:T(8,128)S(1)} %get-tuple-element.17), channel_id=1, source_target_pairs={{0,1},{1,2},{2,3},{3,4},{4,5},{5,6},{6,7},{7,8},{8,9},{9,10},{10,1... | collective-permute-start | bytes 663560 | tf_op jit(solution)/shard_map/ppermute | solution.py:368
  18.2 16.2 %collective-permute-start.3 = (f32[3,3,24,256]{3,2,1,0:T(8,128)S(1)}, f32[3,3,24,256]{3,2,1,0:T(8,128)S(1)}, u32[]{:S(2)}, u32[]{:S(2)}) collective-permute-start(f32[3,3,24,256]{3,2,1,0:T(8,128)S(1)} %get-tuple-element.15), channel_id=1, source_target_pairs={{0,63},{1,0},{2,1},{3,2},{4,3},{5,4},{6,5},{7,6},{8,7},{9,8},{10,9... | collective-permute-start | bytes 663560 | tf_op jit(solution)/shard_map/ppermute | solution.py:368
  22.8 8.5 %collective-permute-start.6 = (f32[3,3,16,256]{3,2,1,0:T(8,128)S(1)}, f32[3,3,16,256]{3,2,1,0:T(8,128)S(1)}, u32[]{:S(2)}, u32[]{:S(2)}) collective-permute-start(f32[3,3,16,256]{3,2,1,0:T(8,128)S(1)} %first.1), channel_id=1, source_target_pairs={{0,1},{1,2},{2,3},{3,4},{4,5},{5,6},{6,7},{7,8},{8,9},{9,10},{10,1... | collective-permute-start | bytes 442376 | tf_op jit(solution)/shard_map/ppermute | solution.py:368
  26.0 5.4 %copy-start.2 = (bf16[2,64,24]{2,1,0:T(8,128)(2,1)S(1)}, bf16[2,64,24]{2,1,0:T(8,128)(2,1)}, u32[]{:S(2)}) copy-start(bf16[2,64,24]{2,1,0:T(8,128)(2,1)} %constant.8.clone.refs_2_) | copy-start | bytes 18436

commit v7 on v6

--- a/solution.py
+++ b/solution.py
@@ -21,6 +21,7 @@
 UP_STAGES = ((0, (0, 1)), (104, (2,)))
 DOWN_STAGES = ((0, (0,)), (104, (1,)))
 XB = 16
+UNROLL = 8
 OB = 8
 EB = 8
 LANES = 128
@@ -59,16 +60,18 @@
     return lax.rem(lax.axis_index("cross"), 2)
 
 
-def split_dot(mat, val, flip=False):
+def split(val):
     hi = val.astype(jnp.bfloat16)
-    lo = (val - hi.astype(jnp.float32)).astype(jnp.bfloat16)
-    if flip:
-        return jnp.dot(hi, mat, preferred_element_type=jnp.float32) + jnp.dot(
-            lo, mat, preferred_element_type=jnp.float32
-        )
-    return jnp.dot(mat, hi, preferred_element_type=jnp.float32) + jnp.dot(
-        mat, lo, preferred_element_type=jnp.float32
-    )
+    return hi, (val - hi.astype(jnp.float32)).astype(jnp.bfloat16)
+
+
+def dot(a, b):
+    return jnp.dot(a, b, preferred_element_type=jnp.float32)
+
+
+def split_dot(mat, val):
+    hi, lo = split(val)
+    return dot(mat, hi) + dot(mat, lo)
 
 
 def pack_rows(held, out, first, row):
@@ -108,12 +111,12 @@
 
 def first_kernel(vel, up, buf, sem):
     xs = up.shape[2]
-    cp = pltpu.make_async_copy(vel.at[:, pl.ds(0, xs)], buf, sem)
-    cp.start()
-    cp.wait()
 
     @pl.when(parity() == 1)
     def _():
+        cp = pltpu.make_async_copy(vel.at[:, pl.ds(0, xs)], buf, sem)
+        cp.start()
+        cp.wait()
         pack_rows(buf, up, buf.shape[3] - 3, 0)
 
 
@@ -201,22 +204,29 @@
 
 
 def inner_kernel(vel, chip, zmat, ymat, adv):
-    comps, n, halves, _, lanes = vel.shape
+    comps, n, halves, tile, lanes = vel.shape
     side = 1 - parity()
 
     def block(b, _):
         rows = pl.ds(b * XB, XB)
         sv = rows_of(vel, 1, rows) * (-1.0 / 60.0)
         sw = rows_of(vel, 2, rows) * (-1.0 / 60.0)
+        size = XB * tile
+        parts = [split(rows_of(vel, c, rows)) for c in range(comps)]
+        stack = [p[0] for p in parts] + [p[1] for p in parts]
+        gz = dot(jnp.concatenate(stack, axis=0), zmat[...])
         for c in range(comps):
-            f = rows_of(vel, c, rows)
-            gz = split_dot(zmat[...], f, flip=True)
-            halo = chip[c, :, rows].reshape(-1, halves * lanes)
-            gy = split_dot(ymat[side], jnp.concatenate([f, halo], axis=0))
-            put_rows(adv, c, rows, sv * gy + sw * gz)
+            halo = split(chip[c, :, rows].reshape(-1, halves * lanes))
+            gy = [
+                dot(ymat[side], jnp.concatenate([p, h], axis=0))
+                for p, h in zip(parts[c], halo)
+            ]
+            low = gz[(comps + c) * size : (comps + c + 1) * size]
+            along_z = gz[c * size : (c + 1) * size] + low
+            put_rows(adv, c, rows, sv * (gy[0] + gy[1]) + sw * along_z)
         return 0
 
-    lax.fori_loop(0, n // XB, block, 0)
+    lax.fori_loop(0, n // XB, block, 0, unroll=UNROLL)
 
 
 def inner(vel, chip, zmat, ymat):

time: 34.6 us -> 34.6 us (level)
  Pallas kernels: 10.6 us -> 8.47 us
  waiting for transfers between devices: 6.87 us -> 8.99 us
    ppermute x8, waiting for transfers between devices: 6.87 us -> 8.99 us  [send(): lax.ppermute(x, axis, [(i, (i + s) % count) for i, s in zip(starts, step)])]
    pallas_call x1, Pallas kernels: 3.04 us -> 1.92 us  [inner(): pl.pallas_call(inner_kernel, out_shape=pltpu.VMEM(vel.shape, jnp.float32)...]
    pallas_call x1, Pallas kernels: 1 us -> 0.01 us  [first(): pl.pallas_call(first_kernel, out_shape=halo_shape(vel, xs), in_specs=[pl....]
  transfers between devices with their start and end apart: 8 -> 8, of which waited for: 3 -> 3; matrix products, arithmetic and copies ran while one was open for 0% -> 0% of each run, Pallas kernels for 28% -> 22%
where the time goes in v7:
time: 34.6 us; the launch traced here: 34.4 us
  starting transfers between devices  14.3 us (41%)
  waiting for transfers between devices  8.99 us (26%)
  Pallas kernels  8.47 us (24%)
  local copies, waits for them, and re-layouts  1.91 us (6%)
  between operations  0.8 us (2%)
    ppermute x8, starting transfers between devices, send(): lax.ppermute(x, axis, [(i, (i + s) % count) for i, s in zip(starts, step)])  14.3 us
    ppermute x8, waiting for transfers between devices, send(): lax.ppermute(x, axis, [(i, (i + s) % count) for i, s in zip(starts, step)])  8.99 us
    pallas_call x4, Pallas kernels, outer(): pl.pallas_call(functools.partial(outer_kernel, x0, side, sizes), out_shap...  3.02 us
    pallas_call x1, Pallas kernels, along(): pl.pallas_call(along_kernel, out_shape=(pltpu.VMEM(vel.shape, jnp.float32...  2.21 us
    pallas_call x1, Pallas kernels, inner(): pl.pallas_call(inner_kernel, out_shape=pltpu.VMEM(vel.shape, jnp.float32)...  1.92 us
    unnamed x10, local copies, waits for them, and re-layouts  1.91 us
    pallas_call x1, Pallas kernels, ends(): pl.pallas_call(ends_kernel, out_shape=(out, out, halo_shape(vel, nx)), in...  0.92 us
  transfers between devices with their start and end apart: 8, of which 3 were waited for; matrix products, arithmetic and copies ran while one was open for 0% of the time, Pallas kernels for 22%

profile of v7, /device:TPU:6, one launch (start us, length us, event | category | flops | bytes accessed | tf_op | source)
XLA Modules:
  0.0 34.4 jit_solution(6401783169075980561)
XLA Ops:
  0.6 0.0 copy-start
  0.6 1.9 %copy-done = f32[3,128,8,256]{3,2,1,0:T(8,128)S(1)} copy-done((f32[3,128,8,256]{3,2,1,0:T(8,128)S(1)}, f32[3,128,8,256]{3,2,1,0:T(8,128)}, u32[]{:S(2)}) %copy-start) | copy-done | bytes 3145752
  2.5 0.9 %ends.1 = (f32[2,3,2,8,128]{4,3,2,1,0:T(8,128)S(1)}, f32[2,3,2,8,128]{4,3,2,1,0:T(8,128)S(1)}, f32[3,3,128,256]{3,2,1,0:T(8,128)S(1)}) custom-call(f32[3,128,2,8,128]{4,3,2,1,0:T(8,128)S(1)} %bitcast.10), custom_call_target="tpu_custom_call" | custom-call | tf_op jit(solution)/shard_map/ends/pallas_call | solution.py:196
  3.4 0.0 copy-start.1
  3.5 0.0 copy-start.3
  3.5 0.0 copy-start.4
  3.5 0.1 collective-permute-start.2
  3.6 0.4 %rest.1 = (f32[3,3,88,256]{3,2,1,0:T(8,128)S(1)}, f32[3,3,24,256]{3,2,1,0:T(8,128)S(1)}, f32[3,3,104,256]{3,2,1,0:T(8,128)S(1)}, f32[3,3,24,256]{3,2,1,0:T(8,128)S(1)}) custom-call(f32[3,128,2,8,128]{4,3,2,1,0:T(8,128)S(1)} %bitcast.11), custom_call_target="tpu_custom_call" | custom-call | tf_op jit(solution)/shard_map/rest/pallas_call | solution.py:160
  4.0 8.4 %collective-permute-start.4 = (f32[3,3,104,256]{3,2,1,0:T(8,128)S(1)}, f32[3,3,104,256]{3,2,1,0:T(8,128)S(1)}, u32[]{:S(2)}, u32[]{:S(2)}) collective-permute-start(f32[3,3,104,256]{3,2,1,0:T(8,128)S(1)} %get-tuple-element.16), channel_id=1, source_target_pairs={{0,63},{1,0},{2,1},{3,2},{4,3},{5,4},{6,5},{7,6},{8,7},{9,8},{10,9... | collective-permute-start | bytes 2875400 | tf_op jit(solution)/shard_map/ppermute | solution.py:378
  12.4 0.0 collective-permute-start.7
  12.4 0.5 %collective-permute-start = (f32[2,3,2,8,128]{4,3,2,1,0:T(8,128)S(1)}, f32[2,3,2,8,128]{4,3,2,1,0:T(8,128)S(1)}, u32[]{:S(2)}, u32[]{:S(2)}) collective-permute-start(f32[2,3,2,8,128]{4,3,2,1,0:T(8,128)S(1)} %get-tuple-element.11), channel_id=1, source_target_pairs={{0,64},{64,128},{128,192},{192,0},{1,65},{65,129},{129,193},{193,1... | collective-permute-start | bytes 147464 | tf_op jit(solution)/shard_map/ppermute | solution.py:378
  12.9 1.5 %collective-permute-start.1 = (f32[2,3,2,8,128]{4,3,2,1,0:T(8,128)S(1)}, f32[2,3,2,8,128]{4,3,2,1,0:T(8,128)S(1)}, u32[]{:S(2)}, u32[]{:S(2)}) collective-permute-start(f32[2,3,2,8,128]{4,3,2,1,0:T(8,128)S(1)} %get-tuple-element.12), channel_id=1, source_target_pairs={{0,192},{64,0},{128,64},{192,128},{1,193},{65,1},{129,65},{193,129... | collective-permute-start | bytes 147464 | tf_op jit(solution)/shard_map/ppermute | solution.py:378
  14.4 2.1 %collective-permute-done.from_left = f32[2,3,2,8,128]{4,3,2,1,0:T(8,128)S(1)} collective-permute-done((f32[2,3,2,8,128]{4,3,2,1,0:T(8,128)S(1)}, f32[2,3,2,8,128]{4,3,2,1,0:T(8,128)S(1)}, u32[]{:S(2)}, u32[]{:S(2)}) %collective-permute-start) | collective-permute-done | bytes 49184 | tf_op jit(solution)/shard_map/ppermute | solution.py:378
  16.5 0.0 collective-permute-start.5
  16.5 1.7 %collective-permute-done.1.from_right = f32[2,3,2,8,128]{4,3,2,1,0:T(8,128)S(1)} collective-permute-done((f32[2,3,2,8,128]{4,3,2,1,0:T(8,128)S(1)}, f32[2,3,2,8,128]{4,3,2,1,0:T(8,128)S(1)}, u32[]{:S(2)}, u32[]{:S(2)}) %collective-permute-start.1) | collective-permute-done | bytes 49184 | tf_op jit(solution)/shard_map/ppermute | solution.py:378
  18.2 3.6 %collective-permute-start.3 = (f32[3,3,24,256]{3,2,1,0:T(8,128)S(1)}, f32[3,3,24,256]{3,2,1,0:T(8,128)S(1)}, u32[]{:S(2)}, u32[]{:S(2)}) collective-permute-start(f32[3,3,24,256]{3,2,1,0:T(8,128)S(1)} %get-tuple-element.15), channel_id=1, source_target_pairs={{0,63},{1,0},{2,1},{3,2},{4,3},{5,4},{6,5},{7,6},{8,7},{9,8},{10,9... | collective-permute-start | bytes 663560 | tf_op jit(solution)/shard_map/ppermute | solution.py:378
  21.8 0.0 collective-permute-done.2.chip
  21.8 0.1 collective-permute-start.6
  21.9 0.0 copy-done.1
  21.9 0.0 copy-done.3
  21.9 0.0 copy-done.4
  22.0 1.9 %inner.1.adv_in = f32[3,128,2,8,128]{4,3,2,1,0:T(8,128)S(1)} custom-call(f32[3,128,2,8,128]{4,3,2,1,0:T(8,128)S(1)} %bitcast.12, f32[3,3,128,256]{3,2,1,0:T(8,128)S(1)} %collective-permute-done.2.chip, bf16[256,256]{1,0:T(8,128)(2,1)S(1)} %copy-done.4, bf16[2,128,176]{2,1,0:T(8,128)(2,1)S(1)} %copy-done.3), custom_call_target="tpu_custom_call" | custom-call | tf_op jit(solution)/shard_map/inner/pallas_call | solution.py:233
  23.9 0.0 copy-start.2
  23.9 2.2 %along.1 = (f32[3,128,2,8,128]{4,3,2,1,0:T(8,128)S(1)}, f32[3,128,2,8,128]{4,3,2,1,0:T(8,128)}) custom-call(f32[3,128,2,8,128]{4,3,2,1,0:T(8,128)S(1)} %bitcast.13, f32[2,3,2,8,128]{4,3,2,1,0:T(8,128)S(1)} %collective-permute-done.from_left, f32[2,3,2,8,128]{4,3,2,1,0:T(8,128)S(1)} %collective-permute-done.1.from_right, ...), custom_call_target="tpu_custom_call", output_to_operand_aliasing={{0}: (3, {})} | custom-call | tf_op jit(solution)/shard_map/along/pallas_call | solution.py:290
  26.1 5.2 %collective-permute-done.6.refs_3_ = f32[3,3,16,256]{3,2,1,0:T(8,128)S(1)} collective-permute-done((f32[3,3,16,256]{3,2,1,0:T(8,128)S(1)}, f32[3,3,16,256]{3,2,1,0:T(8,128)S(1)}, u32[]{:S(2)}, u32[]{:S(2)}) %collective-permute-start.6) | collective-permute-done | bytes 147488 | tf_op jit(solution)/shard_map/ppermute | solution.py:378
  31.3 0.0 collective-permute-done.7.refs_4_
  31.3 0.0 copy-done.2
  31.3 1.9 %outer.4.refs_4_ = f32[3,128,2,8,128]{4,3,2,1,0:T(8,128)} custom-call(f32[3,128,2,8,128]{4,3,2,1,0:T(8,128)S(1)} %bitcast.14, f32[3,128,2,8,128]{4,3,2,1,0:T(8,128)S(1)} %get-tuple-element.14.refs_1_, bf16[2,64,24]{2,1,0:T(8,128)(2,1)S(1)} %copy-done.2, f32[3,3,16,256]{3,2,1,0:T(8,128)S(1)} %collective-permute-done.6.refs_3_, ...), custom_call_target="tpu_custom_call" | custom-call | tf_op jit(solution)/shard_map/outer/pallas_call | solution.py:361
  33.2 0.0 collective-permute-done.5.refs_3_
  33.2 1.1 %outer.5.refs_4_ = f32[3,128,2,8,128]{4,3,2,1,0:T(8,128)} custom-call(f32[3,128,2,8,128]{4,3,2,1,0:T(8,128)S(1)} %bitcast.15, f32[3,128,2,8,128]{4,3,2,1,0:T(8,128)S(1)} %get-tuple-element.14.refs_1_, bf16[2,64,24]{2,1,0:T(8,128)(2,1)S(1)} %copy-done.2, f32[3,3,24,256]{3,2,1,0:T(8,128)S(1)} %collective-permute-done.5.refs_3_, ...), custom_call_target="tpu_custom_call", output_to_operand_aliasing={{}: (4, {})} | custom-call | tf_op jit(solution)/shard_map/outer/pallas_call | solution.py:361
  34.3 0.0 collective-permute-done.4.refs_3_
  34.3 0.1 outer.6.refs_4_
  34.4 0.0 collective-permute-done.3.refs_3_
  34.4 0.1 outer.7
  (1 shorter events, 0.0 us)
Async XLA Ops:
  0.6 1.9 %copy-start = (f32[3,128,8,256]{3,2,1,0:T(8,128)S(1)}, f32[3,128,8,256]{3,2,1,0:T(8,128)}, u32[]{:S(2)}) copy-start(f32[3,128,8,256]{3,2,1,0:T(8,128)} %param.4) | copy-start | bytes 9437188
  3.4 18.5 %copy-start.1 = (f32[3,128,8,256]{3,2,1,0:T(8,128)S(1)}, f32[3,128,8,256]{3,2,1,0:T(8,128)}, u32[]{:S(2)}) copy-start(f32[3,128,8,256]{3,2,1,0:T(8,128)} %param.4) | copy-start | bytes 9437188
  3.5 18.5 %copy-start.3 = (bf16[2,128,176]{2,1,0:T(8,128)(2,1)S(1)}, bf16[2,128,176]{2,1,0:T(8,128)(2,1)}, u32[]{:S(2)}) copy-start(bf16[2,128,176]{2,1,0:T(8,128)(2,1)} %constant.7.clone.ymat) | copy-start | bytes 270340
  3.5 18.5 %copy-start.4 = (bf16[256,256]{1,0:T(8,128)(2,1)S(1)}, bf16[256,256]{1,0:T(8,128)(2,1)}, u32[]{:S(2)}) copy-start(bf16[256,256]{1,0:T(8,128)(2,1)} %constant.6.clone.zmat) | copy-start | bytes 393220
  3.5 18.3 %collective-permute-start.2 = (f32[3,3,128,256]{3,2,1,0:T(8,128)S(1)}, f32[3,3,128,256]{3,2,1,0:T(8,128)S(1)}, u32[]{:S(2)}, u32[]{:S(2)}) collective-permute-start(f32[3,3,128,256]{3,2,1,0:T(8,128)S(1)} %get-tuple-element.13), channel_id=1, source_target_pairs={{0,1},{1,0},{2,3},{3,2},{4,5},{5,4},{6,7},{7,6},{8,9},{9,8},{10,11... | collective-permute-start | bytes 3538952 | tf_op jit(solution)/shard_map/ppermute | solution.py:378
  4.0 30.3 %collective-permute-start.4 = (f32[3,3,104,256]{3,2,1,0:T(8,128)S(1)}, f32[3,3,104,256]{3,2,1,0:T(8,128)S(1)}, u32[]{:S(2)}, u32[]{:S(2)}) collective-permute-start(f32[3,3,104,256]{3,2,1,0:T(8,128)S(1)} %get-tuple-element.16), channel_id=1, source_target_pairs={{0,63},{1,0},{2,1},{3,2},{4,3},{5,4},{6,5},{7,6},{8,7},{9,8},{10,9... | collective-permute-start | bytes 2875400 | tf_op jit(solution)/shard_map/ppermute | solution.py:378
  12.4 19.0 %collective-permute-start.7 = (f32[3,3,88,256]{3,2,1,0:T(8,128)S(1)}, f32[3,3,88,256]{3,2,1,0:T(8,128)S(1)}, u32[]{:S(2)}, u32[]{:S(2)}) collective-permute-start(f32[3,3,88,256]{3,2,1,0:T(8,128)S(1)} %get-tuple-element.18), channel_id=1, source_target_pairs={{0,1},{1,2},{2,3},{3,4},{4,5},{5,6},{6,7},{7,8},{8,9},{9,10},{10,1... | collective-permute-start | bytes 2433032 | tf_op jit(solution)/shard_map/ppermute | solution.py:378
  12.4 4.1 %collective-permute-start = (f32[2,3,2,8,128]{4,3,2,1,0:T(8,128)S(1)}, f32[2,3,2,8,128]{4,3,2,1,0:T(8,128)S(1)}, u32[]{:S(2)}, u32[]{:S(2)}) collective-permute-start(f32[2,3,2,8,128]{4,3,2,1,0:T(8,128)S(1)} %get-tuple-element.11), channel_id=1, source_target_pairs={{0,64},{64,128},{128,192},{192,0},{1,65},{65,129},{129,193},{193,1... | collective-permute-start | bytes 147464 | tf_op jit(solution)/shard_map/ppermute | solution.py:378
  12.9 5.3 %collective-permute-start.1 = (f32[2,3,2,8,128]{4,3,2,1,0:T(8,128)S(1)}, f32[2,3,2,8,128]{4,3,2,1,0:T(8,128)S(1)}, u32[]{:S(2)}, u32[]{:S(2)}) collective-permute-start(f32[2,3,2,8,128]{4,3,2,1,0:T(8,128)S(1)} %get-tuple-element.12), channel_id=1, source_target_pairs={{0,192},{64,0},{128,64},{192,128},{1,193},{65,1},{129,65},{193,129... | collective-permute-start | bytes 147464 | tf_op jit(solution)/shard_map/ppermute | solution.py:378
  16.5 16.7 %collective-permute-start.5 = (f32[3,3,24,256]{3,2,1,0:T(8,128)S(1)}, f32[3,3,24,256]{3,2,1,0:T(8,128)S(1)}, u32[]{:S(2)}, u32[]{:S(2)}) collective-permute-start(f32[3,3,24,256]{3,2,1,0:T(8,128)S(1)} %get-tuple-element.17), channel_id=1, source_target_pairs={{0,1},{1,2},{2,3},{3,4},{4,5},{5,6},{6,7},{7,8},{8,9},{9,10},{10,1... | collective-permute-start | bytes 663560 | tf_op jit(solution)/shard_map/ppermute | solution.py:378
  18.2 16.2 %collective-permute-start.3 = (f32[3,3,24,256]{3,2,1,0:T(8,128)S(1)}, f32[3,3,24,256]{3,2,1,0:T(8,128)S(1)}, u32[]{:S(2)}, u32[]{:S(2)}) collective-permute-start(f32[3,3,24,256]{3,2,1,0:T(8,128)S(1)} %get-tuple-element.15), channel_id=1, source_target_pairs={{0,63},{1,0},{2,1},{3,2},{4,3},{5,4},{6,5},{7,6},{8,7},{9,8},{10,9... | collective-permute-start | bytes 663560 | tf_op jit(solution)/shard_map/ppermute | solution.py:378
  21.8 9.5 %collective-permute-start.6 = (f32[3,3,16,256]{3,2,1,0:T(8,128)S(1)}, f32[3,3,16,256]{3,2,1,0:T(8,128)S(1)}, u32[]{:S(2)}, u32[]{:S(2)}) collective-permute-start(f32[3,3,16,256]{3,2,1,0:T(8,128)S(1)} %first.1), channel_id=1, source_target_pairs={{0,1},{1,2},{2,3},{3,4},{4,5},{5,6},{6,7},{7,8},{8,9},{9,10},{10,1... | collective-permute-start | bytes 442376 | tf_op jit(solution)/shard_map/ppermute | solution.py:378
  23.9 7.5 %copy-start.2 = (bf16[2,64,24]{2,1,0:T(8,128)(2,1)S(1)}, bf16[2,64,24]{2,1,0:T(8,128)(2,1)}, u32[]{:S(2)}) copy-start(bf16[2,64,24]{2,1,0:T(8,128)(2,1)} %constant.8.clone.refs_2_) | copy-start | bytes 18436
